TPU v7x, 512 devices: a whole 4x8x8 slice. The times are simulated.
512 devices in a mesh: lat: 8 (over x, z_hi), lon: 64 (over y, z_lo, core).
Axes of the slice: x: 4, y: 8, z: 8 (z_hi: 2, z_lo: 4; z = z_hi * 4 + z_lo), core: 2. Of those that a mesh axis runs over, the one named last changes fastest.
Arguments:
- queries: bfloat16 [96, 1024, 512], P('lat', 'lon'), may hold values from -6 to 6
- keys: bfloat16 [96, 1024, 512], P('lat', 'lon'), may hold values from -6 to 6
- values: bfloat16 [96, 1024, 512], P('lat', 'lon'), may hold values from -16 to 16
- upstream: bfloat16 [96, 1024, 1024], P('lat', 'lon'), may hold values from -6 to 6
- out_weight: bfloat16 [512, 1024], replicated, may hold values from -0.25 to 0.25
Outputs:
- grad_queries: bfloat16 [96, 1024, 512], P('lat', 'lon')
- grad_keys: bfloat16 [96, 1024, 512], P('lat', 'lon')
- grad_values: bfloat16 [96, 1024, 512], P('lat', 'lon')
- grad_weight: float32 [512, 1024], P('lon')
All inputs are finite; a program needn't handle non-finite values.
Results may differ from a plain program's by a relative error of at most 0.035.
Values may be sent and summed in bfloat16 or wider, within the bound.
No kernel may reach another device: no remote copies, remote signals or barrier semaphores. Data moves between devices by JAX's collectives and lax.ppermute only.
A program may use at most 64 MiB of HBM per device.

v0:
```python
import jax
import jax.numpy as jnp
from jax import lax
from jax.sharding import PartitionSpec as P

HEADS = 8
RADIUS = 6


def shifted(block, axis, distance):
    devices = range(lax.axis_size(axis))
    route = [((i - distance) % len(devices), i) for i in devices]
    return lax.ppermute(block, axis, route)


def passed_along(shard, axis, by):
    size = lax.axis_size(axis)
    pairs = [(i, i + by) for i in range(size) if 0 <= i + by < size]
    return lax.ppermute(shard, axis, pairs)


def extended_2(block, sides, width):
    for axis, dim in sides:
        count = lax.axis_size(axis)
        forward = [(i, i + 1) for i in range(count - 1)]
        forward.append((count - 1, 0))
        backward = [(target, source) for source, target in forward]
        low = lax.ppermute(
            lax.slice_in_dim(block, block.shape[dim] - width, None, axis=dim), axis, forward
        )
        high = lax.ppermute(lax.slice_in_dim(block, 0, width, axis=dim), axis, backward)
        block = jnp.concatenate([low, block, high], axis=dim)
    return block


def window_mask(lat_rows, lon_cols, radius, lat_base, lat_total):
    query_lat = jnp.arange(lat_rows, dtype=jnp.int32)
    query_lon = jnp.arange(lon_cols, dtype=jnp.int32)
    near_lat = jnp.arange(lat_rows + 2 * radius, dtype=jnp.int32)
    near_lon = jnp.arange(lon_cols + 2 * radius, dtype=jnp.int32)
    lat_close = jnp.abs(near_lat[None, :] - radius - query_lat[:, None]) <= radius
    global_lat = lat_base + near_lat - radius
    lat_inside = (global_lat >= 0) & (global_lat < lat_total)
    lat_good = lat_close & lat_inside[None, :]
    lon_close = jnp.abs(near_lon[None, :] - radius - query_lon[:, None]) <= radius
    allowed = lat_good[:, None, :, None] & lon_close[None, :, None, :]
    return allowed.reshape(lat_rows * lon_cols, (lat_rows + 2 * radius) * (lon_cols + 2 * radius))


def strip_height():
    for candidate in (4, 3, 2):
        return candidate
    return 1


def fold_margins(key_sums, lat_rows, lon_cols, radius):
    left_rim = key_sums[:, :radius]
    right_rim = key_sums[:, radius + lon_cols :]
    from_right = shifted(left_rim.astype(jnp.bfloat16), "lon", -1).astype(left_rim.dtype)
    from_left = shifted(right_rim.astype(jnp.bfloat16), "lon", 1).astype(right_rim.dtype)
    middle = key_sums[:, radius : radius + lon_cols]
    middle = middle + jnp.pad(from_left, ((0, 0), (0, lon_cols - radius), (0, 0)))
    middle = middle + jnp.pad(from_right, ((0, 0), (lon_cols - radius, 0), (0, 0)))
    upper_rim = middle[:radius]
    lower_rim = middle[radius + lat_rows :]
    from_below = passed_along(upper_rim.astype(jnp.bfloat16), "lat", -1).astype(upper_rim.dtype)
    from_above = passed_along(lower_rim.astype(jnp.bfloat16), "lat", 1).astype(lower_rim.dtype)
    owned = middle[radius : radius + lat_rows]
    owned = owned + jnp.pad(from_above, ((0, lat_rows - radius), (0, 0), (0, 0)))
    owned = owned + jnp.pad(from_below, ((lat_rows - radius, 0), (0, 0), (0, 0)))
    return owned


def shards(queries, keys, values, upstream, out_weight):
    lat_rows, lon_cols, inner_width = queries.shape
    model_width = upstream.shape[2]
    head_count = HEADS
    head_size = inner_width // head_count
    radius = RADIUS
    score_scale = head_size ** (-0.5)
    ext_lat = lat_rows + 2 * radius
    ext_lon = lon_cols + 2 * radius
    tokens = lat_rows * lon_cols
    strip = strip_height()
    strip_count = lat_rows // strip
    slab_lat = strip + 2 * radius
    slab_count = slab_lat * ext_lon
    strip_tokens = strip * lon_cols
    lat_total = lat_rows * lax.axis_size("lat")
    lat_base = lax.axis_index("lat") * lat_rows
    out_flat = upstream.reshape(tokens, model_width)
    grad_flat = jnp.einsum(
        "td,id->ti", out_flat, out_weight, preferred_element_type=jnp.float32
    ).astype(jnp.bfloat16)
    grad_grid = grad_flat.reshape(lat_rows, lon_cols, inner_width)
    extended = extended_2(jnp.concatenate([keys, values], axis=2), (("lat", 0), ("lon", 1)), radius)

    def forward_strip(strip_id, carry):
        grad_query_all, attended_all, stats_all, sums_all = carry
        first = strip_id * strip
        query_heads = lax.dynamic_slice_in_dim(queries, first, strip, 0).reshape(
            strip_tokens, head_count, head_size
        )
        grad_heads = lax.dynamic_slice_in_dim(grad_grid, first, strip, 0).reshape(
            strip_tokens, head_count, head_size
        )
        slab = lax.dynamic_slice_in_dim(extended, first, slab_lat, 0)
        near_keys = slab[:, :, :inner_width].reshape(slab_count, head_count, head_size)
        near_values = slab[:, :, inner_width:].reshape(slab_count, head_count, head_size)
        allowed = window_mask(strip, lon_cols, radius, lat_base + first, lat_total)
        scores = (
            jnp.einsum("qhd,khd->hqk", query_heads, near_keys, preferred_element_type=jnp.float32)
            * score_scale
        )
        row_max = jnp.max(jnp.where(allowed[None], scores, -jnp.inf), axis=2, keepdims=True)
        raw_weights = jnp.where(allowed[None], jnp.exp(scores - row_max), 0.0)
        totals = jnp.sum(raw_weights, axis=2, keepdims=True)
        softmax_f32 = raw_weights / totals
        softmax_low = softmax_f32.astype(jnp.bfloat16)
        attended = jnp.einsum(
            "hqk,khd->qhd", softmax_low, near_values, preferred_element_type=jnp.float32
        ).astype(jnp.bfloat16)
        row_delta = jnp.sum(grad_heads.astype(jnp.float32) * attended.astype(jnp.float32), axis=2)
        grad_prob = jnp.einsum(
            "qhd,khd->hqk", grad_heads, near_values, preferred_element_type=jnp.float32
        )
        grad_score = (softmax_f32 * (grad_prob - row_delta.T[:, :, None])).astype(jnp.bfloat16)
        grad_query = (
            jnp.einsum("hqk,khd->qhd", grad_score, near_keys, preferred_element_type=jnp.float32)
            * score_scale
        )
        grad_query = grad_query.astype(jnp.bfloat16).reshape(strip, lon_cols, inner_width)
        log_norm = (row_max + jnp.log(totals))[:, :, 0]
        row_stats = jnp.concatenate([log_norm.T, row_delta], axis=1).reshape(
            strip, lon_cols, 2 * head_count
        )
        grad_query_all = lax.dynamic_update_slice_in_dim(grad_query_all, grad_query, first, 0)
        attended_all = lax.dynamic_update_slice_in_dim(
            attended_all, attended.reshape(strip, lon_cols, inner_width), first, 0
        )
        stats_all = lax.dynamic_update_slice_in_dim(stats_all, row_stats, first, 0)
        value_sums = jnp.einsum(
            "hqk,qhd->khd", softmax_low, grad_heads, preferred_element_type=jnp.float32
        )
        key_part = (
            jnp.einsum("hqk,qhd->khd", grad_score, query_heads, preferred_element_type=jnp.float32)
            * score_scale
        )
        slab_sums = jnp.concatenate(
            [
                key_part.reshape(slab_lat, ext_lon, inner_width),
                value_sums.reshape(slab_lat, ext_lon, inner_width),
            ],
            axis=2,
        )
        previous = lax.dynamic_slice_in_dim(sums_all, first, slab_lat, 0)
        sums_all = lax.dynamic_update_slice_in_dim(sums_all, previous + slab_sums, first, 0)
        return (grad_query_all, attended_all, stats_all, sums_all)

    sums_start = jnp.zeros((ext_lat, ext_lon, 2 * inner_width), jnp.float32)
    start = (
        jnp.zeros((lat_rows, lon_cols, inner_width), jnp.bfloat16),
        jnp.zeros((lat_rows, lon_cols, inner_width), jnp.bfloat16),
        jnp.zeros((lat_rows, lon_cols, 2 * head_count), jnp.float32),
        sums_start,
    )
    grad_query, attended_grid, stats_grid, key_sums = lax.fori_loop(
        0, strip_count, forward_strip, start
    )
    owned = fold_margins(key_sums, lat_rows, lon_cols, radius)
    grad_key = owned[:, :, :inner_width].astype(jnp.bfloat16)
    grad_value = owned[:, :, inner_width:].astype(jnp.bfloat16)
    attended_flat = attended_grid.reshape(tokens, inner_width)
    lon_share = lax.psum_scatter(
        jnp.einsum("ti,td->id", attended_flat, out_flat, preferred_element_type=jnp.float32),
        "lon",
        scatter_dimension=0,
        tiled=True,
    )
    weight_part = lax.psum(lon_share.astype(jnp.bfloat16), "lat").astype(jnp.float32)
    grad_weight = weight_part / lat_total
    return (grad_query, grad_key, grad_value, grad_weight)


def solution(mesh):
    placed = (
        P("lat", "lon", None),
        P("lat", "lon", None),
        P("lat", "lon", None),
        P("lat", "lon", None),
        P(),
    )
    return jax.shard_map(
        shards,
        mesh=mesh,
        in_specs=placed,
        out_specs=(
            P("lat", "lon", None),
            P("lat", "lon", None),
            P("lat", "lon", None),
            P("lon", None),
        ),
        check_vma=False,
    )
```

profile of v0, /device:TPU:6, one launch (start us, length us, event | category | flops | bytes accessed | tf_op | source)
XLA Modules:
  0.0 488.0 jit_solution(5883782968312088491)
XLA Ops:
  9.3 10.9 %collective-permute-start = (bf16[6,16,1024]{2,1,0:T(8,128)(2,1)S(1)}, bf16[6,16,1024]{2,1,0:T(8,128)(2,1)S(1)}, u32[]{:S(2)}, u32[]{:S(2)}) collective-permute-start(bf16[6,16,1024]{2,1,0:T(8,128)(2,1)S(1)} %get-tuple-element.276), channel_id=1, source_target_pairs={{0,64},{64,128},{128,192},{192,256},{256,320},{320,384},{384,448},... | collective-permute-start | bytes 589832 | tf_op jit(solution)/shard_map/ppermute | solution.py:28
  20.2 2.2 collective-permute-start.1
  22.4 7.0 %collective-permute-done = bf16[6,16,1024]{2,1,0:T(8,128)(2,1)S(1)} collective-permute-done((bf16[6,16,1024]{2,1,0:T(8,128)(2,1)S(1)}, bf16[6,16,1024]{2,1,0:T(8,128)(2,1)S(1)}, u32[]{:S(2)}, u32[]{:S(2)}) %collective-permute-start) | collective-permute-done | bytes 196640 | tf_op jit(solution)/shard_map/ppermute | solution.py:28
  29.5 7.0 %collective-permute-done.1 = bf16[6,16,1024]{2,1,0:T(8,128)(2,1)S(1)} collective-permute-done((bf16[6,16,1024]{2,1,0:T(8,128)(2,1)S(1)}, bf16[6,16,1024]{2,1,0:T(8,128)(2,1)S(1)}, u32[]{:S(2)}, u32[]{:S(2)}) %collective-permute-start.1) | collective-permute-done | bytes 196640 | tf_op jit(solution)/shard_map/ppermute | solution.py:31
  39.5 7.5 %collective-permute-start.3 = (bf16[24,6,1024]{2,1,0:T(8,128)(2,1)}, bf16[24,6,1024]{2,1,0:T(8,128)(2,1)S(1)}, u32[]{:S(2)}, u32[]{:S(2)}) collective-permute-start(bf16[24,6,1024]{2,1,0:T(8,128)(2,1)} %get-tuple-element.273), channel_id=1, source_target_pairs={{1,0},{2,1},{3,2},{4,3},{5,4},{6,5},{7,6},{8,7},{9,8},{10,9},{11,1... | collective-permute-start | bytes 884744 | tf_op jit(solution)/shard_map/ppermute | solution.py:31
  47.6 3.4 collective-permute-done.2
  55.9 2.0 broadcast_in_dim.82
  58.0 82.4 %while.20 = (s32[]{:T(128)}, bf16[12,16,512]{2,1,0:T(8,128)(2,1)}, bf16[12,16,512]{2,1,0:T(8,128)(2,1)}, f32[24,28,1024]{2,1,0:T(8,128)}, bf16[24,28,1024]{2,1,0...) while((s32[]{:T(128)}, bf16[12,16,512]{2,1,0:T(8,128)(2,1)}, ...), condition=%wide.region_4.5_spmd, body=%wide.region_0.4_spmd.sunk | while | flops 181927424 | bytes 31905408 | solution.py:167
  65.9 2.0 multiply_reduce_fusion.2
  67.9 2.1 convolution_bitcast_fusion.3
  74.6 1.9 copy.46
  77.9 1.9 copy.45
  81.4 4.1 fusion.93
  93.3 2.0 multiply_reduce_fusion.2
  95.4 2.1 convolution_bitcast_fusion.3
  102.0 1.9 copy.46
  108.8 4.1 fusion.93
  120.8 2.0 multiply_reduce_fusion.2
  122.8 2.1 convolution_bitcast_fusion.3
  132.9 1.9 copy.45
  136.3 4.1 fusion.93
  140.4 2.9 convolution_bitcast_fusion.1
  143.3 2.3 convert.20
  145.8 4.1 collective-permute-start.4
  149.9 5.4 %collective-permute-start.5 = (bf16[24,6,1024]{2,1,0:T(8,128)(2,1)S(1)}, bf16[24,6,1024]{2,1,0:T(8,128)(2,1)S(1)}, u32[]{:S(2)}, u32[]{:S(2)}) collective-permute-start(bf16[24,6,1024]{2,1,0:T(8,128)(2,1)S(1)} %get-tuple-element.269), channel_id=1, source_target_pairs={{1,0},{2,1},{3,2},{4,3},{5,4},{6,5},{7,6},{8,7},{9,8},{10,9},{11,1... | collective-permute-start | bytes 884744 | tf_op jit(solution)/shard_map/ppermute | solution.py:13
  155.3 3.8 collective-permute-done.4
  161.1 8.9 %collective-permute-start.6 = (bf16[6,16,1024]{2,1,0:T(8,128)(2,1)S(1)}, bf16[6,16,1024]{2,1,0:T(8,128)(2,1)S(1)}, u32[]{:S(2)}, u32[]{:S(2)}) collective-permute-start(bf16[6,16,1024]{2,1,0:T(8,128)(2,1)S(1)} %get-tuple-element.270), channel_id=1, source_target_pairs={{0,64},{64,128},{128,192},{192,256},{256,320},{320,384},{384,448},... | collective-permute-start | bytes 589832 | tf_op jit(solution)/shard_map/ppermute | solution.py:19
  170.0 3.0 collective-permute-start.7
  172.9 2.7 collective-permute-done.6
  175.7 6.6 %collective-permute-done.7 = bf16[6,16,1024]{2,1,0:T(8,128)(2,1)S(1)} collective-permute-done((bf16[6,16,1024]{2,1,0:T(8,128)(2,1)S(1)}, bf16[6,16,1024]{2,1,0:T(8,128)(2,1)S(1)}, u32[]{:S(2)}, u32[]{:S(2)}) %collective-permute-start.7) | collective-permute-done | bytes 196640 | tf_op jit(solution)/shard_map/ppermute | solution.py:19
  183.2 248.0 %reduce-scatter.2.cloned.1.call-done = f32[8,1024]{1,0:T(8,128)} async-done(((f32[512,1024]{1,0:T(8,128)}), f32[8,1024]{1,0:T(8,128)}) %reduce-scatter.2.cloned.1.call-update) | async-done | bytes 32784 | tf_op jit(solution)/shard_map/reduce_scatter | solution.py:174
  431.9 48.6 %psum.7 = bf16[8,1024]{1,0:T(8,128)(2,1)S(1)} all-reduce(bf16[8,1024]{1,0:T(8,128)(2,1)S(1)} %convert_element_type.100), channel_id=1, replica_groups=mesh['lat'=8,'lon'=64] {'lat'}, use_global_device_ids=true, to_apply=%region_6.7 | all-reduce | flops 8192 | bytes 32768 | tf_op jit(solution)/shard_map/psum | solution.py:180
  (119 shorter events, 64.8 us)
Async XLA Ops:
  7.2 39.9 %copy-start = (bf16[512,1024]{1,0:T(8,128)(2,1)S(1)}, bf16[512,1024]{1,0:T(8,128)(2,1)}, u32[]{:S(2)}) copy-start(bf16[512,1024]{1,0:T(8,128)(2,1)} %param.11) | copy-start | bytes 3145732
  7.2 424.0 %reduce-scatter.2.cloned.1.call-start = ((), (), s32[]{:S(2)}) async-start(), calls=%async_computation.1 | async-start | bytes 2129920 | tf_op jit(solution)/shard_map/reduce_scatter | solution.py:174
  8.3 38.8 %copy-start.2 = (bf16[12,16,1024]{2,1,0:T(8,128)(2,1)S(1)}, bf16[12,16,1024]{2,1,0:T(8,128)(2,1)}, u32[]{:S(2)}) copy-start(bf16[12,16,1024]{2,1,0:T(8,128)(2,1)} %param.10) | copy-start | bytes 1179652
  9.3 20.2 %collective-permute-start = (bf16[6,16,1024]{2,1,0:T(8,128)(2,1)S(1)}, bf16[6,16,1024]{2,1,0:T(8,128)(2,1)S(1)}, u32[]{:S(2)}, u32[]{:S(2)}) collective-permute-start(bf16[6,16,1024]{2,1,0:T(8,128)(2,1)S(1)} %get-tuple-element.276), channel_id=1, source_target_pairs={{0,64},{64,128},{128,192},{192,256},{256,320},{320,384},{384,448},... | collective-permute-start | bytes 589832 | tf_op jit(solution)/shard_map/ppermute | solution.py:28
  20.2 16.2 %collective-permute-start.1 = (bf16[6,16,1024]{2,1,0:T(8,128)(2,1)S(1)}, bf16[6,16,1024]{2,1,0:T(8,128)(2,1)S(1)}, u32[]{:S(2)}, u32[]{:S(2)}) collective-permute-start(bf16[6,16,1024]{2,1,0:T(8,128)(2,1)S(1)} %get-tuple-element.277), channel_id=1, source_target_pairs={{64,0},{128,64},{192,128},{256,192},{320,256},{384,320},{448,384},... | collective-permute-start | bytes 589832 | tf_op jit(solution)/shard_map/ppermute | solution.py:31
  37.6 13.4 %collective-permute-start.2 = (bf16[24,6,1024]{2,1,0:T(8,128)(2,1)}, bf16[24,6,1024]{2,1,0:T(8,128)(2,1)S(1)}, u32[]{:S(2)}, u32[]{:S(2)}) collective-permute-start(bf16[24,6,1024]{2,1,0:T(8,128)(2,1)} %get-tuple-element.272), channel_id=1, source_target_pairs={{0,1},{1,2},{2,3},{3,4},{4,5},{5,6},{6,7},{7,8},{8,9},{9,10},{10,1... | collective-permute-start | bytes 884744 | tf_op jit(solution)/shard_map/ppermute | solution.py:28
  39.5 13.1 %collective-permute-start.3 = (bf16[24,6,1024]{2,1,0:T(8,128)(2,1)}, bf16[24,6,1024]{2,1,0:T(8,128)(2,1)S(1)}, u32[]{:S(2)}, u32[]{:S(2)}) collective-permute-start(bf16[24,6,1024]{2,1,0:T(8,128)(2,1)} %get-tuple-element.273), channel_id=1, source_target_pairs={{1,0},{2,1},{3,2},{4,3},{5,4},{6,5},{7,6},{8,7},{9,8},{10,9},{11,1... | collective-permute-start | bytes 884744 | tf_op jit(solution)/shard_map/ppermute | solution.py:31
  143.3 17.3 %copy-start.1 = (f32[24,28,1024]{2,1,0:T(8,128)S(1)}, f32[24,28,1024]{2,1,0:T(8,128)}, u32[]{:S(2)}) copy-start(f32[24,28,1024]{2,1,0:T(8,128)} %get-tuple-element.228) | copy-start | bytes 8257540
  145.8 13.3 %collective-permute-start.4 = (bf16[24,6,1024]{2,1,0:T(8,128)(2,1)S(1)}, bf16[24,6,1024]{2,1,0:T(8,128)(2,1)S(1)}, u32[]{:S(2)}, u32[]{:S(2)}) collective-permute-start(bf16[24,6,1024]{2,1,0:T(8,128)(2,1)S(1)} %get-tuple-element.268), channel_id=1, source_target_pairs={{63,0},{0,1},{1,2},{2,3},{3,4},{4,5},{5,6},{6,7},{7,8},{8,9},{9,10... | collective-permute-start | bytes 884744 | tf_op jit(solution)/shard_map/ppermute | solution.py:13
  149.9 10.7 %collective-permute-start.5 = (bf16[24,6,1024]{2,1,0:T(8,128)(2,1)S(1)}, bf16[24,6,1024]{2,1,0:T(8,128)(2,1)S(1)}, u32[]{:S(2)}, u32[]{:S(2)}) collective-permute-start(bf16[24,6,1024]{2,1,0:T(8,128)(2,1)S(1)} %get-tuple-element.269), channel_id=1, source_target_pairs={{1,0},{2,1},{3,2},{4,3},{5,4},{6,5},{7,6},{8,7},{9,8},{10,9},{11,1... | collective-permute-start | bytes 884744 | tf_op jit(solution)/shard_map/ppermute | solution.py:13
  161.1 14.6 %collective-permute-start.6 = (bf16[6,16,1024]{2,1,0:T(8,128)(2,1)S(1)}, bf16[6,16,1024]{2,1,0:T(8,128)(2,1)S(1)}, u32[]{:S(2)}, u32[]{:S(2)}) collective-permute-start(bf16[6,16,1024]{2,1,0:T(8,128)(2,1)S(1)} %get-tuple-element.270), channel_id=1, source_target_pairs={{0,64},{64,128},{128,192},{192,256},{256,320},{320,384},{384,448},... | collective-permute-start | bytes 589832 | tf_op jit(solution)/shard_map/ppermute | solution.py:19
  170.0 12.3 %collective-permute-start.7 = (bf16[6,16,1024]{2,1,0:T(8,128)(2,1)S(1)}, bf16[6,16,1024]{2,1,0:T(8,128)(2,1)S(1)}, u32[]{:S(2)}, u32[]{:S(2)}) collective-permute-start(bf16[6,16,1024]{2,1,0:T(8,128)(2,1)S(1)} %get-tuple-element.271), channel_id=1, source_target_pairs={{64,0},{128,64},{192,128},{256,192},{320,256},{384,320},{448,384},... | collective-permute-start | bytes 589832 | tf_op jit(solution)/shard_map/ppermute | solution.py:19
Sparse Core Ops, SparseCore 0:
  143.4 287.7 reduce-scatter.1
where the time goes:
time: 490 us; the launch traced here: 488 us
  waiting for transfers between devices  282 us (58%)
  local copies, waits for them, and re-layouts  49.6 us (10%)
  blocking collectives  48.6 us (10%)
  starting transfers between devices  44 us (9%)
  matrix products  26.7 us (5%)
  other arithmetic  22.9 us (5%)
  between operations  14.2 us (3%)
    reduce_scatter x1, waiting for transfers between devices, shards(): lax.psum_scatter(jnp.einsum('ti,td->id', attended_flat, out_flat, preferr...  248 us
    psum x1, blocking collectives, shards(): lax.psum(lon_share.astype(jnp.bfloat16), 'lat').astype(jnp.float32)  48.6 us
    ppermute x2, starting transfers between devices, extended_2(): lax.ppermute(lax.slice_in_dim(block, block.shape[dim] - width, None, axis...  12.8 us
    dynamic_update_slice x3, other arithmetic, forward_strip(): lax.dynamic_update_slice_in_dim(sums_all, previous + slab_sums, first, 0)  12.2 us
    ppermute x2, starting transfers between devices, passed_along(): return lax.ppermute(shard, axis, pairs)  11.8 us
    ppermute x2, waiting for transfers between devices, extended_2(): lax.ppermute(lax.slice_in_dim(block, block.shape[dim] - width, None, axis...  10.5 us
  transfers between devices with their start and end apart: 9, of which 9 were waited for; matrix products, arithmetic and copies ran while one was open for 1% of the time, Pallas kernels for 0%

commit v1 on v0

v1 whole, which is shorter than its diff:
```python
import functools

import jax
import jax.numpy as jnp
from jax import lax
from jax.experimental import pallas as pl
from jax.experimental.pallas import tpu as pltpu
from jax.sharding import PartitionSpec as P

HEADS = 8
RADIUS = 6
SIDE = 8
STRIP = 4
PACK = 4

NT = (((1,), (1,)), ((), ()))
NN = (((1,), (0,)), ((), ()))


def mm(a, b, dims):
    return lax.dot_general(a, b, dims, preferred_element_type=jnp.float32)


def attention_kernel(
    lat_total,
    base_ref,
    q_ref,
    g_ref,
    ext_ref,
    halo_ref,
    up_ref,
    dq_ref,
    own_ref,
    left_ref,
    right_ref,
    gw_ref,
    kv,
    kt,
    vt,
    acc,
    att_t,
    dq_t,
):
    rows, cols, inner = q_ref.shape
    ext_rows = rows + 2 * RADIUS
    wide = cols + 2 * SIDE
    head = inner // HEADS
    scale = head ** (-0.5)
    group = PACK * head
    strip_q = STRIP * cols
    slab_rows = STRIP + 2 * RADIUS
    slab = slab_rows * wide
    lanes = PACK * strip_q
    base = base_ref[0]

    kv[:, 0:cols, :] = ext_ref[...]
    kv[:, cols:wide, :] = halo_ref[...]
    kt[...] = kv[:, :, 0:inner].reshape(ext_rows * wide, inner).T
    vt[...] = kv[:, :, inner:].reshape(ext_rows * wide, inner).T
    acc[...] = jnp.zeros_like(acc)

    key = lax.broadcasted_iota(jnp.int32, (slab, lanes), 0)
    query = lax.broadcasted_iota(jnp.int32, (slab, lanes), 1) & (strip_q - 1)
    row = key // wide
    place = key & (wide - 1)
    col = jnp.where(
        place < cols, place, jnp.where(place < cols + SIDE, place - cols - SIDE, place - SIDE)
    )
    row_gap = row - query // cols
    col_gap = jnp.abs(col - (query & (cols - 1)))
    near = (row_gap >= 0) & (row_gap <= 2 * RADIUS) & (col_gap <= RADIUS)
    diag = (lax.broadcasted_iota(jnp.int32, (lanes, group), 0) // strip_q) == (
        lax.broadcasted_iota(jnp.int32, (lanes, group), 1) // head
    )

    def spread(block):
        tall = jnp.concatenate([block.astype(jnp.float32)] * PACK, axis=0)
        return jnp.where(diag, tall, 0.0).astype(jnp.bfloat16)

    def diagonal(square):
        return jnp.concatenate(
            [
                square[h * head : (h + 1) * head, h * strip_q : (h + 1) * strip_q]
                for h in range(PACK)
            ],
            axis=0,
        )

    for s in range(rows // STRIP):
        first = s * STRIP
        low = RADIUS - base - first
        allowed = near & (row >= low) & (row < low + lat_total)
        window = slice(first * wide, first * wide + slab)
        for part in range(HEADS // PACK):
            chans = slice(part * group, (part + 1) * group)
            vchans = slice(inner + part * group, inner + (part + 1) * group)
            keys = kv[first : first + slab_rows, :, chans].reshape(slab, group)
            values = kv[first : first + slab_rows, :, vchans].reshape(slab, group)
            q_wide = spread(
                q_ref[first : first + STRIP, :, chans].reshape(strip_q, group) * scale
            )
            g_wide = spread(g_ref[first : first + STRIP, :, chans].reshape(strip_q, group))
            scores = jnp.where(allowed, mm(keys, q_wide, NT), -1e30)
            weights = jnp.exp(scores - jnp.max(scores, axis=0, keepdims=True))
            probs = weights * (1.0 / jnp.sum(weights, axis=0, keepdims=True))
            low_probs = probs.astype(jnp.bfloat16)
            grad_prob = mm(values, g_wide, NT)
            delta = jnp.sum(low_probs.astype(jnp.float32) * grad_prob, axis=0, keepdims=True)
            grad_score = (probs * (grad_prob - delta)).astype(jnp.bfloat16)
            here = slice(s * strip_q, (s + 1) * strip_q)
            att_t[chans, here] = diagonal(mm(vt[chans, window], low_probs, NN))
            dq_t[chans, here] = diagonal(mm(kt[chans, window], grad_score, NN)) * scale
            acc[first : first + slab_rows, :, chans] += mm(grad_score, q_wide, NN).reshape(
                slab_rows, wide, group
            )
            acc[first : first + slab_rows, :, vchans] += mm(low_probs, g_wide, NN).reshape(
                slab_rows, wide, group
            )

    dq_ref[...] = dq_t[...].T.astype(jnp.bfloat16).reshape(rows, cols, inner)
    own_ref[...] = acc[:, 0:cols, :]
    left_ref[...] = acc[:, cols : cols + SIDE, :].astype(jnp.bfloat16)
    right_ref[...] = acc[:, cols + SIDE : wide, :].astype(jnp.bfloat16)
    gw_ref[...] = mm(att_t[...].astype(jnp.bfloat16), up_ref[...], NN).astype(jnp.bfloat16)


def attention(base, queries, grads, extended, halo, upstream, lat_total, interpret=False):
    rows, cols, inner = queries.shape
    ext_rows = rows + 2 * RADIUS
    wide = cols + 2 * SIDE
    tokens = rows * cols
    model = upstream.shape[1]
    vmem = pl.BlockSpec(memory_space=pltpu.VMEM)
    return pl.pallas_call(
        functools.partial(attention_kernel, lat_total),
        out_shape=(
            jax.ShapeDtypeStruct((rows, cols, inner), jnp.bfloat16),
            jax.ShapeDtypeStruct((ext_rows, cols, 2 * inner), jnp.float32),
            jax.ShapeDtypeStruct((ext_rows, SIDE, 2 * inner), jnp.bfloat16),
            jax.ShapeDtypeStruct((ext_rows, SIDE, 2 * inner), jnp.bfloat16),
            jax.ShapeDtypeStruct((inner, model), jnp.bfloat16),
        ),
        in_specs=[pl.BlockSpec(memory_space=pltpu.SMEM)] + [vmem] * 5,
        out_specs=(vmem,) * 5,
        scratch_shapes=[
            pltpu.VMEM((ext_rows, wide, 2 * inner), jnp.bfloat16),
            pltpu.VMEM((inner, ext_rows * wide), jnp.bfloat16),
            pltpu.VMEM((inner, ext_rows * wide), jnp.bfloat16),
            pltpu.VMEM((ext_rows, wide, 2 * inner), jnp.float32),
            pltpu.VMEM((inner, tokens), jnp.float32),
            pltpu.VMEM((inner, tokens), jnp.float32),
        ],
        compiler_params=pltpu.CompilerParams(vmem_limit_bytes=48 << 20),
        cost_estimate=pl.CostEstimate(
            flops=2_600_000_000, bytes_accessed=8_000_000, transcendentals=800_000
        ),
        interpret=interpret,
    )(base, queries, grads, extended, halo, upstream)


def ring(block, axis, by):
    size = lax.axis_size(axis)
    return lax.ppermute(block, axis, [(i, (i + by) % size) for i in range(size)])


def line(block, axis, by):
    size = lax.axis_size(axis)
    return lax.ppermute(
        block, axis, [(i, i + by) for i in range(size) if 0 <= i + by < size]
    )


def reduce_weight(part, out_rows):
    lon = lax.axis_size("lon")
    me = lax.axis_index("lon")
    model = part.shape[1]
    cores, near = 2, 4
    far = lon // (cores * near)
    core = me % cores
    blocks = part.reshape(far, near, cores, out_rows, model)
    keep = lax.dynamic_index_in_dim(blocks, core, 2, keepdims=False)
    give = lax.dynamic_index_in_dim(blocks, 1 - core, 2, keepdims=False)
    got = lax.ppermute(give, "lon", [(i, i ^ 1) for i in range(lon)])
    half = (keep.astype(jnp.float32) + got.astype(jnp.float32)).astype(jnp.bfloat16)
    stride = near * cores
    far_groups = [[j + stride * i for i in range(far)] for j in range(stride)]
    split = lax.all_to_all(
        half.reshape(far, near * out_rows, model), "lon", 0, 0, axis_index_groups=far_groups, tiled=True
    )
    quarter = jnp.sum(split.astype(jnp.float32), axis=0).astype(jnp.bfloat16)
    near_groups = [
        [f * stride + n * cores + c for n in range(near)] for f in range(far) for c in range(cores)
    ]
    split = lax.all_to_all(
        quarter.reshape(near, out_rows, model), "lon", 0, 0, axis_index_groups=near_groups, tiled=True
    )
    share = jnp.sum(split.astype(jnp.float32), axis=0).astype(jnp.bfloat16)
    lat = lax.axis_size("lat")
    copies = jnp.broadcast_to(share[None], (lat,) + share.shape)
    every = lax.all_to_all(copies, "lat", 0, 0, tiled=True)
    return jnp.sum(every.astype(jnp.float32), axis=0)


def shards(queries, keys, values, upstream, out_weight):
    rows, cols, inner = queries.shape
    model = upstream.shape[2]
    tokens = rows * cols
    lat_total = rows * lax.axis_size("lat")
    base = (lax.axis_index("lat") * rows).astype(jnp.int32).reshape(1)
    up_flat = upstream.reshape(tokens, model)
    grads = (
        jnp.einsum("td,id->ti", up_flat, out_weight, preferred_element_type=jnp.float32)
        .astype(jnp.bfloat16)
        .reshape(rows, cols, inner)
    )
    both = jnp.concatenate([keys, values], axis=2)
    above = ring(both[rows - RADIUS :], "lat", 1)
    below = ring(both[:RADIUS], "lat", -1)
    extended = jnp.concatenate([above, both, below], axis=0)
    west = ring(extended[:, cols - SIDE :], "lon", 1)
    east = ring(extended[:, :SIDE], "lon", -1)
    halo = jnp.concatenate([west, east], axis=1)
    grad_query, own, left, right, weight_term = attention(
        base, queries, grads, extended, halo, up_flat, lat_total
    )
    from_east = ring(left, "lon", -1)
    from_west = ring(right, "lon", 1)
    sums = own + jnp.concatenate([from_west, from_east], axis=1).astype(jnp.float32)
    from_below = line(sums[:RADIUS].astype(jnp.bfloat16), "lat", -1)
    from_above = line(sums[RADIUS + rows :].astype(jnp.bfloat16), "lat", 1)
    owned = sums[RADIUS : RADIUS + rows] + jnp.concatenate(
        [from_above, from_below], axis=0
    ).astype(jnp.float32)
    grad_key = owned[:, :, :inner].astype(jnp.bfloat16)
    grad_value = owned[:, :, inner:].astype(jnp.bfloat16)
    grad_weight = reduce_weight(weight_term, inner // lax.axis_size("lon")) / lat_total
    return (grad_query, grad_key, grad_value, grad_weight)


def solution(mesh):
    placed = P("lat", "lon", None)
    return jax.shard_map(
        shards,
        mesh=mesh,
        in_specs=(placed, placed, placed, placed, P()),
        out_specs=(placed, placed, placed, P("lon", None)),
        check_vma=False,
    )
```

time: 490 us -> 126 us (0.26)
  waiting for transfers between devices: 282 us -> 34.2 us
  blocking collectives: 48.6 us -> 0 us
  local copies, waits for them, and re-layouts: 49.6 us -> 5.41 us
  matrix products: 26.7 us -> 0.5 us
  starting transfers between devices: 44 us -> 68.4 us
  other arithmetic: 22.9 us -> 8.42 us
  between operations: 14.2 us -> 0.88 us
  Pallas kernels: 0 us -> 6.17 us
    reduce_scatter x1 -> x0, waiting for transfers between devices: 248 us -> none  [shards(): lax.psum_scatter(jnp.einsum('ti,td->id', attended_flat, out_flat, preferr...]
    psum x1 -> x0, blocking collectives: 48.6 us -> none  [shards(): lax.psum(lon_share.astype(jnp.bfloat16), 'lat').astype(jnp.float32)]
    dot_general x20 -> x1, matrix products: 26.7 us -> 0.5 us  [shards(): jnp.einsum('td,id->ti', up_flat, out_weight, preferred_element_type=jnp.f...]
    all_to_all x0 -> x3, starting transfers between devices: none -> 21.8 us  [the longest x1 9.67 us: reduce_weight(): every = lax.all_to_all(copies, 'lat', 0, 0, tiled=True)]
    reshape x36 -> x0, local copies, waits for them, and re-layouts: 20.4 us -> none  [the longest x6 5.75 us: forward_strip(): slab[:, :, inner_width:].reshape(slab_count, head_count, head_size)]
    dynamic_update_slice x3 -> x0, other arithmetic: 12.2 us -> none  [forward_strip(): lax.dynamic_update_slice_in_dim(sums_all, previous + slab_sums, first, 0)]
    all_to_all x0 -> x3, waiting for transfers between devices: none -> 10.3 us  [the longest x1 7.75 us: reduce_weight(): every = lax.all_to_all(copies, 'lat', 0, 0, tiled=True)]
    ppermute x8 -> x9, waiting for transfers between devices: 33.7 us -> 23.9 us  [the longest x6 18.6 us: ring(): lax.ppermute(block, axis, [(i, (i + by) % size) for i in range(size)])]
  transfers between devices with their start and end apart: 9 -> 12, of which waited for: 9 -> 8; matrix products, arithmetic and copies ran while one was open for 1% -> 6% of each run, Pallas kernels for 0% -> 0%
where the time goes in v1:
time: 126 us; the launch traced here: 124 us
  starting transfers between devices  68.4 us (54%)
  waiting for transfers between devices  34.2 us (27%)
  other arithmetic  8.42 us (7%)
  Pallas kernels  6.17 us (5%)
  local copies, waits for them, and re-layouts  5.41 us (4%)
    ppermute x6, starting transfers between devices, ring(): lax.ppermute(block, axis, [(i, (i + by) % size) for i in range(size)])  32.6 us
    ppermute x6, waiting for transfers between devices, ring(): lax.ppermute(block, axis, [(i, (i + by) % size) for i in range(size)])  18.6 us
    ppermute x2, starting transfers between devices, line(): lax.ppermute(block, axis, [(i, i + by) for i in range(size) if 0 <= i + b...  10.6 us
    all_to_all x1, starting transfers between devices, reduce_weight(): every = lax.all_to_all(copies, 'lat', 0, 0, tiled=True)  9.67 us
    all_to_all x1, starting transfers between devices, reduce_weight(): lax.all_to_all(half.reshape(far, near * out_rows, model), 'lon', 0, 0, ax...  8.25 us
    all_to_all x1, waiting for transfers between devices, reduce_weight(): every = lax.all_to_all(copies, 'lat', 0, 0, tiled=True)  7.75 us
    pallas_call x1, Pallas kernels, attention(): pl.pallas_call(functools.partial(attention_kernel, lat_total), out_shape=...  6.17 us
    ppermute x2, waiting for transfers between devices, line(): lax.ppermute(block, axis, [(i, i + by) for i in range(size) if 0 <= i + b...  5.32 us
  transfers between devices with their start and end apart: 12, of which 8 were waited for; matrix products, arithmetic and copies ran while one was open for 6% of the time, Pallas kernels for 0%

profile of v1, /device:TPU:6, one launch (start us, length us, event | category | flops | bytes accessed | tf_op | source)
XLA Modules:
  0.0 124.0 jit_solution(8206302687040531153)
XLA Ops:
  0.6 1.0 constant_dynamic-update-slice_fusion.1
  1.7 0.9 constant_dynamic-update-slice_fusion
  2.7 10.9 %collective-permute-start = (bf16[6,16,1024]{2,1,0:T(8,128)(2,1)S(1)}, bf16[6,16,1024]{2,1,0:T(8,128)(2,1)S(1)}, u32[]{:S(2)}, u32[]{:S(2)}) collective-permute-start(bf16[6,16,1024]{2,1,0:T(8,128)(2,1)S(1)} %get-tuple-element.22), channel_id=1, source_target_pairs={{0,64},{64,128},{128,192},{192,256},{256,320},{320,384},{384,448},... | collective-permute-start | bytes 589832 | tf_op jit(solution)/shard_map/ppermute | solution.py:163
  13.6 2.3 %collective-permute-start.1 = (bf16[6,16,1024]{2,1,0:T(8,128)(2,1)S(1)}, bf16[6,16,1024]{2,1,0:T(8,128)(2,1)S(1)}, u32[]{:S(2)}, u32[]{:S(2)}) collective-permute-start(bf16[6,16,1024]{2,1,0:T(8,128)(2,1)S(1)} %get-tuple-element.23), channel_id=1, source_target_pairs={{0,448},{64,0},{128,64},{192,128},{256,192},{320,256},{384,320},{4... | collective-permute-start | bytes 589832 | tf_op jit(solution)/shard_map/ppermute | solution.py:163
  15.9 6.9 %collective-permute-done = bf16[6,16,1024]{2,1,0:T(8,128)(2,1)S(1)} collective-permute-done((bf16[6,16,1024]{2,1,0:T(8,128)(2,1)S(1)}, bf16[6,16,1024]{2,1,0:T(8,128)(2,1)S(1)}, u32[]{:S(2)}, u32[]{:S(2)}) %collective-permute-start) | collective-permute-done | bytes 196640 | tf_op jit(solution)/shard_map/ppermute | solution.py:163
  22.8 7.0 %collective-permute-done.1 = bf16[6,16,1024]{2,1,0:T(8,128)(2,1)S(1)} collective-permute-done((bf16[6,16,1024]{2,1,0:T(8,128)(2,1)S(1)}, bf16[6,16,1024]{2,1,0:T(8,128)(2,1)S(1)}, u32[]{:S(2)}, u32[]{:S(2)}) %collective-permute-start.1) | collective-permute-done | bytes 196640 | tf_op jit(solution)/shard_map/ppermute | solution.py:163
  30.0 1.9 %collective-permute-start.2 = (bf16[24,8,1024]{2,1,0:T(8,128)(2,1)S(1)}, bf16[24,8,1024]{2,1,0:T(8,128)(2,1)S(1)}, u32[]{:S(2)}, u32[]{:S(2)}) collective-permute-start(bf16[24,8,1024]{2,1,0:T(8,128)(2,1)S(1)} %get-tuple-element.18), channel_id=1, source_target_pairs={{0,1},{1,2},{2,3},{3,4},{4,5},{5,6},{6,7},{7,8},{8,9},{9,10},{10,1... | collective-permute-start | bytes 1179656 | tf_op jit(solution)/shard_map/ppermute | solution.py:163
  31.9 7.6 %collective-permute-start.3 = (bf16[24,8,1024]{2,1,0:T(8,128)(2,1)S(1)}, bf16[24,8,1024]{2,1,0:T(8,128)(2,1)}, u32[]{:S(2)}, u32[]{:S(2)}) collective-permute-start(bf16[24,8,1024]{2,1,0:T(8,128)(2,1)S(1)} %get-tuple-element.19), channel_id=1, source_target_pairs={{0,63},{1,0},{2,1},{3,2},{4,3},{5,4},{6,5},{7,6},{8,7},{9,8},{10,9... | collective-permute-start | bytes 1179656 | tf_op jit(solution)/shard_map/ppermute | solution.py:163
  40.0 3.1 %collective-permute-done.2 = bf16[24,8,1024]{2,1,0:T(8,128)(2,1)S(1)} collective-permute-done((bf16[24,8,1024]{2,1,0:T(8,128)(2,1)S(1)}, bf16[24,8,1024]{2,1,0:T(8,128)(2,1)S(1)}, u32[]{:S(2)}, u32[]{:S(2)}) %collective-permute-start.2) | collective-permute-done | bytes 393248 | tf_op jit(solution)/shard_map/ppermute | solution.py:163
  43.2 1.6 %collective-permute-done.3 = bf16[24,8,1024]{2,1,0:T(8,128)(2,1)} collective-permute-done((bf16[24,8,1024]{2,1,0:T(8,128)(2,1)S(1)}, bf16[24,8,1024]{2,1,0:T(8,128)(2,1)}, u32[]{:S(2)}, u32[]{:S(2)}) %collective-permute-start.3) | collective-permute-done | bytes 393248 | tf_op jit(solution)/shard_map/ppermute | solution.py:163
  44.7 1.1 pad_maximum_fusion.1.halo_ref
  45.8 6.2 %shard_map.84 = (bf16[12,16,512]{2,1,0:T(8,128)(2,1)}, f32[24,16,1024]{2,1,0:T(8,128)S(1)}, bf16[24,8,1024]{2,1,0:T(8,128)(2,1)S(1)}, bf16[24,8,1024]{2,1,0:T(8,128)(2,1)S(1)}, bf16[512,1024]{1,0:T(8,128)(2,1)S(1)}) custom-call(s32[1]{0:T(128)} %bitcast.base_ref, bf16[12,16,512]{2,1,0:T(8,128)(2,1)S(1)} %copy-done.6, bf16[12,16,512]{2,1,0:T(8,128)(2,1)S(1)} %bitcast.18, ...), custom_call_target="tpu_custom_call" | custom-call | flops 2600000000 | bytes 8000000 | tf_op jit(solution)/shard_map/pallas_call | solution.py:134
  52.0 1.0 copy-done.1
  53.0 0.9 dynamic-slice_bitcast_fusion
  53.8 3.4 %collective-permute-start.8 = (bf16[8,4,8,1024]{3,2,1,0:T(8,128)(2,1)}, bf16[8,4,8,1024]{3,2,1,0:T(8,128)(2,1)S(1)}, u32[]{:S(2)}, u32[]{:S(2)}) collective-permute-start(bf16[8,4,8,1024]{3,2,1,0:T(8,128)(2,1)} %dynamic-slice_bitcast_fusion), channel_id=1, source_target_pairs={{0,1},{1,0},{2,3},{3,2},{4,5},{5,4},{6,7},{7,6},{8,9},{9,8},{10,11... | collective-permute-start | bytes 1572872 | tf_op jit(solution)/shard_map/ppermute | solution.py:183
  57.2 1.9 %collective-permute-start.4 = (bf16[24,8,1024]{2,1,0:T(8,128)(2,1)}, bf16[24,8,1024]{2,1,0:T(8,128)(2,1)}, u32[]{:S(2)}, u32[]{:S(2)}) collective-permute-start(bf16[24,8,1024]{2,1,0:T(8,128)(2,1)} %copy-done.5), channel_id=1, source_target_pairs={{0,1},{1,2},{2,3},{3,4},{4,5},{5,6},{6,7},{7,8},{8,9},{9,10},{10,1... | collective-permute-start | bytes 1179656 | tf_op jit(solution)/shard_map/ppermute | solution.py:163
  59.2 8.0 %collective-permute-start.5 = (bf16[24,8,1024]{2,1,0:T(8,128)(2,1)}, bf16[24,8,1024]{2,1,0:T(8,128)(2,1)}, u32[]{:S(2)}, u32[]{:S(2)}) collective-permute-start(bf16[24,8,1024]{2,1,0:T(8,128)(2,1)} %copy-done.4), channel_id=1, source_target_pairs={{0,63},{1,0},{2,1},{3,2},{4,3},{5,4},{6,5},{7,6},{8,7},{9,8},{10,9... | collective-permute-start | bytes 1179656 | tf_op jit(solution)/shard_map/ppermute | solution.py:163
  67.2 2.1 %fusion.2 = bf16[8,32,1024]{2,1,0:T(8,128)(2,1)} fusion(bf16[8,4,8,1024]{3,2,1,0:T(8,128)(2,1)S(1)} %collective-permute-done.8, bf16[8,4,2,8,1024]{4,3,2,1,0:T(8,128)(2,1)} %bitcast.15, s32[]{:T(128)S(6)} %select_n.15), kind=kLoop, calls=%fused_computation.8 | loop fusion | flops 1048576 | bytes 1572868 | tf_op jit(solution)/shard_map/reshape | solution.py:188
  69.2 8.3 %all-to-all-start = ((bf16[8,32,1024]{2,1,0:T(8,128)(2,1)}), bf16[8,32,1024]{2,1,0:T(8,128)(2,1)S(1)}, u32[]{:S(2)}, u32[]{:S(2)}) async-start(bf16[8,32,1024]{2,1,0:T(8,128)(2,1)} %fusion.2), calls=%async_computation | async-start | bytes 1048576 | tf_op jit(solution)/shard_map/all_to_all | solution.py:187
  77.5 2.6 %fusion.3 = (bf16[24,16,1024]{2,1,0:T(8,128)(2,1)S(1)}, f32[24,16,1024]{2,1,0:T(8,128)}) fusion(f32[24,16,1024]{2,1,0:T(8,128)S(1)} %get-tuple-element.10, bf16[24,8,1024]{2,1,0:T(8,128)(2,1)} %collective-permute-done.5, bf16[24,8,1024]{2,1,0:T(8,128)(2,1)} %collective-permute-done.4), kind=kLoop, calls=%fused_computation.14 | loop fusion | flops 2359296 | bytes 4718592 | tf_op jit(solution)/shard_map/convert.6
  80.1 7.9 %collective-permute-start.6 = (bf16[6,16,1024]{2,1,0:T(8,128)(2,1)S(1)}, bf16[6,16,1024]{2,1,0:T(8,128)(2,1)S(1)}, u32[]{:S(2)}, u32[]{:S(2)}) collective-permute-start(bf16[6,16,1024]{2,1,0:T(8,128)(2,1)S(1)} %get-tuple-element.16), channel_id=1, source_target_pairs={{0,64},{64,128},{128,192},{192,256},{256,320},{320,384},{384,448},... | collective-permute-start | bytes 589832 | tf_op jit(solution)/shard_map/ppermute | solution.py:168
  88.0 2.8 %collective-permute-start.7 = (bf16[6,16,1024]{2,1,0:T(8,128)(2,1)S(1)}, bf16[6,16,1024]{2,1,0:T(8,128)(2,1)S(1)}, u32[]{:S(2)}, u32[]{:S(2)}) collective-permute-start(bf16[6,16,1024]{2,1,0:T(8,128)(2,1)S(1)} %get-tuple-element.17), channel_id=1, source_target_pairs={{64,0},{128,64},{192,128},{256,192},{320,256},{384,320},{448,384},... | collective-permute-start | bytes 589832 | tf_op jit(solution)/shard_map/ppermute | solution.py:168
  90.8 0.7 all-to-all-done
  91.5 0.7 reduce_sum.33
  92.2 3.9 %all-to-all-start.1 = ((bf16[4,8,1024]{2,1,0:T(8,128)(2,1)}), bf16[4,8,1024]{2,1,0:T(8,128)(2,1)S(1)}, u32[]{:S(2)}, u32[]{:S(2)}) async-start(bf16[4,8,1024]{2,1,0:T(8,128)(2,1)} %bitcast.7), calls=%async_computation.1 | async-start | bytes 131072 | tf_op jit(solution)/shard_map/all_to_all | solution.py:194
  96.1 5.3 %collective-permute-done.7 = bf16[6,16,1024]{2,1,0:T(8,128)(2,1)S(1)} collective-permute-done((bf16[6,16,1024]{2,1,0:T(8,128)(2,1)S(1)}, bf16[6,16,1024]{2,1,0:T(8,128)(2,1)S(1)}, u32[]{:S(2)}, u32[]{:S(2)}) %collective-permute-start.7) | collective-permute-done | bytes 196640 | tf_op jit(solution)/shard_map/ppermute | solution.py:168
  101.4 1.2 fusion.1
  102.6 1.9 %all-to-all-done.1 = bf16[4,8,1024]{2,1,0:T(8,128)(2,1)S(1)} async-done(((bf16[4,8,1024]{2,1,0:T(8,128)(2,1)}), bf16[4,8,1024]{2,1,0:T(8,128)(2,1)S(1)}, u32[]{:S(2)}, u32[]{:S(2)}) %all-to-all-start.1) | async-done | bytes 65568 | tf_op jit(solution)/shard_map/all_to_all | solution.py:194
  104.5 0.7 broadcast_in_dim.2
  105.2 9.7 %all-to-all-start.2 = ((bf16[8,8,1024]{2,1,0:T(8,128)(2,1)}), bf16[8,8,1024]{2,1,0:T(8,128)(2,1)S(1)}, u32[]{:S(2)}, u32[]{:S(2)}) async-start(bf16[8,8,1024]{2,1,0:T(8,128)(2,1)} %broadcast_in_dim.2), calls=%async_computation.2 | async-start | bytes 262144 | tf_op jit(solution)/shard_map/all_to_all | solution.py:200
  114.8 0.8 fusion.6
  115.6 7.7 %all-to-all-done.2 = bf16[8,8,1024]{2,1,0:T(8,128)(2,1)S(1)} async-done(((bf16[8,8,1024]{2,1,0:T(8,128)(2,1)}), bf16[8,8,1024]{2,1,0:T(8,128)(2,1)S(1)}, u32[]{:S(2)}, u32[]{:S(2)}) %all-to-all-start.2) | async-done | bytes 131104 | tf_op jit(solution)/shard_map/all_to_all | solution.py:200
  (25 shorter events, 1.4 us)
Async XLA Ops:
  0.6 38.9 %copy-start = (bf16[512,1024]{1,0:T(8,128)(2,1)S(1)}, bf16[512,1024]{1,0:T(8,128)(2,1)}, u32[]{:S(2)}) copy-start(bf16[512,1024]{1,0:T(8,128)(2,1)} %param.9) | copy-start | bytes 3145732
  2.7 20.2 %collective-permute-start = (bf16[6,16,1024]{2,1,0:T(8,128)(2,1)S(1)}, bf16[6,16,1024]{2,1,0:T(8,128)(2,1)S(1)}, u32[]{:S(2)}, u32[]{:S(2)}) collective-permute-start(bf16[6,16,1024]{2,1,0:T(8,128)(2,1)S(1)} %get-tuple-element.22), channel_id=1, source_target_pairs={{0,64},{64,128},{128,192},{192,256},{256,320},{320,384},{384,448},... | collective-permute-start | bytes 589832 | tf_op jit(solution)/shard_map/ppermute | solution.py:163
  13.6 25.9 %copy-start.2 = (bf16[12,16,1024]{2,1,0:T(8,128)(2,1)S(1)}, bf16[12,16,1024]{2,1,0:T(8,128)(2,1)}, u32[]{:S(2)}) copy-start(bf16[12,16,1024]{2,1,0:T(8,128)(2,1)} %param.8) | copy-start | bytes 1179652
  13.6 16.2 %collective-permute-start.1 = (bf16[6,16,1024]{2,1,0:T(8,128)(2,1)S(1)}, bf16[6,16,1024]{2,1,0:T(8,128)(2,1)S(1)}, u32[]{:S(2)}, u32[]{:S(2)}) collective-permute-start(bf16[6,16,1024]{2,1,0:T(8,128)(2,1)S(1)} %get-tuple-element.23), channel_id=1, source_target_pairs={{0,448},{64,0},{128,64},{192,128},{256,192},{320,256},{384,320},{4... | collective-permute-start | bytes 589832 | tf_op jit(solution)/shard_map/ppermute | solution.py:163
  30.0 13.2 %collective-permute-start.2 = (bf16[24,8,1024]{2,1,0:T(8,128)(2,1)S(1)}, bf16[24,8,1024]{2,1,0:T(8,128)(2,1)S(1)}, u32[]{:S(2)}, u32[]{:S(2)}) collective-permute-start(bf16[24,8,1024]{2,1,0:T(8,128)(2,1)S(1)} %get-tuple-element.18), channel_id=1, source_target_pairs={{0,1},{1,2},{2,3},{3,4},{4,5},{5,6},{6,7},{7,8},{8,9},{9,10},{10,1... | collective-permute-start | bytes 1179656 | tf_op jit(solution)/shard_map/ppermute | solution.py:163
  31.9 12.8 %collective-permute-start.3 = (bf16[24,8,1024]{2,1,0:T(8,128)(2,1)S(1)}, bf16[24,8,1024]{2,1,0:T(8,128)(2,1)}, u32[]{:S(2)}, u32[]{:S(2)}) collective-permute-start(bf16[24,8,1024]{2,1,0:T(8,128)(2,1)S(1)} %get-tuple-element.19), channel_id=1, source_target_pairs={{0,63},{1,0},{2,1},{3,2},{4,3},{5,4},{6,5},{7,6},{8,7},{9,8},{10,9... | collective-permute-start | bytes 1179656 | tf_op jit(solution)/shard_map/ppermute | solution.py:163
  39.5 6.3 %copy-start.3 = (bf16[12,16,1024]{2,1,0:T(8,128)(2,1)S(1)}, bf16[12,16,1024]{2,1,0:T(8,128)(2,1)}, u32[]{:S(2)}) copy-start(bf16[12,16,1024]{2,1,0:T(8,128)(2,1)} %param.8) | copy-start | bytes 1179652
  39.5 6.3 %copy-start.6 = (bf16[12,16,512]{2,1,0:T(8,128)(2,1)S(1)}, bf16[12,16,512]{2,1,0:T(8,128)(2,1)}, u32[]{:S(2)}) copy-start(bf16[12,16,512]{2,1,0:T(8,128)(2,1)} %q_ref.1) | copy-start | bytes 589828
  52.0 1.0 copy-start.1
  52.0 1.8 %copy-start.4 = (bf16[24,8,1024]{2,1,0:T(8,128)(2,1)}, bf16[24,8,1024]{2,1,0:T(8,128)(2,1)S(1)}, u32[]{:S(2)}) copy-start(bf16[24,8,1024]{2,1,0:T(8,128)(2,1)S(1)} %get-tuple-element.12) | copy-start | bytes 1179652
  52.0 1.8 %copy-start.5 = (bf16[24,8,1024]{2,1,0:T(8,128)(2,1)}, bf16[24,8,1024]{2,1,0:T(8,128)(2,1)S(1)}, u32[]{:S(2)}) copy-start(bf16[24,8,1024]{2,1,0:T(8,128)(2,1)S(1)} %get-tuple-element.11) | copy-start | bytes 1179652
  53.8 13.3 %collective-permute-start.8 = (bf16[8,4,8,1024]{3,2,1,0:T(8,128)(2,1)}, bf16[8,4,8,1024]{3,2,1,0:T(8,128)(2,1)S(1)}, u32[]{:S(2)}, u32[]{:S(2)}) collective-permute-start(bf16[8,4,8,1024]{3,2,1,0:T(8,128)(2,1)} %dynamic-slice_bitcast_fusion), channel_id=1, source_target_pairs={{0,1},{1,0},{2,3},{3,2},{4,5},{5,4},{6,7},{7,6},{8,9},{9,8},{10,11... | collective-permute-start | bytes 1572872 | tf_op jit(solution)/shard_map/ppermute | solution.py:183
  57.2 20.3 %collective-permute-start.4 = (bf16[24,8,1024]{2,1,0:T(8,128)(2,1)}, bf16[24,8,1024]{2,1,0:T(8,128)(2,1)}, u32[]{:S(2)}, u32[]{:S(2)}) collective-permute-start(bf16[24,8,1024]{2,1,0:T(8,128)(2,1)} %copy-done.5), channel_id=1, source_target_pairs={{0,1},{1,2},{2,3},{3,4},{4,5},{5,6},{6,7},{7,8},{8,9},{9,10},{10,1... | collective-permute-start | bytes 1179656 | tf_op jit(solution)/shard_map/ppermute | solution.py:163
  59.2 18.3 %collective-permute-start.5 = (bf16[24,8,1024]{2,1,0:T(8,128)(2,1)}, bf16[24,8,1024]{2,1,0:T(8,128)(2,1)}, u32[]{:S(2)}, u32[]{:S(2)}) collective-permute-start(bf16[24,8,1024]{2,1,0:T(8,128)(2,1)} %copy-done.4), channel_id=1, source_target_pairs={{0,63},{1,0},{2,1},{3,2},{4,3},{5,4},{6,5},{7,6},{8,7},{9,8},{10,9... | collective-permute-start | bytes 1179656 | tf_op jit(solution)/shard_map/ppermute | solution.py:163
  69.2 22.2 %all-to-all-start = ((bf16[8,32,1024]{2,1,0:T(8,128)(2,1)}), bf16[8,32,1024]{2,1,0:T(8,128)(2,1)S(1)}, u32[]{:S(2)}, u32[]{:S(2)}) async-start(bf16[8,32,1024]{2,1,0:T(8,128)(2,1)} %fusion.2), calls=%async_computation | async-start | bytes 1048576 | tf_op jit(solution)/shard_map/all_to_all | solution.py:187
  80.1 15.9 %collective-permute-start.6 = (bf16[6,16,1024]{2,1,0:T(8,128)(2,1)S(1)}, bf16[6,16,1024]{2,1,0:T(8,128)(2,1)S(1)}, u32[]{:S(2)}, u32[]{:S(2)}) collective-permute-start(bf16[6,16,1024]{2,1,0:T(8,128)(2,1)S(1)} %get-tuple-element.16), channel_id=1, source_target_pairs={{0,64},{64,128},{128,192},{192,256},{256,320},{320,384},{384,448},... | collective-permute-start | bytes 589832 | tf_op jit(solution)/shard_map/ppermute | solution.py:168
  88.0 13.4 %collective-permute-start.7 = (bf16[6,16,1024]{2,1,0:T(8,128)(2,1)S(1)}, bf16[6,16,1024]{2,1,0:T(8,128)(2,1)S(1)}, u32[]{:S(2)}, u32[]{:S(2)}) collective-permute-start(bf16[6,16,1024]{2,1,0:T(8,128)(2,1)S(1)} %get-tuple-element.17), channel_id=1, source_target_pairs={{64,0},{128,64},{192,128},{256,192},{320,256},{384,320},{448,384},... | collective-permute-start | bytes 589832 | tf_op jit(solution)/shard_map/ppermute | solution.py:168
  92.2 12.3 %all-to-all-start.1 = ((bf16[4,8,1024]{2,1,0:T(8,128)(2,1)}), bf16[4,8,1024]{2,1,0:T(8,128)(2,1)S(1)}, u32[]{:S(2)}, u32[]{:S(2)}) async-start(bf16[4,8,1024]{2,1,0:T(8,128)(2,1)} %bitcast.7), calls=%async_computation.1 | async-start | bytes 131072 | tf_op jit(solution)/shard_map/all_to_all | solution.py:194
  105.2 18.2 %all-to-all-start.2 = ((bf16[8,8,1024]{2,1,0:T(8,128)(2,1)}), bf16[8,8,1024]{2,1,0:T(8,128)(2,1)S(1)}, u32[]{:S(2)}, u32[]{:S(2)}) async-start(bf16[8,8,1024]{2,1,0:T(8,128)(2,1)} %broadcast_in_dim.2), calls=%async_computation.2 | async-start | bytes 262144 | tf_op jit(solution)/shard_map/all_to_all | solution.py:200

commit v2 on v1

v2 whole, which is shorter than its diff:
```python
import functools

import jax
import jax.numpy as jnp
from jax import lax
from jax.experimental import pallas as pl
from jax.experimental.pallas import tpu as pltpu
from jax.sharding import PartitionSpec as P

HEADS = 8
RADIUS = 6
SIDE = 8
STRIP = 4
PACK = 4

NT = (((1,), (1,)), ((), ()))
NN = (((1,), (0,)), ((), ()))


def mm(a, b, dims):
    return lax.dot_general(a, b, dims, preferred_element_type=jnp.float32)


def spread(block, diag):
    tall = jnp.concatenate([block.astype(jnp.float32)] * PACK, axis=0)
    return jnp.where(diag, tall, 0.0).astype(jnp.bfloat16)


def diagonal(square, head, strip_q):
    return jnp.concatenate(
        [square[h * head : (h + 1) * head, h * strip_q : (h + 1) * strip_q] for h in range(PACK)],
        axis=0,
    )


def masks(rows, cols, inner):
    head = inner // HEADS
    wide = cols + 2 * SIDE
    strip_q = STRIP * cols
    slab = (STRIP + 2 * RADIUS) * wide
    lanes = PACK * strip_q
    key = lax.broadcasted_iota(jnp.int32, (slab, lanes), 0)
    query = lax.broadcasted_iota(jnp.int32, (slab, lanes), 1) & (strip_q - 1)
    row = key // wide
    place = key & (wide - 1)
    col = jnp.where(
        place < cols, place, jnp.where(place < cols + SIDE, place - cols - SIDE, place - SIDE)
    )
    row_gap = row - query // cols
    col_gap = jnp.abs(col - (query & (cols - 1)))
    near = (row_gap >= 0) & (row_gap <= 2 * RADIUS) & (col_gap <= RADIUS)
    diag = (lax.broadcasted_iota(jnp.int32, (lanes, PACK * head), 0) // strip_q) == (
        lax.broadcasted_iota(jnp.int32, (lanes, PACK * head), 1) // head
    )
    return near, row, diag


def forward_kernel(
    lat_total, place_ref, q_ref, ext_ref, west_ref, east_ref, up_ref,
    kv_ref, norm_ref, keep_ref, give_ref, vt, att_t,
):
    rows, cols, inner = q_ref.shape
    ext_rows = rows + 2 * RADIUS
    wide = cols + 2 * SIDE
    head = inner // HEADS
    scale = head ** (-0.5)
    group = PACK * head
    strip_q = STRIP * cols
    slab_rows = STRIP + 2 * RADIUS
    slab = slab_rows * wide
    base, core = place_ref[0], place_ref[1]

    kv_ref[:, 0:cols, :] = ext_ref[...]
    kv_ref[:, cols:wide, :] = jnp.concatenate(
        [west_ref[...].astype(jnp.float32), east_ref[...].astype(jnp.float32)], axis=1
    ).astype(jnp.bfloat16)
    vt[...] = kv_ref[:, :, inner:].reshape(ext_rows * wide, inner).T
    near, row, diag = masks(rows, cols, inner)

    for s in range(rows // STRIP):
        first = s * STRIP
        low = RADIUS - base - first
        allowed = near & (row >= low) & (row < low + lat_total)
        window = slice(first * wide, first * wide + slab)
        here = slice(s * strip_q, (s + 1) * strip_q)
        for part in range(HEADS // PACK):
            chans = slice(part * group, (part + 1) * group)
            keys = kv_ref[first : first + slab_rows, :, chans].reshape(slab, group)
            q_wide = spread(
                q_ref[first : first + STRIP, :, chans].reshape(strip_q, group) * scale, diag
            )
            scores = jnp.where(allowed, mm(keys, q_wide, NT), -1e30)
            top = jnp.max(scores, axis=0, keepdims=True)
            weights = jnp.exp(scores - top)
            total = jnp.sum(weights, axis=0, keepdims=True)
            probs = (weights * (1.0 / total)).astype(jnp.bfloat16)
            at = s * (HEADS // PACK) + part
            norm_ref[at : at + 1, :] = top + jnp.log(total)
            att_t[chans, here] = diagonal(mm(vt[chans, window], probs, NN), head, strip_q)

    weight = mm(att_t[...].astype(jnp.bfloat16), up_ref[...], NN)
    out_rows = keep_ref.shape[1]
    weight = weight.reshape(keep_ref.shape[0], 2, out_rows, weight.shape[1])
    keep_ref[...] = jnp.where(core == 0, weight[:, 0], weight[:, 1])
    give_ref[...] = jnp.where(core == 0, weight[:, 1], weight[:, 0]).astype(jnp.bfloat16)


def backward_kernel(
    lat_total, place_ref, q_ref, g_ref, kv_ref, norm_ref,
    dq_ref, mid_k_ref, mid_v_ref, rim_ref, left_ref, right_ref, kt, acc, dq_t,
):
    rows, cols, inner = q_ref.shape
    ext_rows = rows + 2 * RADIUS
    wide = cols + 2 * SIDE
    head = inner // HEADS
    scale = head ** (-0.5)
    group = PACK * head
    strip_q = STRIP * cols
    slab_rows = STRIP + 2 * RADIUS
    slab = slab_rows * wide
    base = place_ref[0]

    kt[...] = kv_ref[:, :, 0:inner].reshape(ext_rows * wide, inner).T
    acc[...] = jnp.zeros_like(acc)
    near, row, diag = masks(rows, cols, inner)

    for s in range(rows // STRIP):
        first = s * STRIP
        low = RADIUS - base - first
        allowed = near & (row >= low) & (row < low + lat_total)
        window = slice(first * wide, first * wide + slab)
        here = slice(s * strip_q, (s + 1) * strip_q)
        for part in range(HEADS // PACK):
            chans = slice(part * group, (part + 1) * group)
            vchans = slice(inner + part * group, inner + (part + 1) * group)
            keys = kv_ref[first : first + slab_rows, :, chans].reshape(slab, group)
            values = kv_ref[first : first + slab_rows, :, vchans].reshape(slab, group)
            q_wide = spread(
                q_ref[first : first + STRIP, :, chans].reshape(strip_q, group) * scale, diag
            )
            g_wide = spread(g_ref[first : first + STRIP, :, chans].reshape(strip_q, group), diag)
            at = s * (HEADS // PACK) + part
            scores = jnp.where(allowed, mm(keys, q_wide, NT), -1e30)
            probs = jnp.exp(scores - norm_ref[at : at + 1, :])
            low_probs = probs.astype(jnp.bfloat16)
            grad_prob = mm(values, g_wide, NT)
            delta = jnp.sum(low_probs.astype(jnp.float32) * grad_prob, axis=0, keepdims=True)
            grad_score = (probs * (grad_prob - delta)).astype(jnp.bfloat16)
            dq_t[chans, here] = diagonal(mm(kt[chans, window], grad_score, NN), head, strip_q) * scale
            acc[first : first + slab_rows, :, chans] += mm(grad_score, q_wide, NN).reshape(
                slab_rows, wide, group
            )
            acc[first : first + slab_rows, :, vchans] += mm(low_probs, g_wide, NN).reshape(
                slab_rows, wide, group
            )

    left_ref[...] = acc[:, cols : cols + SIDE, :].astype(jnp.bfloat16)
    right_ref[...] = acc[:, cols + SIDE : wide, :].astype(jnp.bfloat16)
    rim_ref[0:RADIUS] = acc[0:RADIUS, 0:cols, :]
    rim_ref[RADIUS:] = acc[RADIUS + rows :, 0:cols, :]
    mid_k_ref[...] = acc[RADIUS : RADIUS + rows, 0:cols, 0:inner]
    mid_v_ref[...] = acc[RADIUS : RADIUS + rows, 0:cols, inner:]
    dq_ref[...] = dq_t[...].T.astype(jnp.bfloat16).reshape(rows, cols, inner)


def share_kernel(parts_ref, copies_ref):
    total = jnp.sum(parts_ref[...].astype(jnp.float32), axis=0).astype(jnp.bfloat16)
    copies_ref[...] = jnp.broadcast_to(total[None], copies_ref.shape)


def pack_kernel(keys_ref, values_ref, both_ref):
    inner = keys_ref.shape[2]
    both_ref[:, :, 0:inner] = keys_ref[...]
    both_ref[:, :, inner:] = values_ref[...]


def wide(block):
    return block.astype(jnp.float32)


def rim_kernel(rim_ref, west_ref, east_ref, top_ref, bottom_ref):
    deep = top_ref.shape[0]
    for out, at, there in (
        (top_ref, 0, 0),
        (bottom_ref, deep, west_ref.shape[0] - deep),
    ):
        side = jnp.concatenate(
            [wide(west_ref[there : there + deep]), wide(east_ref[there : there + deep])], axis=1
        )
        out[...] = (rim_ref[at : at + deep] + side).astype(jnp.bfloat16)


def finish_kernel(
    mid_k_ref, mid_v_ref, west_ref, east_ref, above_ref, below_ref, keys_ref, values_ref
):
    inner = mid_k_ref.shape[2]
    deep = above_ref.shape[0]
    for out, mid, chans in (
        (keys_ref, mid_k_ref, slice(0, inner)),
        (values_ref, mid_v_ref, slice(inner, 2 * inner)),
    ):
        for at, pole in ((0, above_ref), (deep, below_ref)):
            there = slice(deep + at, 2 * deep + at)
            side = jnp.concatenate(
                [wide(west_ref[there, :, chans]), wide(east_ref[there, :, chans])], axis=1
            )
            total = mid[at : at + deep] + side + wide(pole[:, :, chans])
            out[at : at + deep] = total.astype(jnp.bfloat16)


VMEM = pl.BlockSpec(memory_space=pltpu.VMEM)
SMEM = pl.BlockSpec(memory_space=pltpu.SMEM)
PARAMS = pltpu.CompilerParams(vmem_limit_bytes=20 << 20)
SMALL = pltpu.CompilerParams(vmem_limit_bytes=8 << 20)


def shape(dims, kind=jnp.bfloat16):
    return jax.ShapeDtypeStruct(dims, kind)


def forward(place, queries, extended, west, east, upstream, lat_total, out_rows):
    rows, cols, inner = queries.shape
    ext_rows, wide = rows + 2 * RADIUS, cols + 2 * SIDE
    model = upstream.shape[1]
    return pl.pallas_call(
        functools.partial(forward_kernel, lat_total),
        out_shape=(
            shape((ext_rows, wide, 2 * inner)),
            shape((8, PACK * STRIP * cols), jnp.float32),
            shape((inner // (2 * out_rows), out_rows, model), jnp.float32),
            shape((inner // (2 * out_rows), out_rows, model)),
        ),
        in_specs=[SMEM] + [VMEM] * 5,
        out_specs=(VMEM,) * 4,
        scratch_shapes=[
            pltpu.VMEM((inner, ext_rows * wide), jnp.bfloat16),
            pltpu.VMEM((inner, rows * cols), jnp.float32),
        ],
        compiler_params=PARAMS,
        cost_estimate=pl.CostEstimate(
            flops=1_000_000_000, bytes_accessed=5_000_000, transcendentals=800_000
        ),
        name="forward",
    )(place, queries, extended, west, east, upstream)


def backward(place, queries, grads, kv, norm, lat_total):
    rows, cols, inner = queries.shape
    ext_rows, wide = rows + 2 * RADIUS, cols + 2 * SIDE
    return pl.pallas_call(
        functools.partial(backward_kernel, lat_total),
        out_shape=(
            shape((rows, cols, inner)),
            shape((rows, cols, inner), jnp.float32),
            shape((rows, cols, inner), jnp.float32),
            shape((2 * RADIUS, cols, 2 * inner), jnp.float32),
            shape((ext_rows, SIDE, 2 * inner)),
            shape((ext_rows, SIDE, 2 * inner)),
        ),
        in_specs=[SMEM] + [VMEM] * 4,
        out_specs=(VMEM,) * 6,
        scratch_shapes=[
            pltpu.VMEM((inner, ext_rows * wide), jnp.bfloat16),
            pltpu.VMEM((ext_rows, wide, 2 * inner), jnp.float32),
            pltpu.VMEM((inner, rows * cols), jnp.float32),
        ],
        compiler_params=PARAMS,
        cost_estimate=pl.CostEstimate(
            flops=20_000_000_000, bytes_accessed=70_000_000, transcendentals=800_000
        ),
        name="backward",
    )(place, queries, grads, kv, norm)


def ring(block, axis, by):
    size = lax.axis_size(axis)
    return lax.ppermute(block, axis, [(i, (i + by) % size) for i in range(size)])


def line(block, axis, by):
    size = lax.axis_size(axis)
    return lax.ppermute(
        block, axis, [(i, i + by) for i in range(size) if 0 <= i + by < size]
    )


def shards(queries, keys, values, upstream, out_weight):
    rows, cols, inner = queries.shape
    model = upstream.shape[2]
    tokens = rows * cols
    lat, lon = lax.axis_size("lat"), lax.axis_size("lon")
    lat_total = rows * lat
    out_rows = inner // lon
    place = jnp.stack([lax.axis_index("lat") * rows, lax.axis_index("lon") % 2]).astype(jnp.int32)
    up_flat = upstream.reshape(tokens, model)
    grads = (
        jnp.einsum("td,id->ti", up_flat, out_weight, preferred_element_type=jnp.float32)
        .astype(jnp.bfloat16)
        .reshape(rows, cols, inner)
    )
    both = pl.pallas_call(
        pack_kernel, out_shape=shape((rows, cols, 2 * inner)), name="pack", compiler_params=SMALL
    )(keys, values)
    above = line(both[rows - RADIUS :], "lat", 1)
    below = line(both[:RADIUS], "lat", -1)
    extended = jnp.concatenate([above, both, below], axis=0)
    west = ring(extended[:, cols - SIDE :], "lon", 1)
    east = ring(extended[:, :SIDE], "lon", -1)
    kv, norm, keep, give = forward(
        place, queries, extended, west, east, up_flat, lat_total, out_rows
    )
    got = lax.ppermute(give, "lon", [(i, i ^ 1) for i in range(lon)])
    half = (keep + got.astype(jnp.float32)).astype(jnp.bfloat16)
    same_core = [[2 * i + c for i in range(lon // 2)] for c in range(2)]
    terms = lax.all_to_all(half, "lon", 0, 0, axis_index_groups=same_core, tiled=True)

    grad_query, mid_k, mid_v, rim, left, right = backward(
        place, queries, grads, kv, norm, lat_total
    )
    from_east = ring(left, "lon", -1)
    from_west = ring(right, "lon", 1)
    rim, _ = lax.optimization_barrier((rim, half))
    top, bottom = pl.pallas_call(
        rim_kernel,
        out_shape=(shape((RADIUS, cols, 2 * inner)),) * 2,
        name="rim", compiler_params=SMALL,
    )(rim, from_west, from_east)
    from_below = line(top, "lat", -1)
    from_above = line(bottom, "lat", 1)
    terms, _ = lax.optimization_barrier((terms, top))
    copies = pl.pallas_call(
        share_kernel, out_shape=shape((lat, out_rows, model)), name="share", compiler_params=SMALL
    )(terms)
    every = lax.all_to_all(copies, "lat", 0, 0, tiled=True)
    grad_weight = jnp.sum(every.astype(jnp.float32), axis=0) / lat_total
    mid_k, mid_v, _ = lax.optimization_barrier((mid_k, mid_v, copies))
    grad_key, grad_value = pl.pallas_call(
        finish_kernel,
        out_shape=(shape((rows, cols, inner)),) * 2,
        name="finish", compiler_params=SMALL,
        cost_estimate=pl.CostEstimate(flops=50_000_000_000, bytes_accessed=4_000_000, transcendentals=0),
    )(mid_k, mid_v, from_west, from_east, from_above, from_below)
    return (grad_query, grad_key, grad_value, grad_weight)


def solution(mesh):
    placed = P("lat", "lon", None)
    return jax.shard_map(
        shards,
        mesh=mesh,
        in_specs=(placed, placed, placed, placed, P()),
        out_specs=(placed, placed, placed, P("lon", None)),
        check_vma=False,
    )
```

time: 126 us -> 123 us (0.976)
  the two profiles are of different devices: /device:TPU:6 before, /device:TPU:5 now
where the time goes in v2:
time: 123 us
  starting transfers between devices  58.4 us (47%)
  waiting for transfers between devices  44.1 us (36%)
  Pallas kernels  10.7 us (9%)
  local copies, waits for them, and re-layouts  6.33 us (5%)
  other arithmetic  1.76 us (1%)
    ppermute x4, starting transfers between devices, line(): lax.ppermute(block, axis, [(i, i + by) for i in range(size) if 0 <= i + b...  22.8 us
    ppermute x4, waiting for transfers between devices, ring(): lax.ppermute(block, axis, [(i, (i + by) % size) for i in range(size)])  21.1 us
    ppermute x4, waiting for transfers between devices, line(): lax.ppermute(block, axis, [(i, i + by) for i in range(size) if 0 <= i + b...  17.5 us
    ppermute x4, starting transfers between devices, ring(): lax.ppermute(block, axis, [(i, (i + by) % size) for i in range(size)])  14.7 us
    all_to_all x1, starting transfers between devices, shards(): lax.all_to_all(half, 'lon', 0, 0, axis_index_groups=same_core, tiled=True)  10.5 us
    all_to_all x1, starting transfers between devices, shards(): every = lax.all_to_all(copies, 'lat', 0, 0, tiled=True)  6.43 us
    pallas_call x1, Pallas kernels, backward(): pl.pallas_call(functools.partial(backward_kernel, lat_total), out_shape=(...  5.47 us
    unnamed x22, local copies, waits for them, and re-layouts  5.36 us
  transfers between devices with their start and end apart: 11, of which 9 were waited for; matrix products, arithmetic and copies ran while one was open for 0% of the time, Pallas kernels for 6%

profile of v2, /device:TPU:5, one launch (start us, length us, event | category | flops | bytes accessed | tf_op | source)
XLA Modules:
  0.0 122.7 jit_solution(6811492358773681207)
XLA Ops:
  0.7 1.0 copy-done.2
  1.7 0.9 copy-done.3
  2.7 10.6 %collective-permute-start = (bf16[6,16,1024]{2,1,0:T(8,128)(2,1)S(1)}, bf16[6,16,1024]{2,1,0:T(8,128)(2,1)S(1)}, u32[]{:S(2)}, u32[]{:S(2)}) collective-permute-start(bf16[6,16,1024]{2,1,0:T(8,128)(2,1)S(1)} %get-tuple-element.42), channel_id=1, source_target_pairs={{0,64},{64,128},{128,192},{192,256},{256,320},{320,384},{384,448},... | collective-permute-start | bytes 589832 | tf_op jit(solution)/shard_map/ppermute | solution.py:282
  13.3 2.1 %collective-permute-start.1 = (bf16[6,16,1024]{2,1,0:T(8,128)(2,1)S(1)}, bf16[6,16,1024]{2,1,0:T(8,128)(2,1)S(1)}, u32[]{:S(2)}, u32[]{:S(2)}) collective-permute-start(bf16[6,16,1024]{2,1,0:T(8,128)(2,1)S(1)} %get-tuple-element.43), channel_id=1, source_target_pairs={{64,0},{128,64},{192,128},{256,192},{320,256},{384,320},{448,384},... | collective-permute-start | bytes 589832 | tf_op jit(solution)/shard_map/ppermute | solution.py:282
  15.4 2.5 %collective-permute-done = bf16[6,16,1024]{2,1,0:T(8,128)(2,1)S(1)} collective-permute-done((bf16[6,16,1024]{2,1,0:T(8,128)(2,1)S(1)}, bf16[6,16,1024]{2,1,0:T(8,128)(2,1)S(1)}, u32[]{:S(2)}, u32[]{:S(2)}) %collective-permute-start) | collective-permute-done | bytes 196640 | tf_op jit(solution)/shard_map/ppermute | solution.py:282
  17.9 10.1 %collective-permute-done.1 = bf16[6,16,1024]{2,1,0:T(8,128)(2,1)S(1)} collective-permute-done((bf16[6,16,1024]{2,1,0:T(8,128)(2,1)S(1)}, bf16[6,16,1024]{2,1,0:T(8,128)(2,1)S(1)}, u32[]{:S(2)}, u32[]{:S(2)}) %collective-permute-start.1) | collective-permute-done | bytes 196640 | tf_op jit(solution)/shard_map/ppermute | solution.py:282
  28.1 0.9 fusion
  29.0 4.7 %collective-permute-start.2 = (bf16[24,8,1024]{2,1,0:T(8,128)(2,1)}, bf16[24,8,1024]{2,1,0:T(8,128)(2,1)S(1)}, u32[]{:S(2)}, u32[]{:S(2)}) collective-permute-start(bf16[24,8,1024]{2,1,0:T(8,128)(2,1)} %get-tuple-element.41), channel_id=1, source_target_pairs={{0,1},{1,2},{2,3},{3,4},{4,5},{5,6},{6,7},{7,8},{8,9},{9,10},{10,1... | collective-permute-start | bytes 1179656 | tf_op jit(solution)/shard_map/ppermute | solution.py:277
  33.8 4.3 %collective-permute-start.3 = (bf16[24,8,1024]{2,1,0:T(8,128)(2,1)}, bf16[24,8,1024]{2,1,0:T(8,128)(2,1)S(1)}, u32[]{:S(2)}, u32[]{:S(2)}) collective-permute-start(bf16[24,8,1024]{2,1,0:T(8,128)(2,1)} %get-tuple-element.40), channel_id=1, source_target_pairs={{0,63},{1,0},{2,1},{3,2},{4,3},{5,4},{6,5},{7,6},{8,7},{9,8},{10,9... | collective-permute-start | bytes 1179656 | tf_op jit(solution)/shard_map/ppermute | solution.py:277
  38.2 0.6 collective-permute-done.2.west_ref
  38.8 8.5 %collective-permute-done.3.east_ref = bf16[24,8,1024]{2,1,0:T(8,128)(2,1)S(1)} collective-permute-done((bf16[24,8,1024]{2,1,0:T(8,128)(2,1)}, bf16[24,8,1024]{2,1,0:T(8,128)(2,1)S(1)}, u32[]{:S(2)}, u32[]{:S(2)}) %collective-permute-start.3) | collective-permute-done | bytes 393248 | tf_op jit(solution)/shard_map/ppermute | solution.py:277
  47.3 3.5 %forward.1 = (bf16[24,32,1024]{2,1,0:T(8,128)(2,1)S(1)}, f32[8,256]{1,0:T(8,128)S(1)}, f32[32,8,1024]{2,1,0:T(8,128)S(1)}, bf16[32,8,1024]{2,1,0:T(8,128)(2,1)S(1)}) custom-call(s32[2]{0:T(128)S(1)} %pad_add_fusion.place_ref, bf16[12,16,512]{2,1,0:T(8,128)(2,1)S(1)} %copy-done.4, bf16[24,16,1024]{2,1,0:T(8,128)(2,1)S(1)} %pad_maximum_fusion.ext_ref, ...), custom_call_target="tpu_custom_call" | custom-call | flops 1000000000 | bytes 5000000 | tf_op jit(solution)/shard_map/forward/pallas_call | solution.py:225
  50.9 4.0 %collective-permute-start.4 = (bf16[32,8,1024]{2,1,0:T(8,128)(2,1)S(1)}, bf16[32,8,1024]{2,1,0:T(8,128)(2,1)S(1)}, u32[]{:S(2)}, u32[]{:S(2)}) collective-permute-start(bf16[32,8,1024]{2,1,0:T(8,128)(2,1)S(1)} %get-tuple-element.28), channel_id=1, source_target_pairs={{0,1},{1,0},{2,3},{3,2},{4,5},{5,4},{6,7},{7,6},{8,9},{9,8},{10,11... | collective-permute-start | bytes 1572872 | tf_op jit(solution)/shard_map/ppermute | solution.py:312
  55.4 1.0 collective-permute-done.4
  56.4 1.0 add_convert_fusion
  57.3 10.5 %all-to-all-start = ((bf16[32,8,1024]{2,1,0:T(8,128)(2,1)}), bf16[32,8,1024]{2,1,0:T(8,128)(2,1)S(1)}, u32[]{:S(2)}, u32[]{:S(2)}) async-start(bf16[32,8,1024]{2,1,0:T(8,128)(2,1)} %add_convert_fusion), calls=%async_computation | async-start | bytes 1048576 | tf_op jit(solution)/shard_map/all_to_all | solution.py:315
  67.9 1.4 %copy-done.6 = bf16[24,32,1024]{2,1,0:T(8,128)(2,1)S(1)} copy-done((bf16[24,32,1024]{2,1,0:T(8,128)(2,1)S(1)}, bf16[24,32,1024]{2,1,0:T(8,128)(2,1)}, u32[]{:S(2)}) %copy-start.6) | copy-done | bytes 1572888
  69.3 5.5 %backward.1 = (bf16[12,16,512]{2,1,0:T(8,128)(2,1)}, f32[12,16,512]{2,1,0:T(8,128)S(1)}, f32[12,16,512]{2,1,0:T(8,128)S(1)}, f32[12,16,1024]{2,1,0:T(8,128)S(1)}...) custom-call(s32[2]{0:T(128)S(1)} %pad_add_fusion.place_ref, bf16[12,16,512]{2,1,0:T(8,128)(2,1)S(1)} %copy-done.4, ...), custom_call_target="tpu_custom_call" | custom-call | flops 20000000000 | bytes 70000000 | tf_op jit(solution)/shard_map/backward/pallas_call | solution.py:250
  74.7 3.7 %collective-permute-start.5 = (bf16[24,8,1024]{2,1,0:T(8,128)(2,1)S(1)}, bf16[24,8,1024]{2,1,0:T(8,128)(2,1)S(1)}, u32[]{:S(2)}, u32[]{:S(2)}) collective-permute-start(bf16[24,8,1024]{2,1,0:T(8,128)(2,1)S(1)} %get-tuple-element.31), channel_id=1, source_target_pairs={{0,1},{1,2},{2,3},{3,4},{4,5},{5,6},{6,7},{7,8},{8,9},{9,10},{10,1... | collective-permute-start | bytes 1179656 | tf_op jit(solution)/shard_map/ppermute | solution.py:277
  78.5 1.9 %collective-permute-start.6 = (bf16[24,8,1024]{2,1,0:T(8,128)(2,1)S(1)}, bf16[24,8,1024]{2,1,0:T(8,128)(2,1)S(1)}, u32[]{:S(2)}, u32[]{:S(2)}) collective-permute-start(bf16[24,8,1024]{2,1,0:T(8,128)(2,1)S(1)} %get-tuple-element.32), channel_id=1, source_target_pairs={{0,63},{1,0},{2,1},{3,2},{4,3},{5,4},{6,5},{7,6},{8,7},{9,8},{10,9... | collective-permute-start | bytes 1179656 | tf_op jit(solution)/shard_map/ppermute | solution.py:277
  80.4 4.3 %collective-permute-done.5.west_ref = bf16[24,8,1024]{2,1,0:T(8,128)(2,1)S(1)} collective-permute-done((bf16[24,8,1024]{2,1,0:T(8,128)(2,1)S(1)}, bf16[24,8,1024]{2,1,0:T(8,128)(2,1)S(1)}, u32[]{:S(2)}, u32[]{:S(2)}) %collective-permute-start.5) | collective-permute-done | bytes 393248 | tf_op jit(solution)/shard_map/ppermute | solution.py:277
  84.7 7.7 %collective-permute-done.6.east_ref = bf16[24,8,1024]{2,1,0:T(8,128)(2,1)S(1)} collective-permute-done((bf16[24,8,1024]{2,1,0:T(8,128)(2,1)S(1)}, bf16[24,8,1024]{2,1,0:T(8,128)(2,1)S(1)}, u32[]{:S(2)}, u32[]{:S(2)}) %collective-permute-start.6) | collective-permute-done | bytes 393248 | tf_op jit(solution)/shard_map/ppermute | solution.py:277
  92.5 3.5 %collective-permute-start.7 = (bf16[6,16,1024]{2,1,0:T(8,128)(2,1)S(1)}, bf16[6,16,1024]{2,1,0:T(8,128)(2,1)S(1)}, u32[]{:S(2)}, u32[]{:S(2)}) collective-permute-start(bf16[6,16,1024]{2,1,0:T(8,128)(2,1)S(1)} %get-tuple-element.37), channel_id=1, source_target_pairs={{0,64},{64,128},{128,192},{192,256},{256,320},{320,384},{384,448},... | collective-permute-start | bytes 589832 | tf_op jit(solution)/shard_map/ppermute | solution.py:282
  96.0 6.6 %collective-permute-start.8 = (bf16[6,16,1024]{2,1,0:T(8,128)(2,1)S(1)}, bf16[6,16,1024]{2,1,0:T(8,128)(2,1)S(1)}, u32[]{:S(2)}, u32[]{:S(2)}) collective-permute-start(bf16[6,16,1024]{2,1,0:T(8,128)(2,1)S(1)} %get-tuple-element.33), channel_id=1, source_target_pairs={{64,0},{128,64},{192,128},{256,192},{320,256},{384,320},{448,384},... | collective-permute-start | bytes 589832 | tf_op jit(solution)/shard_map/ppermute | solution.py:282
  102.7 0.7 share.1
  103.4 6.4 %all-to-all-start.1 = ((bf16[8,8,1024]{2,1,0:T(8,128)(2,1)}), bf16[8,8,1024]{2,1,0:T(8,128)(2,1)S(1)}, u32[]{:S(2)}, u32[]{:S(2)}) async-start(bf16[8,8,1024]{2,1,0:T(8,128)(2,1)} %share.1), calls=%async_computation.1 | async-start | bytes 262144 | tf_op jit(solution)/shard_map/all_to_all | solution.py:334
  109.8 4.9 %collective-permute-done.8.below_ref = bf16[6,16,1024]{2,1,0:T(8,128)(2,1)S(1)} collective-permute-done((bf16[6,16,1024]{2,1,0:T(8,128)(2,1)S(1)}, bf16[6,16,1024]{2,1,0:T(8,128)(2,1)S(1)}, u32[]{:S(2)}, u32[]{:S(2)}) %collective-permute-start.8) | collective-permute-done | bytes 196640 | tf_op jit(solution)/shard_map/ppermute | solution.py:282
  114.7 1.0 copy-done.8
  115.7 1.0 copy-done.10
  116.7 0.8 finish.1
  117.5 4.5 %all-to-all-done.1 = bf16[8,8,1024]{2,1,0:T(8,128)(2,1)S(1)} async-done(((bf16[8,8,1024]{2,1,0:T(8,128)(2,1)}), bf16[8,8,1024]{2,1,0:T(8,128)(2,1)S(1)}, u32[]{:S(2)}, u32[]{:S(2)}) %all-to-all-start.1) | async-done | bytes 131104 | tf_op jit(solution)/shard_map/all_to_all | solution.py:334
  122.0 0.6 broadcast_multiply_fusion
  (26 shorter events, 0.9 us)
Async XLA Ops:
  0.6 54.2 %copy-start = (bf16[512,1024]{1,0:T(8,128)(2,1)S(1)}, bf16[512,1024]{1,0:T(8,128)(2,1)}, u32[]{:S(2)}) copy-start(bf16[512,1024]{1,0:T(8,128)(2,1)} %param.9) | copy-start | bytes 3145732
  0.6 1.0 copy-start.2
  1.7 0.9 copy-start.3
  2.7 15.2 %collective-permute-start = (bf16[6,16,1024]{2,1,0:T(8,128)(2,1)S(1)}, bf16[6,16,1024]{2,1,0:T(8,128)(2,1)S(1)}, u32[]{:S(2)}, u32[]{:S(2)}) collective-permute-start(bf16[6,16,1024]{2,1,0:T(8,128)(2,1)S(1)} %get-tuple-element.42), channel_id=1, source_target_pairs={{0,64},{64,128},{128,192},{192,256},{256,320},{320,384},{384,448},... | collective-permute-start | bytes 589832 | tf_op jit(solution)/shard_map/ppermute | solution.py:282
  13.3 34.0 %copy-start.1 = (bf16[12,16,1024]{2,1,0:T(8,128)(2,1)S(1)}, bf16[12,16,1024]{2,1,0:T(8,128)(2,1)}, u32[]{:S(2)}) copy-start(bf16[12,16,1024]{2,1,0:T(8,128)(2,1)} %param.8) | copy-start | bytes 1179652
  13.3 34.0 %copy-start.4 = (bf16[12,16,512]{2,1,0:T(8,128)(2,1)S(1)}, bf16[12,16,512]{2,1,0:T(8,128)(2,1)}, u32[]{:S(2)}) copy-start(bf16[12,16,512]{2,1,0:T(8,128)(2,1)} %q_ref.3) | copy-start | bytes 589828
  13.3 14.7 %collective-permute-start.1 = (bf16[6,16,1024]{2,1,0:T(8,128)(2,1)S(1)}, bf16[6,16,1024]{2,1,0:T(8,128)(2,1)S(1)}, u32[]{:S(2)}, u32[]{:S(2)}) collective-permute-start(bf16[6,16,1024]{2,1,0:T(8,128)(2,1)S(1)} %get-tuple-element.43), channel_id=1, source_target_pairs={{64,0},{128,64},{192,128},{256,192},{320,256},{384,320},{448,384},... | collective-permute-start | bytes 589832 | tf_op jit(solution)/shard_map/ppermute | solution.py:282
  29.0 9.8 %collective-permute-start.2 = (bf16[24,8,1024]{2,1,0:T(8,128)(2,1)}, bf16[24,8,1024]{2,1,0:T(8,128)(2,1)S(1)}, u32[]{:S(2)}, u32[]{:S(2)}) collective-permute-start(bf16[24,8,1024]{2,1,0:T(8,128)(2,1)} %get-tuple-element.41), channel_id=1, source_target_pairs={{0,1},{1,2},{2,3},{3,4},{4,5},{5,6},{6,7},{7,8},{8,9},{9,10},{10,1... | collective-permute-start | bytes 1179656 | tf_op jit(solution)/shard_map/ppermute | solution.py:277
  33.8 13.5 %collective-permute-start.3 = (bf16[24,8,1024]{2,1,0:T(8,128)(2,1)}, bf16[24,8,1024]{2,1,0:T(8,128)(2,1)S(1)}, u32[]{:S(2)}, u32[]{:S(2)}) collective-permute-start(bf16[24,8,1024]{2,1,0:T(8,128)(2,1)} %get-tuple-element.40), channel_id=1, source_target_pairs={{0,63},{1,0},{2,1},{3,2},{4,3},{5,4},{6,5},{7,6},{8,7},{9,8},{10,9... | collective-permute-start | bytes 1179656 | tf_op jit(solution)/shard_map/ppermute | solution.py:277
  50.9 5.5 %copy-start.5 = (bf16[24,32,1024]{2,1,0:T(8,128)(2,1)}, bf16[24,32,1024]{2,1,0:T(8,128)(2,1)S(1)}, u32[]{:S(2)}) copy-start(bf16[24,32,1024]{2,1,0:T(8,128)(2,1)S(1)} %get-tuple-element.22.kv_ref) | copy-start | bytes 4718596
  50.9 5.5 %collective-permute-start.4 = (bf16[32,8,1024]{2,1,0:T(8,128)(2,1)S(1)}, bf16[32,8,1024]{2,1,0:T(8,128)(2,1)S(1)}, u32[]{:S(2)}, u32[]{:S(2)}) collective-permute-start(bf16[32,8,1024]{2,1,0:T(8,128)(2,1)S(1)} %get-tuple-element.28), channel_id=1, source_target_pairs={{0,1},{1,0},{2,3},{3,2},{4,5},{5,4},{6,7},{7,6},{8,9},{9,8},{10,11... | collective-permute-start | bytes 1572872 | tf_op jit(solution)/shard_map/ppermute | solution.py:312
  57.3 45.3 %all-to-all-start = ((bf16[32,8,1024]{2,1,0:T(8,128)(2,1)}), bf16[32,8,1024]{2,1,0:T(8,128)(2,1)S(1)}, u32[]{:S(2)}, u32[]{:S(2)}) async-start(bf16[32,8,1024]{2,1,0:T(8,128)(2,1)} %add_convert_fusion), calls=%async_computation | async-start | bytes 1048576 | tf_op jit(solution)/shard_map/all_to_all | solution.py:315
  67.8 1.4 %copy-start.6 = (bf16[24,32,1024]{2,1,0:T(8,128)(2,1)S(1)}, bf16[24,32,1024]{2,1,0:T(8,128)(2,1)}, u32[]{:S(2)}) copy-start(bf16[24,32,1024]{2,1,0:T(8,128)(2,1)} %copy-done.5) | copy-start | bytes 4718596
  74.7 21.3 %copy-start.7 = (f32[12,16,512]{2,1,0:T(8,128)}, f32[12,16,512]{2,1,0:T(8,128)S(1)}, u32[]{:S(2)}) copy-start(f32[12,16,512]{2,1,0:T(8,128)S(1)} %get-tuple-element.35.mid_k_ref) | copy-start | bytes 1179652
  74.7 21.3 %copy-start.9 = (f32[12,16,512]{2,1,0:T(8,128)}, f32[12,16,512]{2,1,0:T(8,128)S(1)}, u32[]{:S(2)}) copy-start(f32[12,16,512]{2,1,0:T(8,128)S(1)} %get-tuple-element.36.mid_v_ref) | copy-start | bytes 1179652
  74.7 10.0 %collective-permute-start.5 = (bf16[24,8,1024]{2,1,0:T(8,128)(2,1)S(1)}, bf16[24,8,1024]{2,1,0:T(8,128)(2,1)S(1)}, u32[]{:S(2)}, u32[]{:S(2)}) collective-permute-start(bf16[24,8,1024]{2,1,0:T(8,128)(2,1)S(1)} %get-tuple-element.31), channel_id=1, source_target_pairs={{0,1},{1,2},{2,3},{3,4},{4,5},{5,6},{6,7},{7,8},{8,9},{9,10},{10,1... | collective-permute-start | bytes 1179656 | tf_op jit(solution)/shard_map/ppermute | solution.py:277
  78.5 14.0 %collective-permute-start.6 = (bf16[24,8,1024]{2,1,0:T(8,128)(2,1)S(1)}, bf16[24,8,1024]{2,1,0:T(8,128)(2,1)S(1)}, u32[]{:S(2)}, u32[]{:S(2)}) collective-permute-start(bf16[24,8,1024]{2,1,0:T(8,128)(2,1)S(1)} %get-tuple-element.32), channel_id=1, source_target_pairs={{0,63},{1,0},{2,1},{3,2},{4,3},{5,4},{6,5},{7,6},{8,7},{9,8},{10,9... | collective-permute-start | bytes 1179656 | tf_op jit(solution)/shard_map/ppermute | solution.py:277
  92.5 17.3 %collective-permute-start.7 = (bf16[6,16,1024]{2,1,0:T(8,128)(2,1)S(1)}, bf16[6,16,1024]{2,1,0:T(8,128)(2,1)S(1)}, u32[]{:S(2)}, u32[]{:S(2)}) collective-permute-start(bf16[6,16,1024]{2,1,0:T(8,128)(2,1)S(1)} %get-tuple-element.37), channel_id=1, source_target_pairs={{0,64},{64,128},{128,192},{192,256},{256,320},{320,384},{384,448},... | collective-permute-start | bytes 589832 | tf_op jit(solution)/shard_map/ppermute | solution.py:282
  96.0 18.7 %collective-permute-start.8 = (bf16[6,16,1024]{2,1,0:T(8,128)(2,1)S(1)}, bf16[6,16,1024]{2,1,0:T(8,128)(2,1)S(1)}, u32[]{:S(2)}, u32[]{:S(2)}) collective-permute-start(bf16[6,16,1024]{2,1,0:T(8,128)(2,1)S(1)} %get-tuple-element.33), channel_id=1, source_target_pairs={{64,0},{128,64},{192,128},{256,192},{320,256},{384,320},{448,384},... | collective-permute-start | bytes 589832 | tf_op jit(solution)/shard_map/ppermute | solution.py:282
  103.4 18.6 %all-to-all-start.1 = ((bf16[8,8,1024]{2,1,0:T(8,128)(2,1)}), bf16[8,8,1024]{2,1,0:T(8,128)(2,1)S(1)}, u32[]{:S(2)}, u32[]{:S(2)}) async-start(bf16[8,8,1024]{2,1,0:T(8,128)(2,1)} %share.1), calls=%async_computation.1 | async-start | bytes 262144 | tf_op jit(solution)/shard_map/all_to_all | solution.py:334
  114.7 1.0 copy-start.8
  115.7 1.0 copy-start.10

commit v3 on v2

--- a/solution.py
+++ b/solution.py
@@ -107,7 +107,7 @@
 
 def backward_kernel(
     lat_total, place_ref, q_ref, g_ref, kv_ref, norm_ref,
-    dq_ref, mid_k_ref, mid_v_ref, rim_ref, left_ref, right_ref, kt, acc, dq_t,
+    dq_ref, mid_ref, rim_ref, left_ref, right_ref, kt, acc, dq_t,
 ):
     rows, cols, inner = q_ref.shape
     ext_rows = rows + 2 * RADIUS
@@ -156,10 +156,9 @@
 
     left_ref[...] = acc[:, cols : cols + SIDE, :].astype(jnp.bfloat16)
     right_ref[...] = acc[:, cols + SIDE : wide, :].astype(jnp.bfloat16)
-    rim_ref[0:RADIUS] = acc[0:RADIUS, 0:cols, :]
-    rim_ref[RADIUS:] = acc[RADIUS + rows :, 0:cols, :]
-    mid_k_ref[...] = acc[RADIUS : RADIUS + rows, 0:cols, 0:inner]
-    mid_v_ref[...] = acc[RADIUS : RADIUS + rows, 0:cols, inner:]
+    rim_ref[0:RADIUS] = acc[0:RADIUS, 0:cols, :].astype(jnp.bfloat16)
+    rim_ref[RADIUS:] = acc[RADIUS + rows :, 0:cols, :].astype(jnp.bfloat16)
+    mid_ref[...] = acc[RADIUS : RADIUS + rows, 0:cols, :].astype(jnp.bfloat16)
     dq_ref[...] = dq_t[...].T.astype(jnp.bfloat16).reshape(rows, cols, inner)
 
 
@@ -168,10 +167,24 @@
     copies_ref[...] = jnp.broadcast_to(total[None], copies_ref.shape)
 
 
-def pack_kernel(keys_ref, values_ref, both_ref):
+def pack_kernel(keys_ref, values_ref, both_ref, sems):
     inner = keys_ref.shape[2]
-    both_ref[:, :, 0:inner] = keys_ref[...]
-    both_ref[:, :, inner:] = values_ref[...]
+    copies = [
+        pltpu.make_async_copy(keys_ref, both_ref.at[:, :, pl.ds(0, inner)], sems.at[0]),
+        pltpu.make_async_copy(values_ref, both_ref.at[:, :, pl.ds(inner, inner)], sems.at[1]),
+    ]
+    for copy in copies:
+        copy.start()
+    for copy in copies:
+        copy.wait()
+
+
+def fold_kernel(keep_ref, got_ref, half_ref):
+    half_ref[...] = (keep_ref[...] + got_ref[...].astype(jnp.float32)).astype(jnp.bfloat16)
+
+
+def mean_kernel(parts, terms_ref, out_ref):
+    out_ref[...] = jnp.sum(terms_ref[...].astype(jnp.float32), axis=0) / parts
 
 
 def wide(block):
@@ -187,30 +200,28 @@
         side = jnp.concatenate(
             [wide(west_ref[there : there + deep]), wide(east_ref[there : there + deep])], axis=1
         )
-        out[...] = (rim_ref[at : at + deep] + side).astype(jnp.bfloat16)
+        out[...] = (wide(rim_ref[at : at + deep]) + side).astype(jnp.bfloat16)
 
 
 def finish_kernel(
-    mid_k_ref, mid_v_ref, west_ref, east_ref, above_ref, below_ref, keys_ref, values_ref
+    mid_ref, west_ref, east_ref, above_ref, below_ref, keys_ref, values_ref
 ):
-    inner = mid_k_ref.shape[2]
+    inner = keys_ref.shape[2]
     deep = above_ref.shape[0]
-    for out, mid, chans in (
-        (keys_ref, mid_k_ref, slice(0, inner)),
-        (values_ref, mid_v_ref, slice(inner, 2 * inner)),
-    ):
+    for out, chans in ((keys_ref, slice(0, inner)), (values_ref, slice(inner, 2 * inner))):
         for at, pole in ((0, above_ref), (deep, below_ref)):
             there = slice(deep + at, 2 * deep + at)
             side = jnp.concatenate(
                 [wide(west_ref[there, :, chans]), wide(east_ref[there, :, chans])], axis=1
             )
-            total = mid[at : at + deep] + side + wide(pole[:, :, chans])
+            total = wide(mid_ref[at : at + deep, :, chans]) + side + wide(pole[:, :, chans])
             out[at : at + deep] = total.astype(jnp.bfloat16)
 
 
 VMEM = pl.BlockSpec(memory_space=pltpu.VMEM)
 SMEM = pl.BlockSpec(memory_space=pltpu.SMEM)
 PARAMS = pltpu.CompilerParams(vmem_limit_bytes=20 << 20)
+FOLD, RIM, FINISH = 6_000_000_000, 6_000_000_000, 6_000_000_000
 SMALL = pltpu.CompilerParams(vmem_limit_bytes=8 << 20)
 
 
@@ -251,14 +262,13 @@
         functools.partial(backward_kernel, lat_total),
         out_shape=(
             shape((rows, cols, inner)),
-            shape((rows, cols, inner), jnp.float32),
-            shape((rows, cols, inner), jnp.float32),
-            shape((2 * RADIUS, cols, 2 * inner), jnp.float32),
+            shape((rows, cols, 2 * inner)),
+            shape((2 * RADIUS, cols, 2 * inner)),
             shape((ext_rows, SIDE, 2 * inner)),
             shape((ext_rows, SIDE, 2 * inner)),
         ),
         in_specs=[SMEM] + [VMEM] * 4,
-        out_specs=(VMEM,) * 6,
+        out_specs=(VMEM,) * 5,
         scratch_shapes=[
             pltpu.VMEM((inner, ext_rows * wide), jnp.bfloat16),
             pltpu.VMEM((ext_rows, wide, 2 * inner), jnp.float32),
@@ -282,6 +292,10 @@
     return lax.ppermute(
         block, axis, [(i, i + by) for i in range(size) if 0 <= i + by < size]
     )
+
+
+def cost(flops):
+    return pl.CostEstimate(flops=flops, bytes_accessed=4_000_000, transcendentals=0)
 
 
 def shards(queries, keys, values, upstream, out_weight):
@@ -299,47 +313,71 @@
         .reshape(rows, cols, inner)
     )
     both = pl.pallas_call(
-        pack_kernel, out_shape=shape((rows, cols, 2 * inner)), name="pack", compiler_params=SMALL
+        pack_kernel,
+        out_shape=shape((rows, cols, 2 * inner)),
+        in_specs=[pl.BlockSpec(memory_space=pl.ANY)] * 2,
+        out_specs=VMEM,
+        scratch_shapes=[pltpu.SemaphoreType.DMA((2,))],
+        compiler_params=SMALL,
+        name="pack",
     )(keys, values)
     above = line(both[rows - RADIUS :], "lat", 1)
     below = line(both[:RADIUS], "lat", -1)
     extended = jnp.concatenate([above, both, below], axis=0)
     west = ring(extended[:, cols - SIDE :], "lon", 1)
     east = ring(extended[:, :SIDE], "lon", -1)
+    place, grads = lax.optimization_barrier((place, grads))
     kv, norm, keep, give = forward(
         place, queries, extended, west, east, up_flat, lat_total, out_rows
     )
     got = lax.ppermute(give, "lon", [(i, i ^ 1) for i in range(lon)])
-    half = (keep + got.astype(jnp.float32)).astype(jnp.bfloat16)
+    grad_query, mid, rim, left, right = backward(
+        place, queries, grads, kv, norm, lat_total
+    )
+    keep, left, right = lax.optimization_barrier((keep, left, right))
+    from_east = ring(left, "lon", -1)
+    from_west = ring(right, "lon", 1)
+    half = pl.pallas_call(
+        fold_kernel,
+        out_shape=shape(keep.shape),
+        compiler_params=SMALL,
+        cost_estimate=cost(FOLD),
+        name="fold",
+    )(keep, got)
     same_core = [[2 * i + c for i in range(lon // 2)] for c in range(2)]
     terms = lax.all_to_all(half, "lon", 0, 0, axis_index_groups=same_core, tiled=True)
-
-    grad_query, mid_k, mid_v, rim, left, right = backward(
-        place, queries, grads, kv, norm, lat_total
-    )
-    from_east = ring(left, "lon", -1)
-    from_west = ring(right, "lon", 1)
-    rim, _ = lax.optimization_barrier((rim, half))
+    from_west, from_east, _ = lax.optimization_barrier((from_west, from_east, half))
     top, bottom = pl.pallas_call(
         rim_kernel,
         out_shape=(shape((RADIUS, cols, 2 * inner)),) * 2,
-        name="rim", compiler_params=SMALL,
+        compiler_params=SMALL,
+        cost_estimate=cost(RIM),
+        name="rim",
     )(rim, from_west, from_east)
     from_below = line(top, "lat", -1)
     from_above = line(bottom, "lat", 1)
     terms, _ = lax.optimization_barrier((terms, top))
     copies = pl.pallas_call(
-        share_kernel, out_shape=shape((lat, out_rows, model)), name="share", compiler_params=SMALL
+        share_kernel,
+        out_shape=shape((lat, out_rows, model)),
+        compiler_params=SMALL,
+        name="share",
     )(terms)
     every = lax.all_to_all(copies, "lat", 0, 0, tiled=True)
-    grad_weight = jnp.sum(every.astype(jnp.float32), axis=0) / lat_total
-    mid_k, mid_v, _ = lax.optimization_barrier((mid_k, mid_v, copies))
+    from_above, from_below, _ = lax.optimization_barrier((from_above, from_below, copies))
     grad_key, grad_value = pl.pallas_call(
         finish_kernel,
         out_shape=(shape((rows, cols, inner)),) * 2,
-        name="finish", compiler_params=SMALL,
-        cost_estimate=pl.CostEstimate(flops=50_000_000_000, bytes_accessed=4_000_000, transcendentals=0),
-    )(mid_k, mid_v, from_west, from_east, from_above, from_below)
+        compiler_params=SMALL,
+        cost_estimate=cost(FINISH),
+        name="finish",
+    )(mid, from_west, from_east, from_above, from_below)
+    grad_weight = pl.pallas_call(
+        functools.partial(mean_kernel, lat_total),
+        out_shape=shape((out_rows, model), jnp.float32),
+        compiler_params=SMALL,
+        name="mean",
+    )(every)
     return (grad_query, grad_key, grad_value, grad_weight)
 
 

time: 123 us -> 130 us (1.057)
  the two profiles are of different devices: /device:TPU:5 before, /device:TPU:6 now
where the time goes in v3:
time: 130 us; the launch traced here: 129 us
  starting transfers between devices  67 us (52%)
  waiting for transfers between devices  42.8 us (33%)
  Pallas kernels  12.3 us (9%)
  local copies, waits for them, and re-layouts  5.44 us (4%)
    ppermute x4, starting transfers between devices, line(): lax.ppermute(block, axis, [(i, i + by) for i in range(size) if 0 <= i + b...  24.5 us
    ppermute x4, starting transfers between devices, ring(): lax.ppermute(block, axis, [(i, (i + by) % size) for i in range(size)])  17.6 us
    all_to_all x1, starting transfers between devices, shards(): every = lax.all_to_all(copies, 'lat', 0, 0, tiled=True)  17.4 us
    all_to_all x1, waiting for transfers between devices, shards(): lax.all_to_all(half, 'lon', 0, 0, axis_index_groups=same_core, tiled=True)  14.4 us
    ppermute x4, waiting for transfers between devices, ring(): lax.ppermute(block, axis, [(i, (i + by) % size) for i in range(size)])  10.8 us
    ppermute x4, waiting for transfers between devices, line(): lax.ppermute(block, axis, [(i, i + by) for i in range(size) if 0 <= i + b...  10.1 us
    all_to_all x1, waiting for transfers between devices, shards(): every = lax.all_to_all(copies, 'lat', 0, 0, tiled=True)  7.52 us
    all_to_all x1, starting transfers between devices, shards(): lax.all_to_all(half, 'lon', 0, 0, axis_index_groups=same_core, tiled=True)  5.64 us
  transfers between devices with their start and end apart: 11, of which 6 were waited for; matrix products, arithmetic and copies ran while one was open for 0% of the time, Pallas kernels for 6%

profile of v3, /device:TPU:6, one launch (start us, length us, event | category | flops | bytes accessed | tf_op | source)
XLA Modules:
  0.0 129.1 jit_solution(1044263146818411802)
XLA Ops:
  0.7 1.0 copy-done.2
  1.7 0.9 copy-done.3
  2.7 10.9 %collective-permute-start = (bf16[6,16,1024]{2,1,0:T(8,128)(2,1)S(1)}, bf16[6,16,1024]{2,1,0:T(8,128)(2,1)S(1)}, u32[]{:S(2)}, u32[]{:S(2)}) collective-permute-start(bf16[6,16,1024]{2,1,0:T(8,128)(2,1)S(1)} %get-tuple-element.52), channel_id=1, source_target_pairs={{0,64},{64,128},{128,192},{192,256},{256,320},{320,384},{384,448},... | collective-permute-start | bytes 589832 | tf_op jit(solution)/shard_map/ppermute | solution.py:292
  13.6 2.3 %collective-permute-start.1 = (bf16[6,16,1024]{2,1,0:T(8,128)(2,1)S(1)}, bf16[6,16,1024]{2,1,0:T(8,128)(2,1)S(1)}, u32[]{:S(2)}, u32[]{:S(2)}) collective-permute-start(bf16[6,16,1024]{2,1,0:T(8,128)(2,1)S(1)} %get-tuple-element.53), channel_id=1, source_target_pairs={{64,0},{128,64},{192,128},{256,192},{320,256},{384,320},{448,384},... | collective-permute-start | bytes 589832 | tf_op jit(solution)/shard_map/ppermute | solution.py:292
  16.0 2.9 %collective-permute-done = bf16[6,16,1024]{2,1,0:T(8,128)(2,1)S(1)} collective-permute-done((bf16[6,16,1024]{2,1,0:T(8,128)(2,1)S(1)}, bf16[6,16,1024]{2,1,0:T(8,128)(2,1)S(1)}, u32[]{:S(2)}, u32[]{:S(2)}) %collective-permute-start) | collective-permute-done | bytes 196640 | tf_op jit(solution)/shard_map/ppermute | solution.py:292
  18.9 7.1 %collective-permute-done.1 = bf16[6,16,1024]{2,1,0:T(8,128)(2,1)S(1)} collective-permute-done((bf16[6,16,1024]{2,1,0:T(8,128)(2,1)S(1)}, bf16[6,16,1024]{2,1,0:T(8,128)(2,1)S(1)}, u32[]{:S(2)}, u32[]{:S(2)}) %collective-permute-start.1) | collective-permute-done | bytes 196640 | tf_op jit(solution)/shard_map/ppermute | solution.py:292
  26.0 0.1 pad_maximum_fusion.ext_ref
  26.1 0.9 fusion
  27.1 6.2 %collective-permute-start.3 = (bf16[24,8,1024]{2,1,0:T(8,128)(2,1)}, bf16[24,8,1024]{2,1,0:T(8,128)(2,1)S(1)}, u32[]{:S(2)}, u32[]{:S(2)}) collective-permute-start(bf16[24,8,1024]{2,1,0:T(8,128)(2,1)} %get-tuple-element.50), channel_id=1, source_target_pairs={{0,63},{1,0},{2,1},{3,2},{4,3},{5,4},{6,5},{7,6},{8,7},{9,8},{10,9... | collective-permute-start | bytes 1179656 | tf_op jit(solution)/shard_map/ppermute | solution.py:287
  33.3 1.9 %collective-permute-start.2 = (bf16[24,8,1024]{2,1,0:T(8,128)(2,1)}, bf16[24,8,1024]{2,1,0:T(8,128)(2,1)S(1)}, u32[]{:S(2)}, u32[]{:S(2)}) collective-permute-start(bf16[24,8,1024]{2,1,0:T(8,128)(2,1)} %get-tuple-element.51), channel_id=1, source_target_pairs={{0,1},{1,2},{2,3},{3,4},{4,5},{5,6},{6,7},{7,8},{8,9},{9,10},{10,1... | collective-permute-start | bytes 1179656 | tf_op jit(solution)/shard_map/ppermute | solution.py:287
  35.4 0.5 convolution_convert_fusion
  35.9 3.1 %collective-permute-done.3.east_ref = bf16[24,8,1024]{2,1,0:T(8,128)(2,1)S(1)} collective-permute-done((bf16[24,8,1024]{2,1,0:T(8,128)(2,1)}, bf16[24,8,1024]{2,1,0:T(8,128)(2,1)S(1)}, u32[]{:S(2)}, u32[]{:S(2)}) %collective-permute-start.3) | collective-permute-done | bytes 393248 | tf_op jit(solution)/shard_map/ppermute | solution.py:287
  38.9 7.7 %collective-permute-done.2.west_ref = bf16[24,8,1024]{2,1,0:T(8,128)(2,1)S(1)} collective-permute-done((bf16[24,8,1024]{2,1,0:T(8,128)(2,1)}, bf16[24,8,1024]{2,1,0:T(8,128)(2,1)S(1)}, u32[]{:S(2)}, u32[]{:S(2)}) %collective-permute-start.2) | collective-permute-done | bytes 393248 | tf_op jit(solution)/shard_map/ppermute | solution.py:287
  46.7 3.5 %forward.1 = (bf16[24,32,1024]{2,1,0:T(8,128)(2,1)S(1)}, f32[8,256]{1,0:T(8,128)S(1)}, f32[32,8,1024]{2,1,0:T(8,128)S(1)}, bf16[32,8,1024]{2,1,0:T(8,128)(2,1)S(1)}) custom-call(s32[2]{0:T(128)S(1)} %pad_add_fusion.place_ref, bf16[12,16,512]{2,1,0:T(8,128)(2,1)S(1)} %copy-done.4, bf16[24,16,1024]{2,1,0:T(8,128)(2,1)S(1)} %pad_maximum_fusion.ext_ref, ...), custom_call_target="tpu_custom_call" | custom-call | flops 1000000000 | bytes 5000000 | tf_op jit(solution)/shard_map/forward/pallas_call | solution.py:236
  50.2 1.9 %collective-permute-start.6 = (bf16[32,8,1024]{2,1,0:T(8,128)(2,1)S(1)}, bf16[32,8,1024]{2,1,0:T(8,128)(2,1)S(1)}, u32[]{:S(2)}, u32[]{:S(2)}) collective-permute-start(bf16[32,8,1024]{2,1,0:T(8,128)(2,1)S(1)} %get-tuple-element.39), channel_id=1, source_target_pairs={{0,1},{1,0},{2,3},{3,2},{4,5},{5,4},{6,7},{7,6},{8,9},{9,8},{10,11... | collective-permute-start | bytes 1572872 | tf_op jit(solution)/shard_map/ppermute | solution.py:333
  52.1 5.5 %backward.1 = (bf16[12,16,512]{2,1,0:T(8,128)(2,1)}, bf16[12,16,1024]{2,1,0:T(8,128)(2,1)S(1)}, bf16[12,16,1024]{2,1,0:T(8,128)(2,1)S(1)}, bf16[24,8,1024]{2,1,0:T(8,128)(2,1)S(1)}, bf16[24,8,1024]{2,1,0:T(8,128)(2,1)S(1)}) custom-call(s32[2]{0:T(128)S(1)} %pad_add_fusion.place_ref, bf16[12,16,512]{2,1,0:T(8,128)(2,1)S(1)} %copy-done.4, ...), custom_call_target="tpu_custom_call" | custom-call | flops 20000000000 | bytes 70000000 | tf_op jit(solution)/shard_map/backward/pallas_call | solution.py:261
  57.7 0.8 copy-done.5
  58.4 0.8 copy-done.7
  59.2 2.4 %collective-permute-start.4 = (bf16[24,8,1024]{2,1,0:T(8,128)(2,1)S(1)}, bf16[24,8,1024]{2,1,0:T(8,128)(2,1)S(1)}, u32[]{:S(2)}, u32[]{:S(2)}) collective-permute-start(bf16[24,8,1024]{2,1,0:T(8,128)(2,1)S(1)} %get-tuple-element.36), channel_id=1, source_target_pairs={{0,1},{1,2},{2,3},{3,4},{4,5},{5,6},{6,7},{7,8},{8,9},{9,10},{10,1... | collective-permute-start | bytes 1179656 | tf_op jit(solution)/shard_map/ppermute | solution.py:287
  61.6 7.1 %collective-permute-start.5 = (bf16[24,8,1024]{2,1,0:T(8,128)(2,1)S(1)}, bf16[24,8,1024]{2,1,0:T(8,128)(2,1)S(1)}, u32[]{:S(2)}, u32[]{:S(2)}) collective-permute-start(bf16[24,8,1024]{2,1,0:T(8,128)(2,1)S(1)} %get-tuple-element.37), channel_id=1, source_target_pairs={{0,63},{1,0},{2,1},{3,2},{4,3},{5,4},{6,5},{7,6},{8,7},{9,8},{10,9... | collective-permute-start | bytes 1179656 | tf_op jit(solution)/shard_map/ppermute | solution.py:287
  68.7 0.9 fold.1
  69.6 5.6 %all-to-all-start = ((bf16[32,8,1024]{2,1,0:T(8,128)(2,1)}), bf16[32,8,1024]{2,1,0:T(8,128)(2,1)S(1)}, u32[]{:S(2)}, u32[]{:S(2)}) async-start(bf16[32,8,1024]{2,1,0:T(8,128)(2,1)} %fold.1), calls=%async_computation | async-start | bytes 1048576 | tf_op jit(solution)/shard_map/all_to_all | solution.py:348
  75.2 1.0 copy-done.8
  76.2 0.1 rim.1
  76.3 4.3 %collective-permute-start.7 = (bf16[6,16,1024]{2,1,0:T(8,128)(2,1)S(1)}, bf16[6,16,1024]{2,1,0:T(8,128)(2,1)S(1)}, u32[]{:S(2)}, u32[]{:S(2)}) collective-permute-start(bf16[6,16,1024]{2,1,0:T(8,128)(2,1)S(1)} %get-tuple-element.43), channel_id=1, source_target_pairs={{0,64},{64,128},{128,192},{192,256},{256,320},{320,384},{384,448},... | collective-permute-start | bytes 589832 | tf_op jit(solution)/shard_map/ppermute | solution.py:292
  80.7 6.9 %collective-permute-start.8 = (bf16[6,16,1024]{2,1,0:T(8,128)(2,1)S(1)}, bf16[6,16,1024]{2,1,0:T(8,128)(2,1)S(1)}, u32[]{:S(2)}, u32[]{:S(2)}) collective-permute-start(bf16[6,16,1024]{2,1,0:T(8,128)(2,1)S(1)} %get-tuple-element.44), channel_id=1, source_target_pairs={{64,0},{128,64},{192,128},{256,192},{320,256},{384,320},{448,384},... | collective-permute-start | bytes 589832 | tf_op jit(solution)/shard_map/ppermute | solution.py:292
  87.6 14.4 %all-to-all-done.parts_ref = bf16[32,8,1024]{2,1,0:T(8,128)(2,1)S(1)} async-done(((bf16[32,8,1024]{2,1,0:T(8,128)(2,1)}), bf16[32,8,1024]{2,1,0:T(8,128)(2,1)S(1)}, u32[]{:S(2)}, u32[]{:S(2)}) %all-to-all-start) | async-done | bytes 524320 | tf_op jit(solution)/shard_map/all_to_all | solution.py:348
  101.9 0.7 share.1
  102.7 17.4 %all-to-all-start.1 = ((bf16[8,8,1024]{2,1,0:T(8,128)(2,1)}), bf16[8,8,1024]{2,1,0:T(8,128)(2,1)S(1)}, u32[]{:S(2)}, u32[]{:S(2)}) async-start(bf16[8,8,1024]{2,1,0:T(8,128)(2,1)} %share.1), calls=%async_computation.1 | async-start | bytes 262144 | tf_op jit(solution)/shard_map/all_to_all | solution.py:366
  120.1 0.8 finish.1
  120.9 7.5 %all-to-all-done.1.terms_ref = bf16[8,8,1024]{2,1,0:T(8,128)(2,1)S(1)} async-done(((bf16[8,8,1024]{2,1,0:T(8,128)(2,1)}), bf16[8,8,1024]{2,1,0:T(8,128)(2,1)S(1)}, u32[]{:S(2)}, u32[]{:S(2)}) %all-to-all-start.1) | async-done | bytes 131104 | tf_op jit(solution)/shard_map/all_to_all | solution.py:366
  128.4 0.6 mean.1
  (21 shorter events, 0.2 us)
Async XLA Ops:
  0.6 34.7 %copy-start = (bf16[512,1024]{1,0:T(8,128)(2,1)S(1)}, bf16[512,1024]{1,0:T(8,128)(2,1)}, u32[]{:S(2)}) copy-start(bf16[512,1024]{1,0:T(8,128)(2,1)} %param.9) | copy-start | bytes 3145732
  0.6 1.0 copy-start.2
  1.7 0.9 copy-start.3
  2.7 16.2 %collective-permute-start = (bf16[6,16,1024]{2,1,0:T(8,128)(2,1)S(1)}, bf16[6,16,1024]{2,1,0:T(8,128)(2,1)S(1)}, u32[]{:S(2)}, u32[]{:S(2)}) collective-permute-start(bf16[6,16,1024]{2,1,0:T(8,128)(2,1)S(1)} %get-tuple-element.52), channel_id=1, source_target_pairs={{0,64},{64,128},{128,192},{192,256},{256,320},{320,384},{384,448},... | collective-permute-start | bytes 589832 | tf_op jit(solution)/shard_map/ppermute | solution.py:292
  13.6 21.7 %copy-start.1 = (bf16[12,16,1024]{2,1,0:T(8,128)(2,1)S(1)}, bf16[12,16,1024]{2,1,0:T(8,128)(2,1)}, u32[]{:S(2)}) copy-start(bf16[12,16,1024]{2,1,0:T(8,128)(2,1)} %param.8) | copy-start | bytes 1179652
  13.6 12.4 %collective-permute-start.1 = (bf16[6,16,1024]{2,1,0:T(8,128)(2,1)S(1)}, bf16[6,16,1024]{2,1,0:T(8,128)(2,1)S(1)}, u32[]{:S(2)}, u32[]{:S(2)}) collective-permute-start(bf16[6,16,1024]{2,1,0:T(8,128)(2,1)S(1)} %get-tuple-element.53), channel_id=1, source_target_pairs={{64,0},{128,64},{192,128},{256,192},{320,256},{384,320},{448,384},... | collective-permute-start | bytes 589832 | tf_op jit(solution)/shard_map/ppermute | solution.py:292
  26.1 20.5 %copy-start.4 = (bf16[12,16,512]{2,1,0:T(8,128)(2,1)S(1)}, bf16[12,16,512]{2,1,0:T(8,128)(2,1)}, u32[]{:S(2)}) copy-start(bf16[12,16,512]{2,1,0:T(8,128)(2,1)} %q_ref.3) | copy-start | bytes 589828
  27.1 11.8 %collective-permute-start.3 = (bf16[24,8,1024]{2,1,0:T(8,128)(2,1)}, bf16[24,8,1024]{2,1,0:T(8,128)(2,1)S(1)}, u32[]{:S(2)}, u32[]{:S(2)}) collective-permute-start(bf16[24,8,1024]{2,1,0:T(8,128)(2,1)} %get-tuple-element.50), channel_id=1, source_target_pairs={{0,63},{1,0},{2,1},{3,2},{4,3},{5,4},{6,5},{7,6},{8,7},{9,8},{10,9... | collective-permute-start | bytes 1179656 | tf_op jit(solution)/shard_map/ppermute | solution.py:287
  33.3 13.3 %collective-permute-start.2 = (bf16[24,8,1024]{2,1,0:T(8,128)(2,1)}, bf16[24,8,1024]{2,1,0:T(8,128)(2,1)S(1)}, u32[]{:S(2)}, u32[]{:S(2)}) collective-permute-start(bf16[24,8,1024]{2,1,0:T(8,128)(2,1)} %get-tuple-element.51), channel_id=1, source_target_pairs={{0,1},{1,2},{2,3},{3,4},{4,5},{5,6},{6,7},{7,8},{8,9},{9,10},{10,1... | collective-permute-start | bytes 1179656 | tf_op jit(solution)/shard_map/ppermute | solution.py:287
  50.2 18.4 %collective-permute-start.6 = (bf16[32,8,1024]{2,1,0:T(8,128)(2,1)S(1)}, bf16[32,8,1024]{2,1,0:T(8,128)(2,1)S(1)}, u32[]{:S(2)}, u32[]{:S(2)}) collective-permute-start(bf16[32,8,1024]{2,1,0:T(8,128)(2,1)S(1)} %get-tuple-element.39), channel_id=1, source_target_pairs={{0,1},{1,0},{2,3},{3,2},{4,5},{5,4},{6,7},{7,6},{8,9},{9,8},{10,11... | collective-permute-start | bytes 1572872 | tf_op jit(solution)/shard_map/ppermute | solution.py:333
  57.6 0.8 copy-start.5
  58.4 0.8 copy-start.7
  59.2 16.0 %collective-permute-start.4 = (bf16[24,8,1024]{2,1,0:T(8,128)(2,1)S(1)}, bf16[24,8,1024]{2,1,0:T(8,128)(2,1)S(1)}, u32[]{:S(2)}, u32[]{:S(2)}) collective-permute-start(bf16[24,8,1024]{2,1,0:T(8,128)(2,1)S(1)} %get-tuple-element.36), channel_id=1, source_target_pairs={{0,1},{1,2},{2,3},{3,4},{4,5},{5,6},{6,7},{7,8},{8,9},{9,10},{10,1... | collective-permute-start | bytes 1179656 | tf_op jit(solution)/shard_map/ppermute | solution.py:287
  61.6 13.6 %collective-permute-start.5 = (bf16[24,8,1024]{2,1,0:T(8,128)(2,1)S(1)}, bf16[24,8,1024]{2,1,0:T(8,128)(2,1)S(1)}, u32[]{:S(2)}, u32[]{:S(2)}) collective-permute-start(bf16[24,8,1024]{2,1,0:T(8,128)(2,1)S(1)} %get-tuple-element.37), channel_id=1, source_target_pairs={{0,63},{1,0},{2,1},{3,2},{4,3},{5,4},{6,5},{7,6},{8,7},{9,8},{10,9... | collective-permute-start | bytes 1179656 | tf_op jit(solution)/shard_map/ppermute | solution.py:287
  69.6 32.4 %all-to-all-start = ((bf16[32,8,1024]{2,1,0:T(8,128)(2,1)}), bf16[32,8,1024]{2,1,0:T(8,128)(2,1)S(1)}, u32[]{:S(2)}, u32[]{:S(2)}) async-start(bf16[32,8,1024]{2,1,0:T(8,128)(2,1)} %fold.1), calls=%async_computation | async-start | bytes 1048576 | tf_op jit(solution)/shard_map/all_to_all | solution.py:348
  75.2 1.0 copy-start.8
  76.2 43.8 %copy-start.6 = (bf16[12,16,1024]{2,1,0:T(8,128)(2,1)S(1)}, bf16[12,16,1024]{2,1,0:T(8,128)(2,1)}, u32[]{:S(2)}) copy-start(bf16[12,16,1024]{2,1,0:T(8,128)(2,1)} %copy-done.5) | copy-start | bytes 1179652
  76.3 43.7 %collective-permute-start.7 = (bf16[6,16,1024]{2,1,0:T(8,128)(2,1)S(1)}, bf16[6,16,1024]{2,1,0:T(8,128)(2,1)S(1)}, u32[]{:S(2)}, u32[]{:S(2)}) collective-permute-start(bf16[6,16,1024]{2,1,0:T(8,128)(2,1)S(1)} %get-tuple-element.43), channel_id=1, source_target_pairs={{0,64},{64,128},{128,192},{192,256},{256,320},{320,384},{384,448},... | collective-permute-start | bytes 589832 | tf_op jit(solution)/shard_map/ppermute | solution.py:292
  80.7 39.4 %collective-permute-start.8 = (bf16[6,16,1024]{2,1,0:T(8,128)(2,1)S(1)}, bf16[6,16,1024]{2,1,0:T(8,128)(2,1)S(1)}, u32[]{:S(2)}, u32[]{:S(2)}) collective-permute-start(bf16[6,16,1024]{2,1,0:T(8,128)(2,1)S(1)} %get-tuple-element.44), channel_id=1, source_target_pairs={{64,0},{128,64},{192,128},{256,192},{320,256},{384,320},{448,384},... | collective-permute-start | bytes 589832 | tf_op jit(solution)/shard_map/ppermute | solution.py:292
  102.7 25.7 %all-to-all-start.1 = ((bf16[8,8,1024]{2,1,0:T(8,128)(2,1)}), bf16[8,8,1024]{2,1,0:T(8,128)(2,1)S(1)}, u32[]{:S(2)}, u32[]{:S(2)}) async-start(bf16[8,8,1024]{2,1,0:T(8,128)(2,1)} %share.1), calls=%async_computation.1 | async-start | bytes 262144 | tf_op jit(solution)/shard_map/all_to_all | solution.py:366

commit v4 on v3

v4 whole, which is shorter than its diff:
```python
import functools

import jax
import jax.numpy as jnp
from jax import lax
from jax.experimental import pallas as pl
from jax.experimental.pallas import tpu as pltpu
from jax.sharding import PartitionSpec as P

HEADS = 8
RADIUS = 6
SIDE = 8
LANES = 128
STRIP = 4
PACK = 4

NT = (((1,), (1,)), ((), ()))
NN = (((1,), (0,)), ((), ()))


def mm(a, b, dims):
    return lax.dot_general(a, b, dims, preferred_element_type=jnp.float32)


def spread(block, diag):
    tall = jnp.concatenate([block.astype(jnp.float32)] * PACK, axis=0)
    return jnp.where(diag, tall, 0.0).astype(jnp.bfloat16)


def diagonal(square, head, strip_q):
    return jnp.concatenate(
        [square[h * head : (h + 1) * head, h * strip_q : (h + 1) * strip_q] for h in range(PACK)],
        axis=0,
    )


def masks(rows, cols, inner):
    head = inner // HEADS
    wide = cols + 2 * SIDE
    strip_q = STRIP * cols
    slab = (STRIP + 2 * RADIUS) * wide
    lanes = PACK * strip_q
    key = lax.broadcasted_iota(jnp.int32, (slab, lanes), 0)
    query = lax.broadcasted_iota(jnp.int32, (slab, lanes), 1) & (strip_q - 1)
    row = key // wide
    place = key & (wide - 1)
    col = jnp.where(
        place < cols, place, jnp.where(place < cols + SIDE, place - cols - SIDE, place - SIDE)
    )
    row_gap = row - query // cols
    col_gap = jnp.abs(col - (query & (cols - 1)))
    near = (row_gap >= 0) & (row_gap <= 2 * RADIUS) & (col_gap <= RADIUS)
    diag = (lax.broadcasted_iota(jnp.int32, (lanes, PACK * head), 0) // strip_q) == (
        lax.broadcasted_iota(jnp.int32, (lanes, PACK * head), 1) // head
    )
    return near, row, diag


def beside(west, east):
    pair = [west.astype(jnp.float32), east.astype(jnp.float32)]
    return jnp.concatenate(pair, axis=1).astype(jnp.bfloat16)


def geometry(rows, cols, inner):
    head = inner // HEADS
    group = PACK * head
    strip_q = STRIP * cols
    slab_rows = STRIP + 2 * RADIUS
    wide = cols + 2 * SIDE
    return head, group, strip_q, slab_rows, wide, slab_rows * wide


def query_kernel(
    lat_total, place_ref, qg_ref, ext_ref, west_ref, east_ref, up_ref,
    dq_ref, stats_ref, keep_ref, give_ref, kv, kt, vt, att_t, dq_t, raw,
):
    rows, cols, inner = dq_ref.shape
    ext_rows = rows + 2 * RADIUS
    head, group, strip_q, slab_rows, wide, slab = geometry(rows, cols, inner)
    scale = head ** (-0.5)
    base, core = place_ref[0], place_ref[1]

    kv[:, 0:cols, :] = ext_ref[...]
    kv[:, cols:wide, :] = beside(west_ref[...], east_ref[...])
    kt[...] = kv[:, :, 0:inner].reshape(ext_rows * wide, inner).T
    vt[...] = kv[:, :, inner:].reshape(ext_rows * wide, inner).T
    near, row, diag = masks(rows, cols, inner)

    for s in range(rows // STRIP):
        first = s * STRIP
        low = RADIUS - base - first
        allowed = near & (row >= low) & (row < low + lat_total)
        window = slice(first * wide, first * wide + slab)
        here = slice(s * strip_q, (s + 1) * strip_q)
        for part in range(HEADS // PACK):
            chans = slice(part * group, (part + 1) * group)
            others = slice(inner + part * group, inner + (part + 1) * group)
            keys = kv[first : first + slab_rows, :, chans].reshape(slab, group)
            values = kv[first : first + slab_rows, :, others].reshape(slab, group)
            q_wide = spread(
                qg_ref[first : first + STRIP, :, chans].reshape(strip_q, group) * scale, diag
            )
            g_wide = spread(qg_ref[first : first + STRIP, :, others].reshape(strip_q, group), diag)
            scores = jnp.where(allowed, mm(keys, q_wide, NT), -1e30)
            top = jnp.max(scores, axis=0, keepdims=True)
            weights = jnp.exp(scores - top)
            total = jnp.sum(weights, axis=0, keepdims=True)
            probs = weights * (1.0 / total)
            low_probs = probs.astype(jnp.bfloat16)
            att_t[chans, here] = diagonal(mm(vt[chans, window], low_probs, NN), head, strip_q)
            grad_prob = mm(values, g_wide, NT)
            delta = jnp.sum(low_probs.astype(jnp.float32) * grad_prob, axis=0, keepdims=True)
            grad_score = (probs * (grad_prob - delta)).astype(jnp.bfloat16)
            dq_t[chans, here] = diagonal(mm(kt[chans, window], grad_score, NN), head, strip_q) * scale
            norm = top + jnp.log(total)
            for h in range(PACK):
                at = part * PACK + h
                own = slice(h * strip_q, (h + 1) * strip_q)
                raw[at : at + 1, here] = norm[:, own]
                raw[HEADS + at : HEADS + at + 1, here] = delta[:, own]

    weight = mm(att_t[...].astype(jnp.bfloat16), up_ref[...], NN)
    weight = weight.reshape(keep_ref.shape[0], 2, keep_ref.shape[1], weight.shape[1])
    keep_ref[...] = jnp.where(core == 0, weight[:, 0], weight[:, 1])
    give_ref[...] = jnp.where(core == 0, weight[:, 1], weight[:, 0]).astype(jnp.bfloat16)
    terms = []
    for kind in range(2):
        rest = raw[kind * HEADS : (kind + 1) * HEADS, :]
        for _ in range(3):
            term = rest.astype(jnp.bfloat16).astype(jnp.float32)
            terms.append(term)
            rest = rest - term
    lanes = stats_ref.shape[2]
    terms.append(jnp.zeros((lanes - 6 * HEADS, rows * cols), jnp.float32))
    table = jnp.concatenate(terms, axis=0)
    stats_ref[...] = table.T.astype(jnp.bfloat16).reshape(rows, cols, lanes)
    dq_ref[...] = dq_t[...].T.astype(jnp.bfloat16).reshape(rows, cols, inner)


def key_kernel(
    lat_total, place_ref, keys_ref, values_ref, q_above, q_own, q_below, s_above, s_own, s_below,
    west_ref, east_ref,
    dk_ref, dv_ref, qg, stats, qt, gt, dk_t, dv_t,
):
    rows, cols, inner = dk_ref.shape
    ext_rows = rows + 2 * RADIUS
    head, group, strip_k, slab_rows, wide, slab = geometry(rows, cols, inner)
    scale = head ** (-0.5)
    lanes = s_own.shape[2]
    base = place_ref[0]

    for at, size, main, extra in (
        (0, RADIUS, q_above, s_above),
        (RADIUS, rows, q_own, s_own),
        (RADIUS + rows, RADIUS, q_below, s_below),
    ):
        qg[at : at + size, 0:cols, :] = main[...]
        stats[at : at + size, 0:cols, :] = extra[...]
    qg[:, cols:wide, :] = beside(west_ref[:, :, 0 : 2 * inner], east_ref[:, :, 0 : 2 * inner])
    stats[:, cols:wide, :] = beside(west_ref[:, :, 2 * inner :], east_ref[:, :, 2 * inner :])
    qt[...] = qg[:, :, 0:inner].reshape(ext_rows * wide, inner).T
    gt[...] = qg[:, :, inner:].reshape(ext_rows * wide, inner).T
    near, row, diag = masks(rows, cols, inner)
    lane = lax.broadcasted_iota(jnp.int32, (lanes, group), 0)
    of_head = lax.broadcasted_iota(jnp.int32, (lanes, group), 1) // strip_k

    def picked(kind, part):
        wanted = ((lane & (HEADS - 1)) == of_head + part * PACK) & (lane // (3 * HEADS) == kind)
        return jnp.where(wanted, 1.0, 0.0).astype(jnp.bfloat16)

    for s in range(rows // STRIP):
        first = s * STRIP
        low = RADIUS - base - first
        allowed = near & (row >= low) & (row < low + lat_total)
        window = slice(first * wide, first * wide + slab)
        here = slice(s * strip_k, (s + 1) * strip_k)
        table = stats[first : first + slab_rows].reshape(slab, lanes)
        for part in range(HEADS // PACK):
            chans = slice(part * group, (part + 1) * group)
            others = slice(inner + part * group, inner + (part + 1) * group)
            queries = qg[first : first + slab_rows, :, chans].reshape(slab, group)
            grads = qg[first : first + slab_rows, :, others].reshape(slab, group)
            k_wide = spread(
                keys_ref[first : first + STRIP, :, chans].reshape(strip_k, group) * scale, diag
            )
            v_wide = spread(values_ref[first : first + STRIP, :, chans].reshape(strip_k, group), diag)
            scores = mm(queries, k_wide, NT) - mm(table, picked(0, part), NN)
            probs = jnp.exp(jnp.where(allowed, scores, -1e30))
            grad_prob = mm(grads, v_wide, NT) - mm(table, picked(1, part), NN)
            grad_score = (probs * grad_prob).astype(jnp.bfloat16)
            dv_t[chans, here] = diagonal(
                mm(gt[chans, window], probs.astype(jnp.bfloat16), NN), head, strip_k
            )
            dk_t[chans, here] = diagonal(mm(qt[chans, window], grad_score, NN), head, strip_k) * scale

    dk_ref[...] = dk_t[...].T.astype(jnp.bfloat16).reshape(rows, cols, inner)
    dv_ref[...] = dv_t[...].T.astype(jnp.bfloat16).reshape(rows, cols, inner)


def edge_kernel(q_above, q_own, q_below, s_above, s_own, s_below, last_ref, first_ref):
    deep, rows = q_above.shape[0], q_own.shape[0]
    cols, chans = q_own.shape[1:]
    for at, size, main, extra in (
        (0, deep, q_above, s_above),
        (deep, rows, q_own, s_own),
        (deep + rows, deep, q_below, s_below),
    ):
        for source, lanes in ((main, slice(0, chans)), (extra, slice(chans, chans + extra.shape[2]))):
            block = source[...].astype(jnp.float32)
            first_ref[at : at + size, :, lanes] = block[:, :SIDE].astype(jnp.bfloat16)
            last_ref[at : at + size, :, lanes] = block[:, cols - SIDE :].astype(jnp.bfloat16)


def share_kernel(parts_ref, copies_ref):
    total = jnp.sum(parts_ref[...].astype(jnp.float32), axis=0).astype(jnp.bfloat16)
    copies_ref[...] = jnp.broadcast_to(total[None], copies_ref.shape)


def pack_kernel(keys_ref, values_ref, both_ref, sems):
    inner = keys_ref.shape[2]
    copies = [
        pltpu.make_async_copy(keys_ref, both_ref.at[:, :, pl.ds(0, inner)], sems.at[0]),
        pltpu.make_async_copy(values_ref, both_ref.at[:, :, pl.ds(inner, inner)], sems.at[1]),
    ]
    for copy in copies:
        copy.start()
    for copy in copies:
        copy.wait()


def fold_kernel(keep_ref, got_ref, half_ref):
    half_ref[...] = (keep_ref[...] + got_ref[...].astype(jnp.float32)).astype(jnp.bfloat16)


def mean_kernel(parts, terms_ref, out_ref):
    out_ref[...] = jnp.sum(terms_ref[...].astype(jnp.float32), axis=0) / parts


VMEM = pl.BlockSpec(memory_space=pltpu.VMEM)
SMEM = pl.BlockSpec(memory_space=pltpu.SMEM)
PARAMS = pltpu.CompilerParams(vmem_limit_bytes=20 << 20)
FOLD, EDGE = 6_000_000_000, 20_000_000_000
QUERY, KEY = 20_000_000_000, 20_000_000_000
SMALL = pltpu.CompilerParams(vmem_limit_bytes=8 << 20)


def shape(dims, kind=jnp.bfloat16):
    return jax.ShapeDtypeStruct(dims, kind)


def cost(flops):
    return pl.CostEstimate(flops=flops, bytes_accessed=4_000_000, transcendentals=0)


def over_queries(place, qg, extended, west, east, upstream, lat_total, out_rows):
    rows, cols = qg.shape[:2]
    inner = qg.shape[2] // 2
    ext_rows, wide = rows + 2 * RADIUS, cols + 2 * SIDE
    model = upstream.shape[1]
    return pl.pallas_call(
        functools.partial(query_kernel, lat_total),
        out_shape=(
            shape((rows, cols, inner)),
            shape((rows, cols, LANES)),
            shape((inner // (2 * out_rows), out_rows, model), jnp.float32),
            shape((inner // (2 * out_rows), out_rows, model)),
        ),
        in_specs=[SMEM] + [VMEM] * 5,
        out_specs=(VMEM,) * 4,
        scratch_shapes=[
            pltpu.VMEM((ext_rows, wide, 2 * inner), jnp.bfloat16),
            pltpu.VMEM((inner, ext_rows * wide), jnp.bfloat16),
            pltpu.VMEM((inner, ext_rows * wide), jnp.bfloat16),
            pltpu.VMEM((inner, rows * cols), jnp.float32),
            pltpu.VMEM((inner, rows * cols), jnp.float32),
            pltpu.VMEM((2 * HEADS, rows * cols), jnp.float32),
        ],
        compiler_params=PARAMS,
        cost_estimate=cost(QUERY),
        name="over_queries",
    )(place, qg, extended, west, east, upstream)


def over_keys(place, keys, values, pieces, west, east, lat_total):
    rows, cols, inner = keys.shape
    ext_rows, wide = rows + 2 * RADIUS, cols + 2 * SIDE
    return pl.pallas_call(
        functools.partial(key_kernel, lat_total),
        out_shape=(shape((rows, cols, inner)),) * 2,
        in_specs=[SMEM] + [VMEM] * 10,
        out_specs=(VMEM,) * 2,
        scratch_shapes=[
            pltpu.VMEM((ext_rows, wide, 2 * inner), jnp.bfloat16),
            pltpu.VMEM((ext_rows, wide, LANES), jnp.bfloat16),
            pltpu.VMEM((inner, ext_rows * wide), jnp.bfloat16),
            pltpu.VMEM((inner, ext_rows * wide), jnp.bfloat16),
            pltpu.VMEM((inner, rows * cols), jnp.float32),
            pltpu.VMEM((inner, rows * cols), jnp.float32),
        ],
        compiler_params=PARAMS,
        cost_estimate=cost(KEY),
        name="over_keys",
    )(place, keys, values, *pieces, west, east)


def ring(block, axis, by):
    size = lax.axis_size(axis)
    return lax.ppermute(block, axis, [(i, (i + by) % size) for i in range(size)])


def line(block, axis, by):
    size = lax.axis_size(axis)
    return lax.ppermute(
        block, axis, [(i, i + by) for i in range(size) if 0 <= i + by < size]
    )


def packed(left, right, name):
    rows, cols, inner = left.shape
    return pl.pallas_call(
        pack_kernel,
        out_shape=shape((rows, cols, 2 * inner)),
        in_specs=[pl.BlockSpec(memory_space=pl.ANY)] * 2,
        out_specs=VMEM,
        scratch_shapes=[pltpu.SemaphoreType.DMA((2,))],
        compiler_params=SMALL,
        name=name,
    )(left, right)


def poles(block):
    above = line(block[block.shape[0] - RADIUS :], "lat", 1)
    below = line(block[:RADIUS], "lat", -1)
    return above, below


def shards(queries, keys, values, upstream, out_weight):
    rows, cols, inner = queries.shape
    model = upstream.shape[2]
    tokens = rows * cols
    lat, lon = lax.axis_size("lat"), lax.axis_size("lon")
    lat_total = rows * lat
    out_rows = inner // lon
    place = jnp.stack([lax.axis_index("lat") * rows, lax.axis_index("lon") % 2]).astype(jnp.int32)
    up_flat = upstream.reshape(tokens, model)
    grads = (
        jnp.einsum("td,id->ti", up_flat, out_weight, preferred_element_type=jnp.float32)
        .astype(jnp.bfloat16)
        .reshape(rows, cols, inner)
    )
    both = packed(keys, values, "pack_kv")
    above, below = poles(both)
    extended = jnp.concatenate([above, both, below], axis=0)
    west = ring(extended[:, cols - SIDE :], "lon", 1)
    east = ring(extended[:, :SIDE], "lon", -1)

    grads, _ = lax.optimization_barrier((grads, extended))
    qg = packed(queries, grads, "pack_qg")
    q_above, q_below = poles(qg)
    grad_query, stats, keep, give = over_queries(
        place, qg, extended, west, east, up_flat, lat_total, out_rows
    )

    got = lax.ppermute(give, "lon", [(i, i ^ 1) for i in range(lon)])
    half = pl.pallas_call(
        fold_kernel,
        out_shape=shape(keep.shape),
        compiler_params=SMALL,
        cost_estimate=cost(FOLD),
        name="fold",
    )(keep, got)
    same_core = [[2 * i + c for i in range(lon // 2)] for c in range(2)]
    terms = lax.all_to_all(half, "lon", 0, 0, axis_index_groups=same_core, tiled=True)

    stats, _ = lax.optimization_barrier((stats, half))
    s_above, s_below = poles(stats)
    q_above, q_below, s_above, s_below = lax.optimization_barrier(
        (q_above, q_below, s_above, s_below)
    )
    pieces = (q_above, qg, q_below, s_above, stats, s_below)
    last, first = pl.pallas_call(
        edge_kernel,
        out_shape=(shape((rows + 2 * RADIUS, SIDE, 2 * inner + LANES)),) * 2,
        compiler_params=SMALL,
        cost_estimate=cost(EDGE),
        name="edge",
    )(*pieces)
    q_west = ring(last, "lon", 1)
    q_east = ring(first, "lon", -1)
    terms, _ = lax.optimization_barrier((terms, first))
    copies = pl.pallas_call(
        share_kernel,
        out_shape=shape((lat, out_rows, model)),
        compiler_params=SMALL,
        name="share",
    )(terms)
    every = lax.all_to_all(copies, "lat", 0, 0, tiled=True)
    q_west, q_east, _ = lax.optimization_barrier((q_west, q_east, copies))
    grad_key, grad_value = over_keys(
        place, keys, values, pieces, q_west, q_east, lat_total
    )
    grad_weight = pl.pallas_call(
        functools.partial(mean_kernel, lat_total),
        out_shape=shape((out_rows, model), jnp.float32),
        compiler_params=SMALL,
        name="mean",
    )(every)
    return (grad_query, grad_key, grad_value, grad_weight)


def solution(mesh):
    placed = P("lat", "lon", None)
    return jax.shard_map(
        shards,
        mesh=mesh,
        in_specs=(placed, placed, placed, placed, P()),
        out_specs=(placed, placed, placed, P("lon", None)),
        check_vma=False,
    )
```

time: 130 us -> 125 us (0.962)
  waiting for transfers between devices: 42.8 us -> 28 us
  starting transfers between devices: 67 us -> 77 us
  local copies, waits for them, and re-layouts: 5.44 us -> 3.41 us
    ppermute x4 -> x6, starting transfers between devices: 24.5 us -> 37.1 us  [line(): lax.ppermute(block, axis, [(i, i + by) for i in range(size) if 0 <= i + b...]
    all_to_all x1, starting transfers between devices: 17.4 us -> 11 us  [shards(): every = lax.all_to_all(copies, 'lat', 0, 0, tiled=True)]
    ppermute x4, waiting for transfers between devices: 10.8 us -> 4.53 us  [ring(): lax.ppermute(block, axis, [(i, (i + by) % size) for i in range(size)])]
    all_to_all x1, waiting for transfers between devices: 14.4 us -> 9.82 us  [shards(): lax.all_to_all(half, 'lon', 0, 0, axis_index_groups=same_core, tiled=True)]
    all_to_all x1, waiting for transfers between devices: 7.52 us -> 3.55 us  [shards(): every = lax.all_to_all(copies, 'lat', 0, 0, tiled=True)]
    ppermute x1, starting transfers between devices: 1.92 us -> 4.11 us  [shards(): got = lax.ppermute(give, 'lon', [(i, i ^ 1) for i in range(lon)])]
    unnamed x18, local copies, waits for them, and re-layouts: 4.47 us -> 2.38 us
    all_to_all x1, starting transfers between devices: 5.64 us -> 7.5 us  [shards(): lax.all_to_all(half, 'lon', 0, 0, axis_index_groups=same_core, tiled=True)]
  transfers between devices with their start and end apart: 11 -> 13, of which waited for: 6 -> 6; matrix products, arithmetic and copies ran while one was open for 0% -> 0% of each run, Pallas kernels for 6% -> 6%
where the time goes in v4:
time: 125 us; the launch traced here: 123 us
  starting transfers between devices  77 us (62%)
  waiting for transfers between devices  28 us (22%)
  Pallas kernels  13.4 us (11%)
  local copies, waits for them, and re-layouts  3.41 us (3%)
    ppermute x6, starting transfers between devices, line(): lax.ppermute(block, axis, [(i, i + by) for i in range(size) if 0 <= i + b...  37.1 us
    ppermute x4, starting transfers between devices, ring(): lax.ppermute(block, axis, [(i, (i + by) % size) for i in range(size)])  17.3 us
    all_to_all x1, starting transfers between devices, shards(): every = lax.all_to_all(copies, 'lat', 0, 0, tiled=True)  11 us
    ppermute x6, waiting for transfers between devices, line(): lax.ppermute(block, axis, [(i, i + by) for i in range(size) if 0 <= i + b...  10.1 us
    all_to_all x1, waiting for transfers between devices, shards(): lax.all_to_all(half, 'lon', 0, 0, axis_index_groups=same_core, tiled=True)  9.82 us
    all_to_all x1, starting transfers between devices, shards(): lax.all_to_all(half, 'lon', 0, 0, axis_index_groups=same_core, tiled=True)  7.5 us
    pallas_call x1, Pallas kernels, over_queries(): pl.pallas_call(functools.partial(query_kernel, lat_total), out_shape=(sha...  5.18 us
    pallas_call x1, Pallas kernels, over_keys(): pl.pallas_call(functools.partial(key_kernel, lat_total), out_shape=(shape...  4.77 us
  transfers between devices with their start and end apart: 13, of which 6 were waited for; matrix products, arithmetic and copies ran while one was open for 0% of the time, Pallas kernels for 6%

profile of v4, /device:TPU:6, one launch (start us, length us, event | category | flops | bytes accessed | tf_op | source)
XLA Modules:
  0.0 123.4 jit_solution(13593646074265637844)
XLA Ops:
  0.7 1.0 copy-done.3
  1.7 0.9 copy-done.5
  2.7 10.9 %collective-permute-start = (bf16[6,16,1024]{2,1,0:T(8,128)(2,1)S(1)}, bf16[6,16,1024]{2,1,0:T(8,128)(2,1)S(1)}, u32[]{:S(2)}, u32[]{:S(2)}) collective-permute-start(bf16[6,16,1024]{2,1,0:T(8,128)(2,1)S(1)} %get-tuple-element.42), channel_id=1, source_target_pairs={{0,64},{64,128},{128,192},{192,256},{256,320},{320,384},{384,448},... | collective-permute-start | bytes 589832 | tf_op jit(solution)/shard_map/ppermute | solution.py:313
  13.6 2.2 %collective-permute-start.1 = (bf16[6,16,1024]{2,1,0:T(8,128)(2,1)S(1)}, bf16[6,16,1024]{2,1,0:T(8,128)(2,1)S(1)}, u32[]{:S(2)}, u32[]{:S(2)}) collective-permute-start(bf16[6,16,1024]{2,1,0:T(8,128)(2,1)S(1)} %get-tuple-element.43), channel_id=1, source_target_pairs={{64,0},{128,64},{192,128},{256,192},{320,256},{384,320},{448,384},... | collective-permute-start | bytes 589832 | tf_op jit(solution)/shard_map/ppermute | solution.py:313
  15.8 3.1 %collective-permute-done = bf16[6,16,1024]{2,1,0:T(8,128)(2,1)S(1)} collective-permute-done((bf16[6,16,1024]{2,1,0:T(8,128)(2,1)S(1)}, bf16[6,16,1024]{2,1,0:T(8,128)(2,1)S(1)}, u32[]{:S(2)}, u32[]{:S(2)}) %collective-permute-start) | collective-permute-done | bytes 196640 | tf_op jit(solution)/shard_map/ppermute | solution.py:313
  18.9 7.0 %collective-permute-done.1 = bf16[6,16,1024]{2,1,0:T(8,128)(2,1)S(1)} collective-permute-done((bf16[6,16,1024]{2,1,0:T(8,128)(2,1)S(1)}, bf16[6,16,1024]{2,1,0:T(8,128)(2,1)S(1)}, u32[]{:S(2)}, u32[]{:S(2)}) %collective-permute-start.1) | collective-permute-done | bytes 196640 | tf_op jit(solution)/shard_map/ppermute | solution.py:313
  25.9 0.1 pad_maximum_fusion.ext_ref
  26.0 1.0 fusion
  27.0 1.9 %collective-permute-start.2 = (bf16[24,8,1024]{2,1,0:T(8,128)(2,1)}, bf16[24,8,1024]{2,1,0:T(8,128)(2,1)S(1)}, u32[]{:S(2)}, u32[]{:S(2)}) collective-permute-start(bf16[24,8,1024]{2,1,0:T(8,128)(2,1)} %get-tuple-element.39), channel_id=1, source_target_pairs={{0,1},{1,2},{2,3},{3,4},{4,5},{5,6},{6,7},{7,8},{8,9},{9,10},{10,1... | collective-permute-start | bytes 1179656 | tf_op jit(solution)/shard_map/ppermute | solution.py:308
  28.9 7.5 %collective-permute-start.3 = (bf16[24,8,1024]{2,1,0:T(8,128)(2,1)}, bf16[24,8,1024]{2,1,0:T(8,128)(2,1)S(1)}, u32[]{:S(2)}, u32[]{:S(2)}) collective-permute-start(bf16[24,8,1024]{2,1,0:T(8,128)(2,1)} %get-tuple-element.38), channel_id=1, source_target_pairs={{0,63},{1,0},{2,1},{3,2},{4,3},{5,4},{6,5},{7,6},{8,7},{9,8},{10,9... | collective-permute-start | bytes 1179656 | tf_op jit(solution)/shard_map/ppermute | solution.py:308
  36.4 0.1 pad_add_fusion.place_ref
  36.5 0.5 convolution_convert_fusion
  37.0 0.4 copy-done.2
  37.5 2.6 %collective-permute-done.2.west_ref = bf16[24,8,1024]{2,1,0:T(8,128)(2,1)S(1)} collective-permute-done((bf16[24,8,1024]{2,1,0:T(8,128)(2,1)}, bf16[24,8,1024]{2,1,0:T(8,128)(2,1)S(1)}, u32[]{:S(2)}, u32[]{:S(2)}) %collective-permute-start.2) | collective-permute-done | bytes 393248 | tf_op jit(solution)/shard_map/ppermute | solution.py:308
  40.2 1.9 %collective-permute-done.3.east_ref = bf16[24,8,1024]{2,1,0:T(8,128)(2,1)S(1)} collective-permute-done((bf16[24,8,1024]{2,1,0:T(8,128)(2,1)}, bf16[24,8,1024]{2,1,0:T(8,128)(2,1)S(1)}, u32[]{:S(2)}, u32[]{:S(2)}) %collective-permute-start.3) | collective-permute-done | bytes 393248 | tf_op jit(solution)/shard_map/ppermute | solution.py:308
  42.1 5.2 %over_queries.1 = (bf16[12,16,512]{2,1,0:T(8,128)(2,1)}, bf16[12,16,128]{2,1,0:T(8,128)(2,1)S(1)}, f32[32,8,1024]{2,1,0:T(8,128)S(1)}, bf16[32,8,1024]{2,1,0:T(8,128)(2,1)S(1)}) custom-call(s32[2]{0:T(128)S(1)} %pad_add_fusion.place_ref, bf16[12,16,1024]{2,1,0:T(8,128)(2,1)S(1)} %pack_qg.1.qg_ref.q_own, bf16[24,16,1024]{2,1,0:T(8,128)(2,1)S(1)} %pad_maximum_fusion.ext_ref, ...), custom_call_target="tpu_custom_call" | custom-call | flops 20000000000 | bytes 4000000 | tf_op jit(solution)/shard_map/over_queries/pallas_call | solution.py:260
  47.3 4.1 %collective-permute-start.6 = (bf16[32,8,1024]{2,1,0:T(8,128)(2,1)S(1)}, bf16[32,8,1024]{2,1,0:T(8,128)(2,1)S(1)}, u32[]{:S(2)}, u32[]{:S(2)}) collective-permute-start(bf16[32,8,1024]{2,1,0:T(8,128)(2,1)S(1)} %get-tuple-element.25), channel_id=1, source_target_pairs={{0,1},{1,0},{2,3},{3,2},{4,5},{5,4},{6,7},{7,6},{8,9},{9,8},{10,11... | collective-permute-start | bytes 1572872 | tf_op jit(solution)/shard_map/ppermute | solution.py:364
  51.4 5.2 %collective-permute-start.4 = (bf16[6,16,1024]{2,1,0:T(8,128)(2,1)S(1)}, bf16[6,16,1024]{2,1,0:T(8,128)(2,1)S(1)}, u32[]{:S(2)}, u32[]{:S(2)}) collective-permute-start(bf16[6,16,1024]{2,1,0:T(8,128)(2,1)S(1)} %get-tuple-element.41), channel_id=1, source_target_pairs={{0,64},{64,128},{128,192},{192,256},{256,320},{320,384},{384,448},... | collective-permute-start | bytes 589832 | tf_op jit(solution)/shard_map/ppermute | solution.py:313
  56.7 8.1 %collective-permute-start.5 = (bf16[6,16,1024]{2,1,0:T(8,128)(2,1)S(1)}, bf16[6,16,1024]{2,1,0:T(8,128)(2,1)S(1)}, u32[]{:S(2)}, u32[]{:S(2)}) collective-permute-start(bf16[6,16,1024]{2,1,0:T(8,128)(2,1)S(1)} %get-tuple-element.40), channel_id=1, source_target_pairs={{64,0},{128,64},{192,128},{256,192},{320,256},{384,320},{448,384},... | collective-permute-start | bytes 589832 | tf_op jit(solution)/shard_map/ppermute | solution.py:313
  64.8 0.9 fold.1
  65.7 1.9 %collective-permute-start.7 = (bf16[6,16,128]{2,1,0:T(8,128)(2,1)S(1)}, bf16[6,16,128]{2,1,0:T(8,128)(2,1)S(1)}, u32[]{:S(2)}, u32[]{:S(2)}) collective-permute-start(bf16[6,16,128]{2,1,0:T(8,128)(2,1)S(1)} %get-tuple-element.45), channel_id=1, source_target_pairs={{0,64},{64,128},{128,192},{192,256},{256,320},{320,384},{384,448},... | collective-permute-start | bytes 73736 | tf_op jit(solution)/shard_map/ppermute | solution.py:313
  67.6 8.7 %collective-permute-start.8 = (bf16[6,16,128]{2,1,0:T(8,128)(2,1)S(1)}, bf16[6,16,128]{2,1,0:T(8,128)(2,1)S(1)}, u32[]{:S(2)}, u32[]{:S(2)}) collective-permute-start(bf16[6,16,128]{2,1,0:T(8,128)(2,1)S(1)} %get-tuple-element.44), channel_id=1, source_target_pairs={{64,0},{128,64},{192,128},{256,192},{320,256},{384,320},{448,384},... | collective-permute-start | bytes 73736 | tf_op jit(solution)/shard_map/ppermute | solution.py:313
  76.4 7.5 %all-to-all-start = ((bf16[32,8,1024]{2,1,0:T(8,128)(2,1)}), bf16[32,8,1024]{2,1,0:T(8,128)(2,1)S(1)}, u32[]{:S(2)}, u32[]{:S(2)}) async-start(bf16[32,8,1024]{2,1,0:T(8,128)(2,1)} %fold.1), calls=%async_computation | async-start | bytes 1048576 | tf_op jit(solution)/shard_map/all_to_all | solution.py:373
  83.9 1.0 edge.1
  85.0 5.9 %collective-permute-start.10 = (bf16[24,8,1152]{2,1,0:T(8,128)(2,1)}, bf16[24,8,1152]{2,1,0:T(8,128)(2,1)S(1)}, u32[]{:S(2)}, u32[]{:S(2)}) collective-permute-start(bf16[24,8,1152]{2,1,0:T(8,128)(2,1)} %get-tuple-element.32), channel_id=1, source_target_pairs={{0,63},{1,0},{2,1},{3,2},{4,3},{5,4},{6,5},{7,6},{8,7},{9,8},{10,9... | collective-permute-start | bytes 1327112 | tf_op jit(solution)/shard_map/ppermute | solution.py:308
  90.9 1.9 %collective-permute-start.9 = (bf16[24,8,1152]{2,1,0:T(8,128)(2,1)}, bf16[24,8,1152]{2,1,0:T(8,128)(2,1)S(1)}, u32[]{:S(2)}, u32[]{:S(2)}) collective-permute-start(bf16[24,8,1152]{2,1,0:T(8,128)(2,1)} %get-tuple-element.31), channel_id=1, source_target_pairs={{0,1},{1,2},{2,3},{3,4},{4,5},{5,6},{6,7},{7,8},{8,9},{9,10},{10,1... | collective-permute-start | bytes 1327112 | tf_op jit(solution)/shard_map/ppermute | solution.py:308
  92.8 9.8 %all-to-all-done.parts_ref = bf16[32,8,1024]{2,1,0:T(8,128)(2,1)S(1)} async-done(((bf16[32,8,1024]{2,1,0:T(8,128)(2,1)}), bf16[32,8,1024]{2,1,0:T(8,128)(2,1)S(1)}, u32[]{:S(2)}, u32[]{:S(2)}) %all-to-all-start) | async-done | bytes 524320 | tf_op jit(solution)/shard_map/all_to_all | solution.py:373
  102.6 0.7 share.1
  103.4 11.0 %all-to-all-start.1 = ((bf16[8,8,1024]{2,1,0:T(8,128)(2,1)}), bf16[8,8,1024]{2,1,0:T(8,128)(2,1)S(1)}, u32[]{:S(2)}, u32[]{:S(2)}) async-start(bf16[8,8,1024]{2,1,0:T(8,128)(2,1)} %share.1), calls=%async_computation.1 | async-start | bytes 262144 | tf_op jit(solution)/shard_map/all_to_all | solution.py:397
  114.5 4.8 %over_keys.1 = (bf16[12,16,512]{2,1,0:T(8,128)(2,1)}, bf16[12,16,512]{2,1,0:T(8,128)(2,1)}) custom-call(s32[2]{0:T(128)S(1)} %copy-done.8, bf16[12,16,512]{2,1,0:T(8,128)(2,1)S(1)} %copy-done.4, bf16[12,16,512]{2,1,0:T(8,128)(2,1)S(1)} %copy-done.6, bf16[6,16,1024]{2,1,0:T(8,128)(2,1)S(1)} %collective-permute-done.4.q_above, ...), custom_call_target="tpu_custom_call" | custom-call | flops 20000000000 | bytes 4000000 | tf_op jit(solution)/shard_map/over_keys/pallas_call | solution.py:287
  119.2 3.5 %all-to-all-done.1.terms_ref = bf16[8,8,1024]{2,1,0:T(8,128)(2,1)S(1)} async-done(((bf16[8,8,1024]{2,1,0:T(8,128)(2,1)}), bf16[8,8,1024]{2,1,0:T(8,128)(2,1)S(1)}, u32[]{:S(2)}, u32[]{:S(2)}) %all-to-all-start.1) | async-done | bytes 131104 | tf_op jit(solution)/shard_map/all_to_all | solution.py:397
  122.8 0.6 mean.1
  (27 shorter events, 0.3 us)
Async XLA Ops:
  0.6 35.9 %copy-start = (bf16[512,1024]{1,0:T(8,128)(2,1)S(1)}, bf16[512,1024]{1,0:T(8,128)(2,1)}, u32[]{:S(2)}) copy-start(bf16[512,1024]{1,0:T(8,128)(2,1)} %param.9) | copy-start | bytes 3145732
  0.6 1.0 copy-start.3
  1.7 0.9 copy-start.5
  2.7 16.2 %collective-permute-start = (bf16[6,16,1024]{2,1,0:T(8,128)(2,1)S(1)}, bf16[6,16,1024]{2,1,0:T(8,128)(2,1)S(1)}, u32[]{:S(2)}, u32[]{:S(2)}) collective-permute-start(bf16[6,16,1024]{2,1,0:T(8,128)(2,1)S(1)} %get-tuple-element.42), channel_id=1, source_target_pairs={{0,64},{64,128},{128,192},{192,256},{256,320},{320,384},{384,448},... | collective-permute-start | bytes 589832 | tf_op jit(solution)/shard_map/ppermute | solution.py:313
  13.6 12.3 %collective-permute-start.1 = (bf16[6,16,1024]{2,1,0:T(8,128)(2,1)S(1)}, bf16[6,16,1024]{2,1,0:T(8,128)(2,1)S(1)}, u32[]{:S(2)}, u32[]{:S(2)}) collective-permute-start(bf16[6,16,1024]{2,1,0:T(8,128)(2,1)S(1)} %get-tuple-element.43), channel_id=1, source_target_pairs={{64,0},{128,64},{192,128},{256,192},{320,256},{384,320},{448,384},... | collective-permute-start | bytes 589832 | tf_op jit(solution)/shard_map/ppermute | solution.py:313
  26.0 10.5 %copy-start.1 = (bf16[12,16,1024]{2,1,0:T(8,128)(2,1)S(1)}, bf16[12,16,1024]{2,1,0:T(8,128)(2,1)}, u32[]{:S(2)}) copy-start(bf16[12,16,1024]{2,1,0:T(8,128)(2,1)} %param.8) | copy-start | bytes 1179652
  27.0 13.2 %collective-permute-start.2 = (bf16[24,8,1024]{2,1,0:T(8,128)(2,1)}, bf16[24,8,1024]{2,1,0:T(8,128)(2,1)S(1)}, u32[]{:S(2)}, u32[]{:S(2)}) collective-permute-start(bf16[24,8,1024]{2,1,0:T(8,128)(2,1)} %get-tuple-element.39), channel_id=1, source_target_pairs={{0,1},{1,2},{2,3},{3,4},{4,5},{5,6},{6,7},{7,8},{8,9},{9,10},{10,1... | collective-permute-start | bytes 1179656 | tf_op jit(solution)/shard_map/ppermute | solution.py:308
  28.9 13.2 %collective-permute-start.3 = (bf16[24,8,1024]{2,1,0:T(8,128)(2,1)}, bf16[24,8,1024]{2,1,0:T(8,128)(2,1)S(1)}, u32[]{:S(2)}, u32[]{:S(2)}) collective-permute-start(bf16[24,8,1024]{2,1,0:T(8,128)(2,1)} %get-tuple-element.38), channel_id=1, source_target_pairs={{0,63},{1,0},{2,1},{3,2},{4,3},{5,4},{6,5},{7,6},{8,7},{9,8},{10,9... | collective-permute-start | bytes 1179656 | tf_op jit(solution)/shard_map/ppermute | solution.py:308
  36.5 5.5 %copy-start.7 = (s32[2]{0:T(128)}, s32[2]{0:T(128)S(1)}, u32[]{:S(2)}) copy-start(s32[2]{0:T(128)S(1)} %pad_add_fusion.place_ref) | copy-start | bytes 28
  36.5 0.9 copy-start.2
  47.3 17.5 %collective-permute-start.6 = (bf16[32,8,1024]{2,1,0:T(8,128)(2,1)S(1)}, bf16[32,8,1024]{2,1,0:T(8,128)(2,1)S(1)}, u32[]{:S(2)}, u32[]{:S(2)}) collective-permute-start(bf16[32,8,1024]{2,1,0:T(8,128)(2,1)S(1)} %get-tuple-element.25), channel_id=1, source_target_pairs={{0,1},{1,0},{2,3},{3,2},{4,5},{5,4},{6,7},{7,6},{8,9},{9,8},{10,11... | collective-permute-start | bytes 1572872 | tf_op jit(solution)/shard_map/ppermute | solution.py:364
  51.4 32.5 %collective-permute-start.4 = (bf16[6,16,1024]{2,1,0:T(8,128)(2,1)S(1)}, bf16[6,16,1024]{2,1,0:T(8,128)(2,1)S(1)}, u32[]{:S(2)}, u32[]{:S(2)}) collective-permute-start(bf16[6,16,1024]{2,1,0:T(8,128)(2,1)S(1)} %get-tuple-element.41), channel_id=1, source_target_pairs={{0,64},{64,128},{128,192},{192,256},{256,320},{320,384},{384,448},... | collective-permute-start | bytes 589832 | tf_op jit(solution)/shard_map/ppermute | solution.py:313
  56.7 27.2 %collective-permute-start.5 = (bf16[6,16,1024]{2,1,0:T(8,128)(2,1)S(1)}, bf16[6,16,1024]{2,1,0:T(8,128)(2,1)S(1)}, u32[]{:S(2)}, u32[]{:S(2)}) collective-permute-start(bf16[6,16,1024]{2,1,0:T(8,128)(2,1)S(1)} %get-tuple-element.40), channel_id=1, source_target_pairs={{64,0},{128,64},{192,128},{256,192},{320,256},{384,320},{448,384},... | collective-permute-start | bytes 589832 | tf_op jit(solution)/shard_map/ppermute | solution.py:313
  65.7 18.2 %collective-permute-start.7 = (bf16[6,16,128]{2,1,0:T(8,128)(2,1)S(1)}, bf16[6,16,128]{2,1,0:T(8,128)(2,1)S(1)}, u32[]{:S(2)}, u32[]{:S(2)}) collective-permute-start(bf16[6,16,128]{2,1,0:T(8,128)(2,1)S(1)} %get-tuple-element.45), channel_id=1, source_target_pairs={{0,64},{64,128},{128,192},{192,256},{256,320},{320,384},{384,448},... | collective-permute-start | bytes 73736 | tf_op jit(solution)/shard_map/ppermute | solution.py:313
  67.6 16.3 %collective-permute-start.8 = (bf16[6,16,128]{2,1,0:T(8,128)(2,1)S(1)}, bf16[6,16,128]{2,1,0:T(8,128)(2,1)S(1)}, u32[]{:S(2)}, u32[]{:S(2)}) collective-permute-start(bf16[6,16,128]{2,1,0:T(8,128)(2,1)S(1)} %get-tuple-element.44), channel_id=1, source_target_pairs={{64,0},{128,64},{192,128},{256,192},{320,256},{384,320},{448,384},... | collective-permute-start | bytes 73736 | tf_op jit(solution)/shard_map/ppermute | solution.py:313
  76.4 26.3 %all-to-all-start = ((bf16[32,8,1024]{2,1,0:T(8,128)(2,1)}), bf16[32,8,1024]{2,1,0:T(8,128)(2,1)S(1)}, u32[]{:S(2)}, u32[]{:S(2)}) async-start(bf16[32,8,1024]{2,1,0:T(8,128)(2,1)} %fold.1), calls=%async_computation | async-start | bytes 1048576 | tf_op jit(solution)/shard_map/all_to_all | solution.py:373
  83.9 30.5 %copy-start.6 = (bf16[12,16,512]{2,1,0:T(8,128)(2,1)S(1)}, bf16[12,16,512]{2,1,0:T(8,128)(2,1)}, u32[]{:S(2)}) copy-start(bf16[12,16,512]{2,1,0:T(8,128)(2,1)} %values_ref.3) | copy-start | bytes 589828
  85.0 29.5 %collective-permute-start.10 = (bf16[24,8,1152]{2,1,0:T(8,128)(2,1)}, bf16[24,8,1152]{2,1,0:T(8,128)(2,1)S(1)}, u32[]{:S(2)}, u32[]{:S(2)}) collective-permute-start(bf16[24,8,1152]{2,1,0:T(8,128)(2,1)} %get-tuple-element.32), channel_id=1, source_target_pairs={{0,63},{1,0},{2,1},{3,2},{4,3},{5,4},{6,5},{7,6},{8,7},{9,8},{10,9... | collective-permute-start | bytes 1327112 | tf_op jit(solution)/shard_map/ppermute | solution.py:308
  90.9 23.5 %collective-permute-start.9 = (bf16[24,8,1152]{2,1,0:T(8,128)(2,1)}, bf16[24,8,1152]{2,1,0:T(8,128)(2,1)S(1)}, u32[]{:S(2)}, u32[]{:S(2)}) collective-permute-start(bf16[24,8,1152]{2,1,0:T(8,128)(2,1)} %get-tuple-element.31), channel_id=1, source_target_pairs={{0,1},{1,2},{2,3},{3,4},{4,5},{5,6},{6,7},{7,8},{8,9},{9,10},{10,1... | collective-permute-start | bytes 1327112 | tf_op jit(solution)/shard_map/ppermute | solution.py:308
  103.4 11.1 %copy-start.4 = (bf16[12,16,512]{2,1,0:T(8,128)(2,1)S(1)}, bf16[12,16,512]{2,1,0:T(8,128)(2,1)}, u32[]{:S(2)}) copy-start(bf16[12,16,512]{2,1,0:T(8,128)(2,1)} %keys_ref.5) | copy-start | bytes 589828
  103.4 11.1 %copy-start.8 = (s32[2]{0:T(128)S(1)}, s32[2]{0:T(128)}, u32[]{:S(2)}) copy-start(s32[2]{0:T(128)} %copy-done.7) | copy-start | bytes 28
  103.4 19.4 %all-to-all-start.1 = ((bf16[8,8,1024]{2,1,0:T(8,128)(2,1)}), bf16[8,8,1024]{2,1,0:T(8,128)(2,1)S(1)}, u32[]{:S(2)}, u32[]{:S(2)}) async-start(bf16[8,8,1024]{2,1,0:T(8,128)(2,1)} %share.1), calls=%async_computation.1 | async-start | bytes 262144 | tf_op jit(solution)/shard_map/all_to_all | solution.py:397

commit v5 on v4

--- a/solution.py
+++ b/solution.py
@@ -72,13 +72,13 @@
 
 def query_kernel(
     lat_total, place_ref, qg_ref, ext_ref, west_ref, east_ref, up_ref,
-    dq_ref, stats_ref, keep_ref, give_ref, kv, kt, vt, att_t, dq_t, raw,
+    dq_ref, stats_ref, term_ref, kv, kt, vt, att_t, dq_t, raw,
 ):
     rows, cols, inner = dq_ref.shape
     ext_rows = rows + 2 * RADIUS
     head, group, strip_q, slab_rows, wide, slab = geometry(rows, cols, inner)
     scale = head ** (-0.5)
-    base, core = place_ref[0], place_ref[1]
+    base = place_ref[0]
 
     kv[:, 0:cols, :] = ext_ref[...]
     kv[:, cols:wide, :] = beside(west_ref[...], east_ref[...])
@@ -120,9 +120,9 @@
                 raw[HEADS + at : HEADS + at + 1, here] = delta[:, own]
 
     weight = mm(att_t[...].astype(jnp.bfloat16), up_ref[...], NN)
-    weight = weight.reshape(keep_ref.shape[0], 2, keep_ref.shape[1], weight.shape[1])
-    keep_ref[...] = jnp.where(core == 0, weight[:, 0], weight[:, 1])
-    give_ref[...] = jnp.where(core == 0, weight[:, 1], weight[:, 0]).astype(jnp.bfloat16)
+    weight = weight.reshape(term_ref.shape[1], 2, term_ref.shape[2], weight.shape[1])
+    for core in range(2):
+        term_ref[core] = weight[:, core].astype(jnp.bfloat16)
     terms = []
     for kind in range(2):
         rest = raw[kind * HEADS : (kind + 1) * HEADS, :]
@@ -228,8 +228,9 @@
         copy.wait()
 
 
-def fold_kernel(keep_ref, got_ref, half_ref):
-    half_ref[...] = (keep_ref[...] + got_ref[...].astype(jnp.float32)).astype(jnp.bfloat16)
+def fold_kernel(pair_ref, half_ref):
+    pair = pair_ref[...].astype(jnp.float32)
+    half_ref[...] = (pair[0] + pair[1]).astype(jnp.bfloat16)
 
 
 def mean_kernel(parts, terms_ref, out_ref):
@@ -239,8 +240,8 @@
 VMEM = pl.BlockSpec(memory_space=pltpu.VMEM)
 SMEM = pl.BlockSpec(memory_space=pltpu.SMEM)
 PARAMS = pltpu.CompilerParams(vmem_limit_bytes=20 << 20)
-FOLD, EDGE = 6_000_000_000, 20_000_000_000
-QUERY, KEY = 20_000_000_000, 20_000_000_000
+FOLD, EDGE = 1_000_000, 4_000_000_000
+QUERY, KEY = 40_000_000_000, 20_000_000_000
 SMALL = pltpu.CompilerParams(vmem_limit_bytes=8 << 20)
 
 
@@ -262,11 +263,10 @@
         out_shape=(
             shape((rows, cols, inner)),
             shape((rows, cols, LANES)),
-            shape((inner // (2 * out_rows), out_rows, model), jnp.float32),
-            shape((inner // (2 * out_rows), out_rows, model)),
+            shape((2, inner // (2 * out_rows), out_rows, model)),
         ),
         in_specs=[SMEM] + [VMEM] * 5,
-        out_specs=(VMEM,) * 4,
+        out_specs=(VMEM,) * 3,
         scratch_shapes=[
             pltpu.VMEM((ext_rows, wide, 2 * inner), jnp.bfloat16),
             pltpu.VMEM((inner, ext_rows * wide), jnp.bfloat16),
@@ -341,7 +341,7 @@
     lat, lon = lax.axis_size("lat"), lax.axis_size("lon")
     lat_total = rows * lat
     out_rows = inner // lon
-    place = jnp.stack([lax.axis_index("lat") * rows, lax.axis_index("lon") % 2]).astype(jnp.int32)
+    place = (lax.axis_index("lat") * rows).astype(jnp.int32).reshape(1)
     up_flat = upstream.reshape(tokens, model)
     grads = (
         jnp.einsum("td,id->ti", up_flat, out_weight, preferred_element_type=jnp.float32)
@@ -357,18 +357,19 @@
     grads, _ = lax.optimization_barrier((grads, extended))
     qg = packed(queries, grads, "pack_qg")
     q_above, q_below = poles(qg)
-    grad_query, stats, keep, give = over_queries(
+    grad_query, stats, term = over_queries(
         place, qg, extended, west, east, up_flat, lat_total, out_rows
     )
 
-    got = lax.ppermute(give, "lon", [(i, i ^ 1) for i in range(lon)])
+    chips = [[2 * i, 2 * i + 1] for i in range(lon // 2)]
+    pair = lax.all_to_all(term, "lon", 0, 0, axis_index_groups=chips, tiled=True)
     half = pl.pallas_call(
         fold_kernel,
-        out_shape=shape(keep.shape),
+        out_shape=shape(term.shape[1:]),
         compiler_params=SMALL,
         cost_estimate=cost(FOLD),
         name="fold",
-    )(keep, got)
+    )(pair)
     same_core = [[2 * i + c for i in range(lon // 2)] for c in range(2)]
     terms = lax.all_to_all(half, "lon", 0, 0, axis_index_groups=same_core, tiled=True)
 

time: 125 us -> 131 us (1.048)
  the two profiles are of different devices: /device:TPU:6 before, /device:TPU:3 now
where the time goes in v5:
time: 131 us
  starting transfers between devices  68.4 us (52%)
  waiting for transfers between devices  32.3 us (25%)
  Pallas kernels  12.2 us (9%)
  blocking collectives  10.4 us (8%)
  local copies, waits for them, and re-layouts  5.84 us (4%)
    ppermute x6, starting transfers between devices, line(): lax.ppermute(block, axis, [(i, i + by) for i in range(size) if 0 <= i + b...  44 us
    ppermute x6, waiting for transfers between devices, line(): lax.ppermute(block, axis, [(i, i + by) for i in range(size) if 0 <= i + b...  23.1 us
    ppermute x4, starting transfers between devices, ring(): lax.ppermute(block, axis, [(i, (i + by) % size) for i in range(size)])  13.7 us
    all_to_all x1, blocking collectives, shards(): lax.all_to_all(term, 'lon', 0, 0, axis_index_groups=chips, tiled=True)  10.4 us
    ppermute x4, waiting for transfers between devices, ring(): lax.ppermute(block, axis, [(i, (i + by) % size) for i in range(size)])  9.22 us
    all_to_all x1, starting transfers between devices, shards(): lax.all_to_all(half, 'lon', 0, 0, axis_index_groups=same_core, tiled=True)  7.21 us
    unnamed x30, local copies, waits for them, and re-layouts  5.72 us
    pallas_call x1, Pallas kernels, over_queries(): pl.pallas_call(functools.partial(query_kernel, lat_total), out_shape=(sha...  4.66 us
  transfers between devices with their start and end apart: 12, of which 4 were waited for; matrix products, arithmetic and copies ran while one was open for 0% of the time, Pallas kernels for 9%

profile of v5, /device:TPU:3, one launch (start us, length us, event | category | flops | bytes accessed | tf_op | source)
XLA Modules:
  0.0 130.6 jit_solution(2969473222020993887)
XLA Ops:
  0.7 1.0 copy-done.3
  1.7 0.9 copy-done.5
  2.7 10.6 %collective-permute-start = (bf16[6,16,1024]{2,1,0:T(8,128)(2,1)S(1)}, bf16[6,16,1024]{2,1,0:T(8,128)(2,1)S(1)}, u32[]{:S(2)}, u32[]{:S(2)}) collective-permute-start(bf16[6,16,1024]{2,1,0:T(8,128)(2,1)S(1)} %get-tuple-element.40), channel_id=1, source_target_pairs={{0,64},{64,128},{128,192},{192,256},{256,320},{320,384},{384,448},... | collective-permute-start | bytes 589832 | tf_op jit(solution)/shard_map/ppermute | solution.py:313
  13.4 1.9 %collective-permute-start.1 = (bf16[6,16,1024]{2,1,0:T(8,128)(2,1)S(1)}, bf16[6,16,1024]{2,1,0:T(8,128)(2,1)S(1)}, u32[]{:S(2)}, u32[]{:S(2)}) collective-permute-start(bf16[6,16,1024]{2,1,0:T(8,128)(2,1)S(1)} %get-tuple-element.41), channel_id=1, source_target_pairs={{64,0},{128,64},{192,128},{256,192},{320,256},{384,320},{448,384},... | collective-permute-start | bytes 589832 | tf_op jit(solution)/shard_map/ppermute | solution.py:313
  15.3 2.6 %collective-permute-done = bf16[6,16,1024]{2,1,0:T(8,128)(2,1)S(1)} collective-permute-done((bf16[6,16,1024]{2,1,0:T(8,128)(2,1)S(1)}, bf16[6,16,1024]{2,1,0:T(8,128)(2,1)S(1)}, u32[]{:S(2)}, u32[]{:S(2)}) %collective-permute-start) | collective-permute-done | bytes 196640 | tf_op jit(solution)/shard_map/ppermute | solution.py:313
  17.9 9.8 %collective-permute-done.1 = bf16[6,16,1024]{2,1,0:T(8,128)(2,1)S(1)} collective-permute-done((bf16[6,16,1024]{2,1,0:T(8,128)(2,1)S(1)}, bf16[6,16,1024]{2,1,0:T(8,128)(2,1)S(1)}, u32[]{:S(2)}, u32[]{:S(2)}) %collective-permute-start.1) | collective-permute-done | bytes 196640 | tf_op jit(solution)/shard_map/ppermute | solution.py:313
  27.7 0.1 pad_maximum_fusion.ext_ref
  27.9 6.8 %collective-permute-start.2 = (bf16[24,8,1024]{2,1,0:T(8,128)(2,1)S(1)}, bf16[24,8,1024]{2,1,0:T(8,128)(2,1)S(1)}, u32[]{:S(2)}, u32[]{:S(2)}) collective-permute-start(bf16[24,8,1024]{2,1,0:T(8,128)(2,1)S(1)} %get-tuple-element.37), channel_id=1, source_target_pairs={{0,1},{1,2},{2,3},{3,4},{4,5},{5,6},{6,7},{7,8},{8,9},{9,10},{10,1... | collective-permute-start | bytes 1179656 | tf_op jit(solution)/shard_map/ppermute | solution.py:308
  34.8 2.3 %collective-permute-start.3 = (bf16[24,8,1024]{2,1,0:T(8,128)(2,1)S(1)}, bf16[24,8,1024]{2,1,0:T(8,128)(2,1)S(1)}, u32[]{:S(2)}, u32[]{:S(2)}) collective-permute-start(bf16[24,8,1024]{2,1,0:T(8,128)(2,1)S(1)} %get-tuple-element.36), channel_id=1, source_target_pairs={{0,63},{1,0},{2,1},{3,2},{4,3},{5,4},{6,5},{7,6},{8,7},{9,8},{10,9... | collective-permute-start | bytes 1179656 | tf_op jit(solution)/shard_map/ppermute | solution.py:308
  37.1 0.5 convolution_convert_fusion
  37.6 0.4 copy-done.2
  38.2 7.3 %collective-permute-start.4 = (bf16[6,16,1024]{2,1,0:T(8,128)(2,1)S(1)}, bf16[6,16,1024]{2,1,0:T(8,128)(2,1)S(1)}, u32[]{:S(2)}, u32[]{:S(2)}) collective-permute-start(bf16[6,16,1024]{2,1,0:T(8,128)(2,1)S(1)} %get-tuple-element.39), channel_id=1, source_target_pairs={{0,64},{64,128},{128,192},{192,256},{256,320},{320,384},{384,448},... | collective-permute-start | bytes 589832 | tf_op jit(solution)/shard_map/ppermute | solution.py:313
  45.4 2.8 %collective-permute-start.5 = (bf16[6,16,1024]{2,1,0:T(8,128)(2,1)S(1)}, bf16[6,16,1024]{2,1,0:T(8,128)(2,1)S(1)}, u32[]{:S(2)}, u32[]{:S(2)}) collective-permute-start(bf16[6,16,1024]{2,1,0:T(8,128)(2,1)S(1)} %get-tuple-element.38), channel_id=1, source_target_pairs={{64,0},{128,64},{192,128},{256,192},{320,256},{384,320},{448,384},... | collective-permute-start | bytes 589832 | tf_op jit(solution)/shard_map/ppermute | solution.py:313
  48.3 4.7 %over_queries.1 = (bf16[12,16,512]{2,1,0:T(8,128)(2,1)}, bf16[12,16,128]{2,1,0:T(8,128)(2,1)S(1)}, bf16[2,32,8,1024]{3,2,1,0:T(8,128)(2,1)S(1)}) custom-call(s32[1]{0:T(128)} %bitcast.place_ref, bf16[12,16,1024]{2,1,0:T(8,128)(2,1)S(1)} %pack_qg.1.qg_ref.q_own, bf16[24,16,1024]{2,1,0:T(8,128)(2,1)S(1)} %pad_maximum_fusion.ext_ref, ...), custom_call_target="tpu_custom_call" | custom-call | flops 40000000000 | bytes 4000000 | tf_op jit(solution)/shard_map/over_queries/pallas_call | solution.py:261
  53.0 10.4 %all_to_all.15.pair_ref = bf16[2,32,8,1024]{3,2,1,0:T(8,128)(2,1)S(1)} all-to-all(bf16[2,32,8,1024]{3,2,1,0:T(8,128)(2,1)S(1)} %get-tuple-element.23), channel_id=1, replica_groups={{0,1},{2,3},{4,5},{6,7},{8,9},{10,11},{12,13},{14,15},{16,17},{18,19},{..., dimensions={0} | all-to-all | bytes 2097152 | tf_op jit(solution)/shard_map/all_to_all | solution.py:365
  63.3 0.9 fold.1
  64.3 7.2 %all-to-all-start.1 = ((bf16[32,8,1024]{2,1,0:T(8,128)(2,1)}), bf16[32,8,1024]{2,1,0:T(8,128)(2,1)S(1)}, u32[]{:S(2)}, u32[]{:S(2)}) async-start(bf16[32,8,1024]{2,1,0:T(8,128)(2,1)} %fold.1), calls=%async_computation.1 | async-start | bytes 1048576 | tf_op jit(solution)/shard_map/all_to_all | solution.py:374
  71.5 19.4 %collective-permute-start.6 = (bf16[6,16,128]{2,1,0:T(8,128)(2,1)S(1)}, bf16[6,16,128]{2,1,0:T(8,128)(2,1)S(1)}, u32[]{:S(2)}, u32[]{:S(2)}) collective-permute-start(bf16[6,16,128]{2,1,0:T(8,128)(2,1)S(1)} %get-tuple-element.43), channel_id=1, source_target_pairs={{0,64},{64,128},{128,192},{192,256},{256,320},{320,384},{384,448},... | collective-permute-start | bytes 73736 | tf_op jit(solution)/shard_map/ppermute | solution.py:313
  90.9 1.9 %collective-permute-start.7 = (bf16[6,16,128]{2,1,0:T(8,128)(2,1)S(1)}, bf16[6,16,128]{2,1,0:T(8,128)(2,1)S(1)}, u32[]{:S(2)}, u32[]{:S(2)}) collective-permute-start(bf16[6,16,128]{2,1,0:T(8,128)(2,1)S(1)} %get-tuple-element.42), channel_id=1, source_target_pairs={{64,0},{128,64},{192,128},{256,192},{320,256},{384,320},{448,384},... | collective-permute-start | bytes 73736 | tf_op jit(solution)/shard_map/ppermute | solution.py:313
  92.9 10.6 %collective-permute-done.7.s_below = bf16[6,16,128]{2,1,0:T(8,128)(2,1)S(1)} collective-permute-done((bf16[6,16,128]{2,1,0:T(8,128)(2,1)S(1)}, bf16[6,16,128]{2,1,0:T(8,128)(2,1)S(1)}, u32[]{:S(2)}, u32[]{:S(2)}) %collective-permute-start.7) | collective-permute-done | bytes 24608 | tf_op jit(solution)/shard_map/ppermute | solution.py:313
  103.5 0.8 edge.1
  104.4 1.9 %collective-permute-start.8 = (bf16[24,8,1152]{2,1,0:T(8,128)(2,1)}, bf16[24,8,1152]{2,1,0:T(8,128)(2,1)S(1)}, u32[]{:S(2)}, u32[]{:S(2)}) collective-permute-start(bf16[24,8,1152]{2,1,0:T(8,128)(2,1)} %get-tuple-element.29), channel_id=1, source_target_pairs={{0,1},{1,2},{2,3},{3,4},{4,5},{5,6},{6,7},{7,8},{8,9},{9,10},{10,1... | collective-permute-start | bytes 1327112 | tf_op jit(solution)/shard_map/ppermute | solution.py:308
  106.3 2.6 %collective-permute-start.9 = (bf16[24,8,1152]{2,1,0:T(8,128)(2,1)S(1)}, bf16[24,8,1152]{2,1,0:T(8,128)(2,1)S(1)}, u32[]{:S(2)}, u32[]{:S(2)}) collective-permute-start(bf16[24,8,1152]{2,1,0:T(8,128)(2,1)S(1)} %get-tuple-element.30), channel_id=1, source_target_pairs={{0,63},{1,0},{2,1},{3,2},{4,3},{5,4},{6,5},{7,6},{8,7},{9,8},{10,9... | collective-permute-start | bytes 1327112 | tf_op jit(solution)/shard_map/ppermute | solution.py:308
  109.0 0.7 share.1
  109.7 3.5 %all-to-all-start.2 = ((bf16[8,8,1024]{2,1,0:T(8,128)(2,1)}), bf16[8,8,1024]{2,1,0:T(8,128)(2,1)S(1)}, u32[]{:S(2)}, u32[]{:S(2)}) async-start(bf16[8,8,1024]{2,1,0:T(8,128)(2,1)} %share.1), calls=%async_computation.2 | async-start | bytes 262144 | tf_op jit(solution)/shard_map/all_to_all | solution.py:398
  113.2 9.2 %collective-permute-done.9.east_ref = bf16[24,8,1152]{2,1,0:T(8,128)(2,1)S(1)} collective-permute-done((bf16[24,8,1152]{2,1,0:T(8,128)(2,1)S(1)}, bf16[24,8,1152]{2,1,0:T(8,128)(2,1)S(1)}, u32[]{:S(2)}, u32[]{:S(2)}) %collective-permute-start.9) | collective-permute-done | bytes 442400 | tf_op jit(solution)/shard_map/ppermute | solution.py:308
  122.4 0.9 copy-done.8
  123.3 0.9 copy-done.10
  124.2 0.7 copy-done.12
  125.0 0.7 copy-done.14
  125.7 4.2 %over_keys.1 = (bf16[12,16,512]{2,1,0:T(8,128)(2,1)}, bf16[12,16,512]{2,1,0:T(8,128)(2,1)}) custom-call(s32[1]{0:T(128)} %bitcast.place_ref, bf16[12,16,512]{2,1,0:T(8,128)(2,1)S(1)} %copy-done.4, bf16[12,16,512]{2,1,0:T(8,128)(2,1)S(1)} %copy-done.6, bf16[6,16,1024]{2,1,0:T(8,128)(2,1)S(1)} %copy-done.8, bf16[12,16,1024]{2,1,0:T(8,128)(2,1)S(1)} %pack_qg.1.qg_ref.q_own, ...), custom_call_target="tpu_custom_call" | custom-call | flops 20000000000 | bytes 4000000 | tf_op jit(solution)/shard_map/over_keys/pallas_call | solution.py:287
  130.0 0.6 mean.1
  (37 shorter events, 0.3 us)
Async XLA Ops:
  0.6 36.5 %copy-start = (bf16[512,1024]{1,0:T(8,128)(2,1)S(1)}, bf16[512,1024]{1,0:T(8,128)(2,1)}, u32[]{:S(2)}) copy-start(bf16[512,1024]{1,0:T(8,128)(2,1)} %param.9) | copy-start | bytes 3145732
  0.6 1.0 copy-start.3
  1.7 0.9 copy-start.5
  2.7 15.2 %collective-permute-start = (bf16[6,16,1024]{2,1,0:T(8,128)(2,1)S(1)}, bf16[6,16,1024]{2,1,0:T(8,128)(2,1)S(1)}, u32[]{:S(2)}, u32[]{:S(2)}) collective-permute-start(bf16[6,16,1024]{2,1,0:T(8,128)(2,1)S(1)} %get-tuple-element.40), channel_id=1, source_target_pairs={{0,64},{64,128},{128,192},{192,256},{256,320},{320,384},{384,448},... | collective-permute-start | bytes 589832 | tf_op jit(solution)/shard_map/ppermute | solution.py:313
  13.4 14.4 %collective-permute-start.1 = (bf16[6,16,1024]{2,1,0:T(8,128)(2,1)S(1)}, bf16[6,16,1024]{2,1,0:T(8,128)(2,1)S(1)}, u32[]{:S(2)}, u32[]{:S(2)}) collective-permute-start(bf16[6,16,1024]{2,1,0:T(8,128)(2,1)S(1)} %get-tuple-element.41), channel_id=1, source_target_pairs={{64,0},{128,64},{192,128},{256,192},{320,256},{384,320},{448,384},... | collective-permute-start | bytes 589832 | tf_op jit(solution)/shard_map/ppermute | solution.py:313
  27.8 9.3 %copy-start.1 = (bf16[12,16,1024]{2,1,0:T(8,128)(2,1)S(1)}, bf16[12,16,1024]{2,1,0:T(8,128)(2,1)}, u32[]{:S(2)}) copy-start(bf16[12,16,1024]{2,1,0:T(8,128)(2,1)} %param.8) | copy-start | bytes 1179652
  27.9 20.4 %collective-permute-start.2 = (bf16[24,8,1024]{2,1,0:T(8,128)(2,1)S(1)}, bf16[24,8,1024]{2,1,0:T(8,128)(2,1)S(1)}, u32[]{:S(2)}, u32[]{:S(2)}) collective-permute-start(bf16[24,8,1024]{2,1,0:T(8,128)(2,1)S(1)} %get-tuple-element.37), channel_id=1, source_target_pairs={{0,1},{1,2},{2,3},{3,4},{4,5},{5,6},{6,7},{7,8},{8,9},{9,10},{10,1... | collective-permute-start | bytes 1179656 | tf_op jit(solution)/shard_map/ppermute | solution.py:308
  34.8 13.5 %collective-permute-start.3 = (bf16[24,8,1024]{2,1,0:T(8,128)(2,1)S(1)}, bf16[24,8,1024]{2,1,0:T(8,128)(2,1)S(1)}, u32[]{:S(2)}, u32[]{:S(2)}) collective-permute-start(bf16[24,8,1024]{2,1,0:T(8,128)(2,1)S(1)} %get-tuple-element.36), channel_id=1, source_target_pairs={{0,63},{1,0},{2,1},{3,2},{4,3},{5,4},{6,5},{7,6},{8,7},{9,8},{10,9... | collective-permute-start | bytes 1179656 | tf_op jit(solution)/shard_map/ppermute | solution.py:308
  37.1 0.9 copy-start.2
  38.2 54.7 %collective-permute-start.4 = (bf16[6,16,1024]{2,1,0:T(8,128)(2,1)S(1)}, bf16[6,16,1024]{2,1,0:T(8,128)(2,1)S(1)}, u32[]{:S(2)}, u32[]{:S(2)}) collective-permute-start(bf16[6,16,1024]{2,1,0:T(8,128)(2,1)S(1)} %get-tuple-element.39), channel_id=1, source_target_pairs={{0,64},{64,128},{128,192},{192,256},{256,320},{320,384},{384,448},... | collective-permute-start | bytes 589832 | tf_op jit(solution)/shard_map/ppermute | solution.py:313
  45.4 47.4 %collective-permute-start.5 = (bf16[6,16,1024]{2,1,0:T(8,128)(2,1)S(1)}, bf16[6,16,1024]{2,1,0:T(8,128)(2,1)S(1)}, u32[]{:S(2)}, u32[]{:S(2)}) collective-permute-start(bf16[6,16,1024]{2,1,0:T(8,128)(2,1)S(1)} %get-tuple-element.38), channel_id=1, source_target_pairs={{64,0},{128,64},{192,128},{256,192},{320,256},{384,320},{448,384},... | collective-permute-start | bytes 589832 | tf_op jit(solution)/shard_map/ppermute | solution.py:313
  64.3 44.7 %all-to-all-start.1 = ((bf16[32,8,1024]{2,1,0:T(8,128)(2,1)}), bf16[32,8,1024]{2,1,0:T(8,128)(2,1)S(1)}, u32[]{:S(2)}, u32[]{:S(2)}) async-start(bf16[32,8,1024]{2,1,0:T(8,128)(2,1)} %fold.1), calls=%async_computation.1 | async-start | bytes 1048576 | tf_op jit(solution)/shard_map/all_to_all | solution.py:374
  71.5 21.4 %collective-permute-start.6 = (bf16[6,16,128]{2,1,0:T(8,128)(2,1)S(1)}, bf16[6,16,128]{2,1,0:T(8,128)(2,1)S(1)}, u32[]{:S(2)}, u32[]{:S(2)}) collective-permute-start(bf16[6,16,128]{2,1,0:T(8,128)(2,1)S(1)} %get-tuple-element.43), channel_id=1, source_target_pairs={{0,64},{64,128},{128,192},{192,256},{256,320},{320,384},{384,448},... | collective-permute-start | bytes 73736 | tf_op jit(solution)/shard_map/ppermute | solution.py:313
  90.9 12.6 %collective-permute-start.7 = (bf16[6,16,128]{2,1,0:T(8,128)(2,1)S(1)}, bf16[6,16,128]{2,1,0:T(8,128)(2,1)S(1)}, u32[]{:S(2)}, u32[]{:S(2)}) collective-permute-start(bf16[6,16,128]{2,1,0:T(8,128)(2,1)S(1)} %get-tuple-element.42), channel_id=1, source_target_pairs={{64,0},{128,64},{192,128},{256,192},{320,256},{384,320},{448,384},... | collective-permute-start | bytes 73736 | tf_op jit(solution)/shard_map/ppermute | solution.py:313
  92.9 11.5 %copy-start.7 = (bf16[6,16,1024]{2,1,0:T(8,128)(2,1)}, bf16[6,16,1024]{2,1,0:T(8,128)(2,1)S(1)}, u32[]{:S(2)}) copy-start(bf16[6,16,1024]{2,1,0:T(8,128)(2,1)S(1)} %collective-permute-done.4.q_above) | copy-start | bytes 589828
  92.9 11.5 %copy-start.9 = (bf16[6,16,1024]{2,1,0:T(8,128)(2,1)}, bf16[6,16,1024]{2,1,0:T(8,128)(2,1)S(1)}, u32[]{:S(2)}) copy-start(bf16[6,16,1024]{2,1,0:T(8,128)(2,1)S(1)} %collective-permute-done.5.q_below) | copy-start | bytes 589828
  92.9 11.5 %copy-start.11 = (bf16[6,16,128]{2,1,0:T(8,128)(2,1)}, bf16[6,16,128]{2,1,0:T(8,128)(2,1)S(1)}, u32[]{:S(2)}) copy-start(bf16[6,16,128]{2,1,0:T(8,128)(2,1)S(1)} %collective-permute-done.6.s_above) | copy-start | bytes 73732
  103.5 0.9 copy-start.13
  103.5 18.8 %copy-start.6 = (bf16[12,16,512]{2,1,0:T(8,128)(2,1)S(1)}, bf16[12,16,512]{2,1,0:T(8,128)(2,1)}, u32[]{:S(2)}) copy-start(bf16[12,16,512]{2,1,0:T(8,128)(2,1)} %values_ref.3) | copy-start | bytes 589828
  104.4 8.8 %collective-permute-start.8 = (bf16[24,8,1152]{2,1,0:T(8,128)(2,1)}, bf16[24,8,1152]{2,1,0:T(8,128)(2,1)S(1)}, u32[]{:S(2)}, u32[]{:S(2)}) collective-permute-start(bf16[24,8,1152]{2,1,0:T(8,128)(2,1)} %get-tuple-element.29), channel_id=1, source_target_pairs={{0,1},{1,2},{2,3},{3,4},{4,5},{5,6},{6,7},{7,8},{8,9},{9,10},{10,1... | collective-permute-start | bytes 1327112 | tf_op jit(solution)/shard_map/ppermute | solution.py:308
  106.3 16.1 %collective-permute-start.9 = (bf16[24,8,1152]{2,1,0:T(8,128)(2,1)S(1)}, bf16[24,8,1152]{2,1,0:T(8,128)(2,1)S(1)}, u32[]{:S(2)}, u32[]{:S(2)}) collective-permute-start(bf16[24,8,1152]{2,1,0:T(8,128)(2,1)S(1)} %get-tuple-element.30), channel_id=1, source_target_pairs={{0,63},{1,0},{2,1},{3,2},{4,3},{5,4},{6,5},{7,6},{8,7},{9,8},{10,9... | collective-permute-start | bytes 1327112 | tf_op jit(solution)/shard_map/ppermute | solution.py:308
  109.7 12.7 %copy-start.4 = (bf16[12,16,512]{2,1,0:T(8,128)(2,1)S(1)}, bf16[12,16,512]{2,1,0:T(8,128)(2,1)}, u32[]{:S(2)}) copy-start(bf16[12,16,512]{2,1,0:T(8,128)(2,1)} %keys_ref.5) | copy-start | bytes 589828
  109.7 20.3 %all-to-all-start.2 = ((bf16[8,8,1024]{2,1,0:T(8,128)(2,1)}), bf16[8,8,1024]{2,1,0:T(8,128)(2,1)S(1)}, u32[]{:S(2)}, u32[]{:S(2)}) async-start(bf16[8,8,1024]{2,1,0:T(8,128)(2,1)} %share.1), calls=%async_computation.2 | async-start | bytes 262144 | tf_op jit(solution)/shard_map/all_to_all | solution.py:398
  122.4 0.9 copy-start.8
  123.3 0.9 copy-start.10
  124.2 0.7 copy-start.12
  125.0 0.7 copy-start.14

commit v6 on v3

--- a/solution.py
+++ b/solution.py
@@ -221,7 +221,7 @@
 VMEM = pl.BlockSpec(memory_space=pltpu.VMEM)
 SMEM = pl.BlockSpec(memory_space=pltpu.SMEM)
 PARAMS = pltpu.CompilerParams(vmem_limit_bytes=20 << 20)
-FOLD, RIM, FINISH = 6_000_000_000, 6_000_000_000, 6_000_000_000
+FOLD, RIM, FINISH = 1_000_000, 1_000_000, 3_000_000_000
 SMALL = pltpu.CompilerParams(vmem_limit_bytes=8 << 20)
 
 
@@ -346,7 +346,7 @@
     )(keep, got)
     same_core = [[2 * i + c for i in range(lon // 2)] for c in range(2)]
     terms = lax.all_to_all(half, "lon", 0, 0, axis_index_groups=same_core, tiled=True)
-    from_west, from_east, _ = lax.optimization_barrier((from_west, from_east, half))
+    rim, _ = lax.optimization_barrier((rim, half))
     top, bottom = pl.pallas_call(
         rim_kernel,
         out_shape=(shape((RADIUS, cols, 2 * inner)),) * 2,
@@ -364,7 +364,7 @@
         name="share",
     )(terms)
     every = lax.all_to_all(copies, "lat", 0, 0, tiled=True)
-    from_above, from_below, _ = lax.optimization_barrier((from_above, from_below, copies))
+    mid, _ = lax.optimization_barrier((mid, copies))
     grad_key, grad_value = pl.pallas_call(
         finish_kernel,
         out_shape=(shape((rows, cols, inner)),) * 2,

time: 130 us -> 125 us (0.962)
  starting transfers between devices: 67 us -> 62.9 us
  local copies, waits for them, and re-layouts: 5.44 us -> 2.95 us
  waiting for transfers between devices: 42.8 us -> 44.3 us
    all_to_all x1, waiting for transfers between devices: 14.4 us -> 0.01 us  [shards(): lax.all_to_all(half, 'lon', 0, 0, axis_index_groups=same_core, tiled=True)]
    ppermute x4, waiting for transfers between devices: 10.8 us -> 23 us  [ring(): lax.ppermute(block, axis, [(i, (i + by) % size) for i in range(size)])]
    all_to_all x1, starting transfers between devices: 17.4 us -> 9.87 us  [shards(): every = lax.all_to_all(copies, 'lat', 0, 0, tiled=True)]
    all_to_all x1, waiting for transfers between devices: 7.52 us -> 10.5 us  [shards(): every = lax.all_to_all(copies, 'lat', 0, 0, tiled=True)]
    unnamed x18 -> x16, local copies, waits for them, and re-layouts: 4.47 us -> 1.97 us
    all_to_all x1, starting transfers between devices: 5.64 us -> 7.88 us  [shards(): lax.all_to_all(half, 'lon', 0, 0, axis_index_groups=same_core, tiled=True)]
  transfers between devices with their start and end apart: 11 -> 11, of which waited for: 6 -> 7; matrix products, arithmetic and copies ran while one was open for 0% -> 0% of each run, Pallas kernels for 6% -> 6%
where the time goes in v6:
time: 125 us; the launch traced here: 124 us
  starting transfers between devices  62.9 us (50%)
  waiting for transfers between devices  44.3 us (35%)
  Pallas kernels  12.3 us (10%)
  local copies, waits for them, and re-layouts  2.95 us (2%)
    ppermute x4, starting transfers between devices, line(): lax.ppermute(block, axis, [(i, i + by) for i in range(size) if 0 <= i + b...  25.6 us
    ppermute x4, waiting for transfers between devices, ring(): lax.ppermute(block, axis, [(i, (i + by) % size) for i in range(size)])  23 us
    ppermute x4, starting transfers between devices, ring(): lax.ppermute(block, axis, [(i, (i + by) % size) for i in range(size)])  17.6 us
    ppermute x4, waiting for transfers between devices, line(): lax.ppermute(block, axis, [(i, i + by) for i in range(size) if 0 <= i + b...  10.7 us
    all_to_all x1, waiting for transfers between devices, shards(): every = lax.all_to_all(copies, 'lat', 0, 0, tiled=True)  10.5 us
    all_to_all x1, starting transfers between devices, shards(): every = lax.all_to_all(copies, 'lat', 0, 0, tiled=True)  9.87 us
    all_to_all x1, starting transfers between devices, shards(): lax.all_to_all(half, 'lon', 0, 0, axis_index_groups=same_core, tiled=True)  7.88 us
    pallas_call x1, Pallas kernels, backward(): pl.pallas_call(functools.partial(backward_kernel, lat_total), out_shape=(...  5.51 us
  transfers between devices with their start and end apart: 11, of which 7 were waited for; matrix products, arithmetic and copies ran while one was open for 0% of the time, Pallas kernels for 6%

profile of v6, /device:TPU:6, one launch (start us, length us, event | category | flops | bytes accessed | tf_op | source)
XLA Modules:
  0.0 124.0 jit_solution(13297516125014703369)
XLA Ops:
  0.7 1.0 copy-done.2
  1.7 0.9 copy-done.3
  2.6 0.1 pack.1
  2.7 10.9 %collective-permute-start = (bf16[6,16,1024]{2,1,0:T(8,128)(2,1)S(1)}, bf16[6,16,1024]{2,1,0:T(8,128)(2,1)S(1)}, u32[]{:S(2)}, u32[]{:S(2)}) collective-permute-start(bf16[6,16,1024]{2,1,0:T(8,128)(2,1)S(1)} %get-tuple-element.48), channel_id=1, source_target_pairs={{0,64},{64,128},{128,192},{192,256},{256,320},{320,384},{384,448},... | collective-permute-start | bytes 589832 | tf_op jit(solution)/shard_map/ppermute | solution.py:292
  13.6 2.3 %collective-permute-start.1 = (bf16[6,16,1024]{2,1,0:T(8,128)(2,1)S(1)}, bf16[6,16,1024]{2,1,0:T(8,128)(2,1)S(1)}, u32[]{:S(2)}, u32[]{:S(2)}) collective-permute-start(bf16[6,16,1024]{2,1,0:T(8,128)(2,1)S(1)} %get-tuple-element.49), channel_id=1, source_target_pairs={{64,0},{128,64},{192,128},{256,192},{320,256},{384,320},{448,384},... | collective-permute-start | bytes 589832 | tf_op jit(solution)/shard_map/ppermute | solution.py:292
  16.0 2.9 %collective-permute-done = bf16[6,16,1024]{2,1,0:T(8,128)(2,1)S(1)} collective-permute-done((bf16[6,16,1024]{2,1,0:T(8,128)(2,1)S(1)}, bf16[6,16,1024]{2,1,0:T(8,128)(2,1)S(1)}, u32[]{:S(2)}, u32[]{:S(2)}) %collective-permute-start) | collective-permute-done | bytes 196640 | tf_op jit(solution)/shard_map/ppermute | solution.py:292
  18.9 7.1 %collective-permute-done.1 = bf16[6,16,1024]{2,1,0:T(8,128)(2,1)S(1)} collective-permute-done((bf16[6,16,1024]{2,1,0:T(8,128)(2,1)S(1)}, bf16[6,16,1024]{2,1,0:T(8,128)(2,1)S(1)}, u32[]{:S(2)}, u32[]{:S(2)}) %collective-permute-start.1) | collective-permute-done | bytes 196640 | tf_op jit(solution)/shard_map/ppermute | solution.py:292
  26.0 0.1 pad_maximum_fusion.ext_ref
  26.1 0.9 fusion
  27.1 6.2 %collective-permute-start.3 = (bf16[24,8,1024]{2,1,0:T(8,128)(2,1)}, bf16[24,8,1024]{2,1,0:T(8,128)(2,1)S(1)}, u32[]{:S(2)}, u32[]{:S(2)}) collective-permute-start(bf16[24,8,1024]{2,1,0:T(8,128)(2,1)} %get-tuple-element.46), channel_id=1, source_target_pairs={{0,63},{1,0},{2,1},{3,2},{4,3},{5,4},{6,5},{7,6},{8,7},{9,8},{10,9... | collective-permute-start | bytes 1179656 | tf_op jit(solution)/shard_map/ppermute | solution.py:287
  33.3 1.9 %collective-permute-start.2 = (bf16[24,8,1024]{2,1,0:T(8,128)(2,1)}, bf16[24,8,1024]{2,1,0:T(8,128)(2,1)S(1)}, u32[]{:S(2)}, u32[]{:S(2)}) collective-permute-start(bf16[24,8,1024]{2,1,0:T(8,128)(2,1)} %get-tuple-element.47), channel_id=1, source_target_pairs={{0,1},{1,2},{2,3},{3,4},{4,5},{5,6},{6,7},{7,8},{8,9},{9,10},{10,1... | collective-permute-start | bytes 1179656 | tf_op jit(solution)/shard_map/ppermute | solution.py:287
  35.3 0.1 pad_add_fusion.place_ref
  35.4 0.5 convolution_convert_fusion
  35.9 3.0 %collective-permute-done.3.east_ref = bf16[24,8,1024]{2,1,0:T(8,128)(2,1)S(1)} collective-permute-done((bf16[24,8,1024]{2,1,0:T(8,128)(2,1)}, bf16[24,8,1024]{2,1,0:T(8,128)(2,1)S(1)}, u32[]{:S(2)}, u32[]{:S(2)}) %collective-permute-start.3) | collective-permute-done | bytes 393248 | tf_op jit(solution)/shard_map/ppermute | solution.py:287
  38.9 7.7 %collective-permute-done.2.west_ref = bf16[24,8,1024]{2,1,0:T(8,128)(2,1)S(1)} collective-permute-done((bf16[24,8,1024]{2,1,0:T(8,128)(2,1)}, bf16[24,8,1024]{2,1,0:T(8,128)(2,1)S(1)}, u32[]{:S(2)}, u32[]{:S(2)}) %collective-permute-start.2) | collective-permute-done | bytes 393248 | tf_op jit(solution)/shard_map/ppermute | solution.py:287
  46.7 3.5 %forward.1 = (bf16[24,32,1024]{2,1,0:T(8,128)(2,1)S(1)}, f32[8,256]{1,0:T(8,128)S(1)}, f32[32,8,1024]{2,1,0:T(8,128)S(1)}, bf16[32,8,1024]{2,1,0:T(8,128)(2,1)S(1)}) custom-call(s32[2]{0:T(128)S(1)} %pad_add_fusion.place_ref, bf16[12,16,512]{2,1,0:T(8,128)(2,1)S(1)} %copy-done.4, bf16[24,16,1024]{2,1,0:T(8,128)(2,1)S(1)} %pad_maximum_fusion.ext_ref, ...), custom_call_target="tpu_custom_call" | custom-call | flops 1000000000 | bytes 5000000 | tf_op jit(solution)/shard_map/forward/pallas_call | solution.py:236
  50.2 1.9 %collective-permute-start.4 = (bf16[32,8,1024]{2,1,0:T(8,128)(2,1)S(1)}, bf16[32,8,1024]{2,1,0:T(8,128)(2,1)S(1)}, u32[]{:S(2)}, u32[]{:S(2)}) collective-permute-start(bf16[32,8,1024]{2,1,0:T(8,128)(2,1)S(1)} %get-tuple-element.35), channel_id=1, source_target_pairs={{0,1},{1,0},{2,3},{3,2},{4,5},{5,4},{6,7},{7,6},{8,9},{9,8},{10,11... | collective-permute-start | bytes 1572872 | tf_op jit(solution)/shard_map/ppermute | solution.py:333
  52.2 5.5 %backward.1 = (bf16[12,16,512]{2,1,0:T(8,128)(2,1)}, bf16[12,16,1024]{2,1,0:T(8,128)(2,1)S(1)}, bf16[12,16,1024]{2,1,0:T(8,128)(2,1)S(1)}, bf16[24,8,1024]{2,1,0:T(8,128)(2,1)S(1)}, bf16[24,8,1024]{2,1,0:T(8,128)(2,1)S(1)}) custom-call(s32[2]{0:T(128)S(1)} %pad_add_fusion.place_ref, bf16[12,16,512]{2,1,0:T(8,128)(2,1)S(1)} %copy-done.5, ...), custom_call_target="tpu_custom_call" | custom-call | flops 20000000000 | bytes 70000000 | tf_op jit(solution)/shard_map/backward/pallas_call | solution.py:261
  57.7 0.9 fold.1
  58.6 7.9 %all-to-all-start = ((bf16[32,8,1024]{2,1,0:T(8,128)(2,1)}), bf16[32,8,1024]{2,1,0:T(8,128)(2,1)S(1)}, u32[]{:S(2)}, u32[]{:S(2)}) async-start(bf16[32,8,1024]{2,1,0:T(8,128)(2,1)} %fold.1), calls=%async_computation | async-start | bytes 1048576 | tf_op jit(solution)/shard_map/all_to_all | solution.py:348
  66.5 1.9 %collective-permute-start.5 = (bf16[24,8,1024]{2,1,0:T(8,128)(2,1)S(1)}, bf16[24,8,1024]{2,1,0:T(8,128)(2,1)S(1)}, u32[]{:S(2)}, u32[]{:S(2)}) collective-permute-start(bf16[24,8,1024]{2,1,0:T(8,128)(2,1)S(1)} %get-tuple-element.38), channel_id=1, source_target_pairs={{0,1},{1,2},{2,3},{3,4},{4,5},{5,6},{6,7},{7,8},{8,9},{9,10},{10,1... | collective-permute-start | bytes 1179656 | tf_op jit(solution)/shard_map/ppermute | solution.py:287
  68.4 7.5 %collective-permute-start.6 = (bf16[24,8,1024]{2,1,0:T(8,128)(2,1)S(1)}, bf16[24,8,1024]{2,1,0:T(8,128)(2,1)S(1)}, u32[]{:S(2)}, u32[]{:S(2)}) collective-permute-start(bf16[24,8,1024]{2,1,0:T(8,128)(2,1)S(1)} %get-tuple-element.39), channel_id=1, source_target_pairs={{0,63},{1,0},{2,1},{3,2},{4,3},{5,4},{6,5},{7,6},{8,7},{9,8},{10,9... | collective-permute-start | bytes 1179656 | tf_op jit(solution)/shard_map/ppermute | solution.py:287
  76.0 12.3 %collective-permute-done.5.west_ref = bf16[24,8,1024]{2,1,0:T(8,128)(2,1)S(1)} collective-permute-done((bf16[24,8,1024]{2,1,0:T(8,128)(2,1)S(1)}, bf16[24,8,1024]{2,1,0:T(8,128)(2,1)S(1)}, u32[]{:S(2)}, u32[]{:S(2)}) %collective-permute-start.5) | collective-permute-done | bytes 393248 | tf_op jit(solution)/shard_map/ppermute | solution.py:287
  88.3 0.1 rim.1
  88.3 3.4 %collective-permute-start.7 = (bf16[6,16,1024]{2,1,0:T(8,128)(2,1)S(1)}, bf16[6,16,1024]{2,1,0:T(8,128)(2,1)S(1)}, u32[]{:S(2)}, u32[]{:S(2)}) collective-permute-start(bf16[6,16,1024]{2,1,0:T(8,128)(2,1)S(1)} %get-tuple-element.43), channel_id=1, source_target_pairs={{0,64},{64,128},{128,192},{192,256},{256,320},{320,384},{384,448},... | collective-permute-start | bytes 589832 | tf_op jit(solution)/shard_map/ppermute | solution.py:292
  91.8 9.0 %collective-permute-start.8 = (bf16[6,16,1024]{2,1,0:T(8,128)(2,1)S(1)}, bf16[6,16,1024]{2,1,0:T(8,128)(2,1)S(1)}, u32[]{:S(2)}, u32[]{:S(2)}) collective-permute-start(bf16[6,16,1024]{2,1,0:T(8,128)(2,1)S(1)} %get-tuple-element.40), channel_id=1, source_target_pairs={{64,0},{128,64},{192,128},{256,192},{320,256},{384,320},{448,384},... | collective-permute-start | bytes 589832 | tf_op jit(solution)/shard_map/ppermute | solution.py:292
  100.7 0.7 share.1
  101.5 9.9 %all-to-all-start.1 = ((bf16[8,8,1024]{2,1,0:T(8,128)(2,1)}), bf16[8,8,1024]{2,1,0:T(8,128)(2,1)S(1)}, u32[]{:S(2)}, u32[]{:S(2)}) async-start(bf16[8,8,1024]{2,1,0:T(8,128)(2,1)} %share.1), calls=%async_computation.1 | async-start | bytes 262144 | tf_op jit(solution)/shard_map/all_to_all | solution.py:366
  111.4 0.7 collective-permute-done.8.below_ref
  112.0 0.8 finish.1
  112.8 10.5 %all-to-all-done.1.terms_ref = bf16[8,8,1024]{2,1,0:T(8,128)(2,1)S(1)} async-done(((bf16[8,8,1024]{2,1,0:T(8,128)(2,1)}), bf16[8,8,1024]{2,1,0:T(8,128)(2,1)S(1)}, u32[]{:S(2)}, u32[]{:S(2)}) %all-to-all-start.1) | async-done | bytes 131104 | tf_op jit(solution)/shard_map/all_to_all | solution.py:366
  123.3 0.6 mean.1
  (19 shorter events, 0.1 us)
Async XLA Ops:
  0.6 34.7 %copy-start = (bf16[512,1024]{1,0:T(8,128)(2,1)S(1)}, bf16[512,1024]{1,0:T(8,128)(2,1)}, u32[]{:S(2)}) copy-start(bf16[512,1024]{1,0:T(8,128)(2,1)} %param.9) | copy-start | bytes 3145732
  0.6 1.0 copy-start.2
  1.7 0.9 copy-start.3
  2.7 16.2 %collective-permute-start = (bf16[6,16,1024]{2,1,0:T(8,128)(2,1)S(1)}, bf16[6,16,1024]{2,1,0:T(8,128)(2,1)S(1)}, u32[]{:S(2)}, u32[]{:S(2)}) collective-permute-start(bf16[6,16,1024]{2,1,0:T(8,128)(2,1)S(1)} %get-tuple-element.48), channel_id=1, source_target_pairs={{0,64},{64,128},{128,192},{192,256},{256,320},{320,384},{384,448},... | collective-permute-start | bytes 589832 | tf_op jit(solution)/shard_map/ppermute | solution.py:292
  13.6 21.7 %copy-start.1 = (bf16[12,16,1024]{2,1,0:T(8,128)(2,1)S(1)}, bf16[12,16,1024]{2,1,0:T(8,128)(2,1)}, u32[]{:S(2)}) copy-start(bf16[12,16,1024]{2,1,0:T(8,128)(2,1)} %param.8) | copy-start | bytes 1179652
  13.6 12.4 %collective-permute-start.1 = (bf16[6,16,1024]{2,1,0:T(8,128)(2,1)S(1)}, bf16[6,16,1024]{2,1,0:T(8,128)(2,1)S(1)}, u32[]{:S(2)}, u32[]{:S(2)}) collective-permute-start(bf16[6,16,1024]{2,1,0:T(8,128)(2,1)S(1)} %get-tuple-element.49), channel_id=1, source_target_pairs={{64,0},{128,64},{192,128},{256,192},{320,256},{384,320},{448,384},... | collective-permute-start | bytes 589832 | tf_op jit(solution)/shard_map/ppermute | solution.py:292
  26.1 20.5 %copy-start.4 = (bf16[12,16,512]{2,1,0:T(8,128)(2,1)S(1)}, bf16[12,16,512]{2,1,0:T(8,128)(2,1)}, u32[]{:S(2)}) copy-start(bf16[12,16,512]{2,1,0:T(8,128)(2,1)} %q_ref.3) | copy-start | bytes 589828
  27.1 11.8 %collective-permute-start.3 = (bf16[24,8,1024]{2,1,0:T(8,128)(2,1)}, bf16[24,8,1024]{2,1,0:T(8,128)(2,1)S(1)}, u32[]{:S(2)}, u32[]{:S(2)}) collective-permute-start(bf16[24,8,1024]{2,1,0:T(8,128)(2,1)} %get-tuple-element.46), channel_id=1, source_target_pairs={{0,63},{1,0},{2,1},{3,2},{4,3},{5,4},{6,5},{7,6},{8,7},{9,8},{10,9... | collective-permute-start | bytes 1179656 | tf_op jit(solution)/shard_map/ppermute | solution.py:287
  33.3 13.3 %collective-permute-start.2 = (bf16[24,8,1024]{2,1,0:T(8,128)(2,1)}, bf16[24,8,1024]{2,1,0:T(8,128)(2,1)S(1)}, u32[]{:S(2)}, u32[]{:S(2)}) collective-permute-start(bf16[24,8,1024]{2,1,0:T(8,128)(2,1)} %get-tuple-element.47), channel_id=1, source_target_pairs={{0,1},{1,2},{2,3},{3,4},{4,5},{5,6},{6,7},{7,8},{8,9},{9,10},{10,1... | collective-permute-start | bytes 1179656 | tf_op jit(solution)/shard_map/ppermute | solution.py:287
  35.9 16.3 %copy-start.5 = (bf16[12,16,512]{2,1,0:T(8,128)(2,1)S(1)}, bf16[12,16,512]{2,1,0:T(8,128)(2,1)}, u32[]{:S(2)}) copy-start(bf16[12,16,512]{2,1,0:T(8,128)(2,1)} %q_ref.3) | copy-start | bytes 589828
  50.2 7.5 %collective-permute-start.4 = (bf16[32,8,1024]{2,1,0:T(8,128)(2,1)S(1)}, bf16[32,8,1024]{2,1,0:T(8,128)(2,1)S(1)}, u32[]{:S(2)}, u32[]{:S(2)}) collective-permute-start(bf16[32,8,1024]{2,1,0:T(8,128)(2,1)S(1)} %get-tuple-element.35), channel_id=1, source_target_pairs={{0,1},{1,0},{2,3},{3,2},{4,5},{5,4},{6,7},{7,6},{8,9},{9,8},{10,11... | collective-permute-start | bytes 1572872 | tf_op jit(solution)/shard_map/ppermute | solution.py:333
  57.7 0.9 copy-start.6
  58.6 42.1 %all-to-all-start = ((bf16[32,8,1024]{2,1,0:T(8,128)(2,1)}), bf16[32,8,1024]{2,1,0:T(8,128)(2,1)S(1)}, u32[]{:S(2)}, u32[]{:S(2)}) async-start(bf16[32,8,1024]{2,1,0:T(8,128)(2,1)} %fold.1), calls=%async_computation | async-start | bytes 1048576 | tf_op jit(solution)/shard_map/all_to_all | solution.py:348
  66.5 21.7 %collective-permute-start.5 = (bf16[24,8,1024]{2,1,0:T(8,128)(2,1)S(1)}, bf16[24,8,1024]{2,1,0:T(8,128)(2,1)S(1)}, u32[]{:S(2)}, u32[]{:S(2)}) collective-permute-start(bf16[24,8,1024]{2,1,0:T(8,128)(2,1)S(1)} %get-tuple-element.38), channel_id=1, source_target_pairs={{0,1},{1,2},{2,3},{3,4},{4,5},{5,6},{6,7},{7,8},{8,9},{9,10},{10,1... | collective-permute-start | bytes 1179656 | tf_op jit(solution)/shard_map/ppermute | solution.py:287
  68.4 19.8 %collective-permute-start.6 = (bf16[24,8,1024]{2,1,0:T(8,128)(2,1)S(1)}, bf16[24,8,1024]{2,1,0:T(8,128)(2,1)S(1)}, u32[]{:S(2)}, u32[]{:S(2)}) collective-permute-start(bf16[24,8,1024]{2,1,0:T(8,128)(2,1)S(1)} %get-tuple-element.39), channel_id=1, source_target_pairs={{0,63},{1,0},{2,1},{3,2},{4,3},{5,4},{6,5},{7,6},{8,7},{9,8},{10,9... | collective-permute-start | bytes 1179656 | tf_op jit(solution)/shard_map/ppermute | solution.py:287
  88.2 23.8 %copy-start.7 = (bf16[12,16,1024]{2,1,0:T(8,128)(2,1)S(1)}, bf16[12,16,1024]{2,1,0:T(8,128)(2,1)}, u32[]{:S(2)}) copy-start(bf16[12,16,1024]{2,1,0:T(8,128)(2,1)} %copy-done.6) | copy-start | bytes 1179652
  88.3 23.0 %collective-permute-start.7 = (bf16[6,16,1024]{2,1,0:T(8,128)(2,1)S(1)}, bf16[6,16,1024]{2,1,0:T(8,128)(2,1)S(1)}, u32[]{:S(2)}, u32[]{:S(2)}) collective-permute-start(bf16[6,16,1024]{2,1,0:T(8,128)(2,1)S(1)} %get-tuple-element.43), channel_id=1, source_target_pairs={{0,64},{64,128},{128,192},{192,256},{256,320},{320,384},{384,448},... | collective-permute-start | bytes 589832 | tf_op jit(solution)/shard_map/ppermute | solution.py:292
  91.8 20.2 %collective-permute-start.8 = (bf16[6,16,1024]{2,1,0:T(8,128)(2,1)S(1)}, bf16[6,16,1024]{2,1,0:T(8,128)(2,1)S(1)}, u32[]{:S(2)}, u32[]{:S(2)}) collective-permute-start(bf16[6,16,1024]{2,1,0:T(8,128)(2,1)S(1)} %get-tuple-element.40), channel_id=1, source_target_pairs={{64,0},{128,64},{192,128},{256,192},{320,256},{384,320},{448,384},... | collective-permute-start | bytes 589832 | tf_op jit(solution)/shard_map/ppermute | solution.py:292
  101.5 21.8 %all-to-all-start.1 = ((bf16[8,8,1024]{2,1,0:T(8,128)(2,1)}), bf16[8,8,1024]{2,1,0:T(8,128)(2,1)S(1)}, u32[]{:S(2)}, u32[]{:S(2)}) async-start(bf16[8,8,1024]{2,1,0:T(8,128)(2,1)} %share.1), calls=%async_computation.1 | async-start | bytes 262144 | tf_op jit(solution)/shard_map/all_to_all | solution.py:366

commit v7 on v6

--- a/solution.py
+++ b/solution.py
@@ -183,6 +183,10 @@
     half_ref[...] = (keep_ref[...] + got_ref[...].astype(jnp.float32)).astype(jnp.bfloat16)
 
 
+def sum_kernel(terms_ref, out_ref):
+    out_ref[...] = jnp.sum(terms_ref[...].astype(jnp.float32), axis=0).astype(jnp.bfloat16)
+
+
 def mean_kernel(parts, terms_ref, out_ref):
     out_ref[...] = jnp.sum(terms_ref[...].astype(jnp.float32), axis=0) / parts
 
@@ -344,8 +348,15 @@
         cost_estimate=cost(FOLD),
         name="fold",
     )(keep, got)
-    same_core = [[2 * i + c for i in range(lon // 2)] for c in range(2)]
-    terms = lax.all_to_all(half, "lon", 0, 0, axis_index_groups=same_core, tiled=True)
+    near, step = 4, 8
+    far = lon // step
+    far_groups = [[j + step * i for i in range(far)] for j in range(step)]
+    near_groups = [
+        [step * f + 2 * n + c for n in range(near)] for f in range(far) for c in range(2)
+    ]
+    spread_far = lax.all_to_all(
+        half.reshape(far, near * out_rows, model), "lon", 0, 0, axis_index_groups=far_groups, tiled=True
+    )
     rim, _ = lax.optimization_barrier((rim, half))
     top, bottom = pl.pallas_call(
         rim_kernel,
@@ -354,9 +365,19 @@
         cost_estimate=cost(RIM),
         name="rim",
     )(rim, from_west, from_east)
+    spread_far, _ = lax.optimization_barrier((spread_far, top))
+    quarter = pl.pallas_call(
+        sum_kernel,
+        out_shape=shape((near * out_rows, model)),
+        compiler_params=SMALL,
+        name="sum_far",
+    )(spread_far)
+    terms = lax.all_to_all(
+        quarter.reshape(near, out_rows, model), "lon", 0, 0, axis_index_groups=near_groups, tiled=True
+    )
+    top, bottom, terms = lax.optimization_barrier((top, bottom, terms))
     from_below = line(top, "lat", -1)
     from_above = line(bottom, "lat", 1)
-    terms, _ = lax.optimization_barrier((terms, top))
     copies = pl.pallas_call(
         share_kernel,
         out_shape=shape((lat, out_rows, model)),

time: 125 us -> 127 us (1.016)
  blocking collectives: 0 us -> 8.11 us
  waiting for transfers between devices: 44.3 us -> 40.8 us
  starting transfers between devices: 62.9 us -> 60.3 us
    all_to_all x0 -> x1, blocking collectives: none -> 8.11 us  [shards(): lax.all_to_all(quarter.reshape(near, out_rows, model), 'lon', 0, 0, axis_...]
    all_to_all x1, starting transfers between devices: 7.88 us -> 5.25 us  [shards(): lax.all_to_all(half.reshape(far, near * out_rows, model), 'lon', 0, 0, ax...]
    all_to_all x1, waiting for transfers between devices: 10.5 us -> 8.22 us  [shards(): every = lax.all_to_all(copies, 'lat', 0, 0, tiled=True)]
  transfers between devices with their start and end apart: 11 -> 11, of which waited for: 7 -> 6; matrix products, arithmetic and copies ran while one was open for 0% -> 0% of each run, Pallas kernels for 6% -> 6%
where the time goes in v7:
time: 127 us; the launch traced here: 126 us
  starting transfers between devices  60.3 us (47%)
  waiting for transfers between devices  40.8 us (32%)
  Pallas kernels  12.3 us (10%)
  blocking collectives  8.11 us (6%)
  local copies, waits for them, and re-layouts  2.95 us (2%)
    ppermute x4, starting transfers between devices, line(): lax.ppermute(block, axis, [(i, i + by) for i in range(size) if 0 <= i + b...  25.7 us
    ppermute x4, waiting for transfers between devices, ring(): lax.ppermute(block, axis, [(i, (i + by) % size) for i in range(size)])  22.5 us
    ppermute x4, starting transfers between devices, ring(): lax.ppermute(block, axis, [(i, (i + by) % size) for i in range(size)])  17.6 us
    ppermute x4, waiting for transfers between devices, line(): lax.ppermute(block, axis, [(i, i + by) for i in range(size) if 0 <= i + b...  10.1 us
    all_to_all x1, starting transfers between devices, shards(): every = lax.all_to_all(copies, 'lat', 0, 0, tiled=True)  9.87 us
    all_to_all x1, waiting for transfers between devices, shards(): every = lax.all_to_all(copies, 'lat', 0, 0, tiled=True)  8.22 us
    all_to_all x1, blocking collectives, shards(): lax.all_to_all(quarter.reshape(near, out_rows, model), 'lon', 0, 0, axis_...  8.11 us
    pallas_call x1, Pallas kernels, backward(): pl.pallas_call(functools.partial(backward_kernel, lat_total), out_shape=(...  5.51 us
  transfers between devices with their start and end apart: 11, of which 6 were waited for; matrix products, arithmetic and copies ran while one was open for 0% of the time, Pallas kernels for 6%

profile of v7, /device:TPU:6, one launch (start us, length us, event | category | flops | bytes accessed | tf_op | source)
XLA Modules:
  0.0 126.0 jit_solution(4277851370440408261)
XLA Ops:
  0.7 1.0 copy-done.2
  1.7 0.9 copy-done.3
  2.7 10.9 %collective-permute-start = (bf16[6,16,1024]{2,1,0:T(8,128)(2,1)S(1)}, bf16[6,16,1024]{2,1,0:T(8,128)(2,1)S(1)}, u32[]{:S(2)}, u32[]{:S(2)}) collective-permute-start(bf16[6,16,1024]{2,1,0:T(8,128)(2,1)S(1)} %get-tuple-element.54), channel_id=1, source_target_pairs={{0,64},{64,128},{128,192},{192,256},{256,320},{320,384},{384,448},... | collective-permute-start | bytes 589832 | tf_op jit(solution)/shard_map/ppermute | solution.py:296
  13.6 2.3 %collective-permute-start.1 = (bf16[6,16,1024]{2,1,0:T(8,128)(2,1)S(1)}, bf16[6,16,1024]{2,1,0:T(8,128)(2,1)S(1)}, u32[]{:S(2)}, u32[]{:S(2)}) collective-permute-start(bf16[6,16,1024]{2,1,0:T(8,128)(2,1)S(1)} %get-tuple-element.55), channel_id=1, source_target_pairs={{64,0},{128,64},{192,128},{256,192},{320,256},{384,320},{448,384},... | collective-permute-start | bytes 589832 | tf_op jit(solution)/shard_map/ppermute | solution.py:296
  16.0 2.9 %collective-permute-done = bf16[6,16,1024]{2,1,0:T(8,128)(2,1)S(1)} collective-permute-done((bf16[6,16,1024]{2,1,0:T(8,128)(2,1)S(1)}, bf16[6,16,1024]{2,1,0:T(8,128)(2,1)S(1)}, u32[]{:S(2)}, u32[]{:S(2)}) %collective-permute-start) | collective-permute-done | bytes 196640 | tf_op jit(solution)/shard_map/ppermute | solution.py:296
  18.9 7.1 %collective-permute-done.1 = bf16[6,16,1024]{2,1,0:T(8,128)(2,1)S(1)} collective-permute-done((bf16[6,16,1024]{2,1,0:T(8,128)(2,1)S(1)}, bf16[6,16,1024]{2,1,0:T(8,128)(2,1)S(1)}, u32[]{:S(2)}, u32[]{:S(2)}) %collective-permute-start.1) | collective-permute-done | bytes 196640 | tf_op jit(solution)/shard_map/ppermute | solution.py:296
  26.0 0.1 pad_maximum_fusion.ext_ref
  26.1 0.9 fusion
  27.1 6.2 %collective-permute-start.3 = (bf16[24,8,1024]{2,1,0:T(8,128)(2,1)}, bf16[24,8,1024]{2,1,0:T(8,128)(2,1)S(1)}, u32[]{:S(2)}, u32[]{:S(2)}) collective-permute-start(bf16[24,8,1024]{2,1,0:T(8,128)(2,1)} %get-tuple-element.52), channel_id=1, source_target_pairs={{0,63},{1,0},{2,1},{3,2},{4,3},{5,4},{6,5},{7,6},{8,7},{9,8},{10,9... | collective-permute-start | bytes 1179656 | tf_op jit(solution)/shard_map/ppermute | solution.py:291
  33.3 1.9 %collective-permute-start.2 = (bf16[24,8,1024]{2,1,0:T(8,128)(2,1)}, bf16[24,8,1024]{2,1,0:T(8,128)(2,1)S(1)}, u32[]{:S(2)}, u32[]{:S(2)}) collective-permute-start(bf16[24,8,1024]{2,1,0:T(8,128)(2,1)} %get-tuple-element.53), channel_id=1, source_target_pairs={{0,1},{1,2},{2,3},{3,4},{4,5},{5,6},{6,7},{7,8},{8,9},{9,10},{10,1... | collective-permute-start | bytes 1179656 | tf_op jit(solution)/shard_map/ppermute | solution.py:291
  35.3 0.1 pad_add_fusion.place_ref
  35.4 0.5 convolution_convert_fusion
  35.9 3.0 %collective-permute-done.3.east_ref = bf16[24,8,1024]{2,1,0:T(8,128)(2,1)S(1)} collective-permute-done((bf16[24,8,1024]{2,1,0:T(8,128)(2,1)}, bf16[24,8,1024]{2,1,0:T(8,128)(2,1)S(1)}, u32[]{:S(2)}, u32[]{:S(2)}) %collective-permute-start.3) | collective-permute-done | bytes 393248 | tf_op jit(solution)/shard_map/ppermute | solution.py:291
  38.9 7.7 %collective-permute-done.2.west_ref = bf16[24,8,1024]{2,1,0:T(8,128)(2,1)S(1)} collective-permute-done((bf16[24,8,1024]{2,1,0:T(8,128)(2,1)}, bf16[24,8,1024]{2,1,0:T(8,128)(2,1)S(1)}, u32[]{:S(2)}, u32[]{:S(2)}) %collective-permute-start.2) | collective-permute-done | bytes 393248 | tf_op jit(solution)/shard_map/ppermute | solution.py:291
  46.7 3.5 %forward.1 = (bf16[24,32,1024]{2,1,0:T(8,128)(2,1)S(1)}, f32[8,256]{1,0:T(8,128)S(1)}, f32[32,8,1024]{2,1,0:T(8,128)S(1)}, bf16[32,8,1024]{2,1,0:T(8,128)(2,1)S(1)}) custom-call(s32[2]{0:T(128)S(1)} %pad_add_fusion.place_ref, bf16[12,16,512]{2,1,0:T(8,128)(2,1)S(1)} %copy-done.4, bf16[24,16,1024]{2,1,0:T(8,128)(2,1)S(1)} %pad_maximum_fusion.ext_ref, ...), custom_call_target="tpu_custom_call" | custom-call | flops 1000000000 | bytes 5000000 | tf_op jit(solution)/shard_map/forward/pallas_call | solution.py:240
  50.2 1.9 %collective-permute-start.4 = (bf16[32,8,1024]{2,1,0:T(8,128)(2,1)S(1)}, bf16[32,8,1024]{2,1,0:T(8,128)(2,1)S(1)}, u32[]{:S(2)}, u32[]{:S(2)}) collective-permute-start(bf16[32,8,1024]{2,1,0:T(8,128)(2,1)S(1)} %get-tuple-element.39), channel_id=1, source_target_pairs={{0,1},{1,0},{2,3},{3,2},{4,5},{5,4},{6,7},{7,6},{8,9},{9,8},{10,11... | collective-permute-start | bytes 1572872 | tf_op jit(solution)/shard_map/ppermute | solution.py:337
  52.2 5.5 %backward.1 = (bf16[12,16,512]{2,1,0:T(8,128)(2,1)}, bf16[12,16,1024]{2,1,0:T(8,128)(2,1)S(1)}, bf16[12,16,1024]{2,1,0:T(8,128)(2,1)S(1)}, bf16[24,8,1024]{2,1,0:T(8,128)(2,1)S(1)}, bf16[24,8,1024]{2,1,0:T(8,128)(2,1)S(1)}) custom-call(s32[2]{0:T(128)S(1)} %pad_add_fusion.place_ref, bf16[12,16,512]{2,1,0:T(8,128)(2,1)S(1)} %copy-done.5, ...), custom_call_target="tpu_custom_call" | custom-call | flops 20000000000 | bytes 70000000 | tf_op jit(solution)/shard_map/backward/pallas_call | solution.py:265
  57.7 0.9 fold.1
  58.6 5.2 %all-to-all-start = ((bf16[8,32,1024]{2,1,0:T(8,128)(2,1)}), bf16[8,32,1024]{2,1,0:T(8,128)(2,1)S(1)}, u32[]{:S(2)}, u32[]{:S(2)}) async-start(bf16[8,32,1024]{2,1,0:T(8,128)(2,1)} %bitcast.4), calls=%async_computation | async-start | bytes 1048576 | tf_op jit(solution)/shard_map/all_to_all | solution.py:357
  63.9 1.9 %collective-permute-start.5 = (bf16[24,8,1024]{2,1,0:T(8,128)(2,1)S(1)}, bf16[24,8,1024]{2,1,0:T(8,128)(2,1)S(1)}, u32[]{:S(2)}, u32[]{:S(2)}) collective-permute-start(bf16[24,8,1024]{2,1,0:T(8,128)(2,1)S(1)} %get-tuple-element.41), channel_id=1, source_target_pairs={{0,1},{1,2},{2,3},{3,4},{4,5},{5,6},{6,7},{7,8},{8,9},{9,10},{10,1... | collective-permute-start | bytes 1179656 | tf_op jit(solution)/shard_map/ppermute | solution.py:291
  65.8 7.5 %collective-permute-start.6 = (bf16[24,8,1024]{2,1,0:T(8,128)(2,1)S(1)}, bf16[24,8,1024]{2,1,0:T(8,128)(2,1)S(1)}, u32[]{:S(2)}, u32[]{:S(2)}) collective-permute-start(bf16[24,8,1024]{2,1,0:T(8,128)(2,1)S(1)} %get-tuple-element.42), channel_id=1, source_target_pairs={{0,63},{1,0},{2,1},{3,2},{4,3},{5,4},{6,5},{7,6},{8,7},{9,8},{10,9... | collective-permute-start | bytes 1179656 | tf_op jit(solution)/shard_map/ppermute | solution.py:291
  73.3 11.7 %collective-permute-done.5.west_ref = bf16[24,8,1024]{2,1,0:T(8,128)(2,1)S(1)} collective-permute-done((bf16[24,8,1024]{2,1,0:T(8,128)(2,1)S(1)}, bf16[24,8,1024]{2,1,0:T(8,128)(2,1)S(1)}, u32[]{:S(2)}, u32[]{:S(2)}) %collective-permute-start.5) | collective-permute-done | bytes 393248 | tf_op jit(solution)/shard_map/ppermute | solution.py:291
  85.1 0.1 rim.1
  85.2 0.1 sum_far.1
  85.3 8.1 %all_to_all.15.parts_ref = bf16[4,8,1024]{2,1,0:T(8,128)(2,1)S(1)} all-to-all(bf16[4,8,1024]{2,1,0:T(8,128)(2,1)S(1)} %bitcast.10), channel_id=1, replica_groups={{0,2,4,6},{1,3,5,7},{8,10,12,14},{9,11,13,15},{16,18,20,22},{17,19,21,2..., dimensions={0} | all-to-all | bytes 131072 | tf_op jit(solution)/shard_map/all_to_all | solution.py:375
  93.4 3.5 %collective-permute-start.7 = (bf16[6,16,1024]{2,1,0:T(8,128)(2,1)S(1)}, bf16[6,16,1024]{2,1,0:T(8,128)(2,1)S(1)}, u32[]{:S(2)}, u32[]{:S(2)}) collective-permute-start(bf16[6,16,1024]{2,1,0:T(8,128)(2,1)S(1)} %get-tuple-element.48), channel_id=1, source_target_pairs={{0,64},{64,128},{128,192},{192,256},{256,320},{320,384},{384,448},... | collective-permute-start | bytes 589832 | tf_op jit(solution)/shard_map/ppermute | solution.py:296
  96.8 9.0 %collective-permute-start.8 = (bf16[6,16,1024]{2,1,0:T(8,128)(2,1)S(1)}, bf16[6,16,1024]{2,1,0:T(8,128)(2,1)S(1)}, u32[]{:S(2)}, u32[]{:S(2)}) collective-permute-start(bf16[6,16,1024]{2,1,0:T(8,128)(2,1)S(1)} %get-tuple-element.49), channel_id=1, source_target_pairs={{64,0},{128,64},{192,128},{256,192},{320,256},{384,320},{448,384},... | collective-permute-start | bytes 589832 | tf_op jit(solution)/shard_map/ppermute | solution.py:296
  105.8 0.7 share.1
  106.5 9.9 %all-to-all-start.2 = ((bf16[8,8,1024]{2,1,0:T(8,128)(2,1)}), bf16[8,8,1024]{2,1,0:T(8,128)(2,1)S(1)}, u32[]{:S(2)}, u32[]{:S(2)}) async-start(bf16[8,8,1024]{2,1,0:T(8,128)(2,1)} %share.1), calls=%async_computation.2 | async-start | bytes 262144 | tf_op jit(solution)/shard_map/all_to_all | solution.py:387
  116.4 0.8 finish.1
  117.2 8.2 %all-to-all-done.2.terms_ref = bf16[8,8,1024]{2,1,0:T(8,128)(2,1)S(1)} async-done(((bf16[8,8,1024]{2,1,0:T(8,128)(2,1)}), bf16[8,8,1024]{2,1,0:T(8,128)(2,1)S(1)}, u32[]{:S(2)}, u32[]{:S(2)}) %all-to-all-start.2) | async-done | bytes 131104 | tf_op jit(solution)/shard_map/all_to_all | solution.py:387
  125.4 0.6 mean.1
  (21 shorter events, 0.2 us)
Async XLA Ops:
  0.6 34.7 %copy-start = (bf16[512,1024]{1,0:T(8,128)(2,1)S(1)}, bf16[512,1024]{1,0:T(8,128)(2,1)}, u32[]{:S(2)}) copy-start(bf16[512,1024]{1,0:T(8,128)(2,1)} %param.9) | copy-start | bytes 3145732
  0.6 1.0 copy-start.2
  1.7 0.9 copy-start.3
  2.7 16.2 %collective-permute-start = (bf16[6,16,1024]{2,1,0:T(8,128)(2,1)S(1)}, bf16[6,16,1024]{2,1,0:T(8,128)(2,1)S(1)}, u32[]{:S(2)}, u32[]{:S(2)}) collective-permute-start(bf16[6,16,1024]{2,1,0:T(8,128)(2,1)S(1)} %get-tuple-element.54), channel_id=1, source_target_pairs={{0,64},{64,128},{128,192},{192,256},{256,320},{320,384},{384,448},... | collective-permute-start | bytes 589832 | tf_op jit(solution)/shard_map/ppermute | solution.py:296
  13.6 21.7 %copy-start.1 = (bf16[12,16,1024]{2,1,0:T(8,128)(2,1)S(1)}, bf16[12,16,1024]{2,1,0:T(8,128)(2,1)}, u32[]{:S(2)}) copy-start(bf16[12,16,1024]{2,1,0:T(8,128)(2,1)} %param.8) | copy-start | bytes 1179652
  13.6 12.4 %collective-permute-start.1 = (bf16[6,16,1024]{2,1,0:T(8,128)(2,1)S(1)}, bf16[6,16,1024]{2,1,0:T(8,128)(2,1)S(1)}, u32[]{:S(2)}, u32[]{:S(2)}) collective-permute-start(bf16[6,16,1024]{2,1,0:T(8,128)(2,1)S(1)} %get-tuple-element.55), channel_id=1, source_target_pairs={{64,0},{128,64},{192,128},{256,192},{320,256},{384,320},{448,384},... | collective-permute-start | bytes 589832 | tf_op jit(solution)/shard_map/ppermute | solution.py:296
  26.1 20.5 %copy-start.4 = (bf16[12,16,512]{2,1,0:T(8,128)(2,1)S(1)}, bf16[12,16,512]{2,1,0:T(8,128)(2,1)}, u32[]{:S(2)}) copy-start(bf16[12,16,512]{2,1,0:T(8,128)(2,1)} %q_ref.3) | copy-start | bytes 589828
  27.1 11.8 %collective-permute-start.3 = (bf16[24,8,1024]{2,1,0:T(8,128)(2,1)}, bf16[24,8,1024]{2,1,0:T(8,128)(2,1)S(1)}, u32[]{:S(2)}, u32[]{:S(2)}) collective-permute-start(bf16[24,8,1024]{2,1,0:T(8,128)(2,1)} %get-tuple-element.52), channel_id=1, source_target_pairs={{0,63},{1,0},{2,1},{3,2},{4,3},{5,4},{6,5},{7,6},{8,7},{9,8},{10,9... | collective-permute-start | bytes 1179656 | tf_op jit(solution)/shard_map/ppermute | solution.py:291
  33.3 13.3 %collective-permute-start.2 = (bf16[24,8,1024]{2,1,0:T(8,128)(2,1)}, bf16[24,8,1024]{2,1,0:T(8,128)(2,1)S(1)}, u32[]{:S(2)}, u32[]{:S(2)}) collective-permute-start(bf16[24,8,1024]{2,1,0:T(8,128)(2,1)} %get-tuple-element.53), channel_id=1, source_target_pairs={{0,1},{1,2},{2,3},{3,4},{4,5},{5,6},{6,7},{7,8},{8,9},{9,10},{10,1... | collective-permute-start | bytes 1179656 | tf_op jit(solution)/shard_map/ppermute | solution.py:291
  35.9 16.3 %copy-start.5 = (bf16[12,16,512]{2,1,0:T(8,128)(2,1)S(1)}, bf16[12,16,512]{2,1,0:T(8,128)(2,1)}, u32[]{:S(2)}) copy-start(bf16[12,16,512]{2,1,0:T(8,128)(2,1)} %q_ref.3) | copy-start | bytes 589828
  50.2 7.5 %collective-permute-start.4 = (bf16[32,8,1024]{2,1,0:T(8,128)(2,1)S(1)}, bf16[32,8,1024]{2,1,0:T(8,128)(2,1)S(1)}, u32[]{:S(2)}, u32[]{:S(2)}) collective-permute-start(bf16[32,8,1024]{2,1,0:T(8,128)(2,1)S(1)} %get-tuple-element.39), channel_id=1, source_target_pairs={{0,1},{1,0},{2,3},{3,2},{4,5},{5,4},{6,7},{7,6},{8,9},{9,8},{10,11... | collective-permute-start | bytes 1572872 | tf_op jit(solution)/shard_map/ppermute | solution.py:337
  57.7 0.9 copy-start.6
  58.6 26.6 %all-to-all-start = ((bf16[8,32,1024]{2,1,0:T(8,128)(2,1)}), bf16[8,32,1024]{2,1,0:T(8,128)(2,1)S(1)}, u32[]{:S(2)}, u32[]{:S(2)}) async-start(bf16[8,32,1024]{2,1,0:T(8,128)(2,1)} %bitcast.4), calls=%async_computation | async-start | bytes 1048576 | tf_op jit(solution)/shard_map/all_to_all | solution.py:357
  63.9 21.2 %collective-permute-start.5 = (bf16[24,8,1024]{2,1,0:T(8,128)(2,1)S(1)}, bf16[24,8,1024]{2,1,0:T(8,128)(2,1)S(1)}, u32[]{:S(2)}, u32[]{:S(2)}) collective-permute-start(bf16[24,8,1024]{2,1,0:T(8,128)(2,1)S(1)} %get-tuple-element.41), channel_id=1, source_target_pairs={{0,1},{1,2},{2,3},{3,4},{4,5},{5,6},{6,7},{7,8},{8,9},{9,10},{10,1... | collective-permute-start | bytes 1179656 | tf_op jit(solution)/shard_map/ppermute | solution.py:291
  65.8 19.3 %collective-permute-start.6 = (bf16[24,8,1024]{2,1,0:T(8,128)(2,1)S(1)}, bf16[24,8,1024]{2,1,0:T(8,128)(2,1)S(1)}, u32[]{:S(2)}, u32[]{:S(2)}) collective-permute-start(bf16[24,8,1024]{2,1,0:T(8,128)(2,1)S(1)} %get-tuple-element.42), channel_id=1, source_target_pairs={{0,63},{1,0},{2,1},{3,2},{4,3},{5,4},{6,5},{7,6},{8,7},{9,8},{10,9... | collective-permute-start | bytes 1179656 | tf_op jit(solution)/shard_map/ppermute | solution.py:291
  85.1 31.3 %copy-start.7 = (bf16[12,16,1024]{2,1,0:T(8,128)(2,1)S(1)}, bf16[12,16,1024]{2,1,0:T(8,128)(2,1)}, u32[]{:S(2)}) copy-start(bf16[12,16,1024]{2,1,0:T(8,128)(2,1)} %copy-done.6) | copy-start | bytes 1179652
  93.4 23.0 %collective-permute-start.7 = (bf16[6,16,1024]{2,1,0:T(8,128)(2,1)S(1)}, bf16[6,16,1024]{2,1,0:T(8,128)(2,1)S(1)}, u32[]{:S(2)}, u32[]{:S(2)}) collective-permute-start(bf16[6,16,1024]{2,1,0:T(8,128)(2,1)S(1)} %get-tuple-element.48), channel_id=1, source_target_pairs={{0,64},{64,128},{128,192},{192,256},{256,320},{320,384},{384,448},... | collective-permute-start | bytes 589832 | tf_op jit(solution)/shard_map/ppermute | solution.py:296
  96.8 19.5 %collective-permute-start.8 = (bf16[6,16,1024]{2,1,0:T(8,128)(2,1)S(1)}, bf16[6,16,1024]{2,1,0:T(8,128)(2,1)S(1)}, u32[]{:S(2)}, u32[]{:S(2)}) collective-permute-start(bf16[6,16,1024]{2,1,0:T(8,128)(2,1)S(1)} %get-tuple-element.49), channel_id=1, source_target_pairs={{64,0},{128,64},{192,128},{256,192},{320,256},{384,320},{448,384},... | collective-permute-start | bytes 589832 | tf_op jit(solution)/shard_map/ppermute | solution.py:296
  106.5 18.9 %all-to-all-start.2 = ((bf16[8,8,1024]{2,1,0:T(8,128)(2,1)}), bf16[8,8,1024]{2,1,0:T(8,128)(2,1)S(1)}, u32[]{:S(2)}, u32[]{:S(2)}) async-start(bf16[8,8,1024]{2,1,0:T(8,128)(2,1)} %share.1), calls=%async_computation.2 | async-start | bytes 262144 | tf_op jit(solution)/shard_map/all_to_all | solution.py:387

commit v8 on v6

--- a/solution.py
+++ b/solution.py
@@ -179,6 +179,20 @@
         copy.wait()
 
 
+def edge_kernel(above_ref, both_ref, below_ref, ext_ref, last_ref, first_ref):
+    deep, rows = above_ref.shape[0], both_ref.shape[0]
+    cols = both_ref.shape[1]
+    for at, size, source in (
+        (0, deep, above_ref),
+        (deep, rows, both_ref),
+        (deep + rows, deep, below_ref),
+    ):
+        ext_ref[at : at + size] = source[...]
+        block = source[...].astype(jnp.float32)
+        first_ref[at : at + size] = block[:, :SIDE].astype(jnp.bfloat16)
+        last_ref[at : at + size] = block[:, cols - SIDE :].astype(jnp.bfloat16)
+
+
 def fold_kernel(keep_ref, got_ref, half_ref):
     half_ref[...] = (keep_ref[...] + got_ref[...].astype(jnp.float32)).astype(jnp.bfloat16)
 
@@ -315,7 +329,7 @@
     both = pl.pallas_call(
         pack_kernel,
         out_shape=shape((rows, cols, 2 * inner)),
-        in_specs=[pl.BlockSpec(memory_space=pl.ANY)] * 2,
+        in_specs=[pl.BlockSpec(memory_space=pltpu.HBM)] * 2,
         out_specs=VMEM,
         scratch_shapes=[pltpu.SemaphoreType.DMA((2,))],
         compiler_params=SMALL,
@@ -323,20 +337,24 @@
     )(keys, values)
     above = line(both[rows - RADIUS :], "lat", 1)
     below = line(both[:RADIUS], "lat", -1)
-    extended = jnp.concatenate([above, both, below], axis=0)
-    west = ring(extended[:, cols - SIDE :], "lon", 1)
-    east = ring(extended[:, :SIDE], "lon", -1)
+    ext_rows = rows + 2 * RADIUS
+    extended, last, first = pl.pallas_call(
+        edge_kernel,
+        out_shape=(
+            shape((ext_rows, cols, 2 * inner)),
+            shape((ext_rows, SIDE, 2 * inner)),
+            shape((ext_rows, SIDE, 2 * inner)),
+        ),
+        compiler_params=SMALL,
+        name="edge",
+    )(above, both, below)
+    west = ring(last, "lon", 1)
+    east = ring(first, "lon", -1)
     place, grads = lax.optimization_barrier((place, grads))
     kv, norm, keep, give = forward(
         place, queries, extended, west, east, up_flat, lat_total, out_rows
     )
     got = lax.ppermute(give, "lon", [(i, i ^ 1) for i in range(lon)])
-    grad_query, mid, rim, left, right = backward(
-        place, queries, grads, kv, norm, lat_total
-    )
-    keep, left, right = lax.optimization_barrier((keep, left, right))
-    from_east = ring(left, "lon", -1)
-    from_west = ring(right, "lon", 1)
     half = pl.pallas_call(
         fold_kernel,
         out_shape=shape(keep.shape),
@@ -346,7 +364,12 @@
     )(keep, got)
     same_core = [[2 * i + c for i in range(lon // 2)] for c in range(2)]
     terms = lax.all_to_all(half, "lon", 0, 0, axis_index_groups=same_core, tiled=True)
-    rim, _ = lax.optimization_barrier((rim, half))
+    after, _ = lax.optimization_barrier((place, half))
+    grad_query, mid, rim, left, right = backward(
+        after, queries, grads, kv, norm, lat_total
+    )
+    from_east = ring(left, "lon", -1)
+    from_west = ring(right, "lon", 1)
     top, bottom = pl.pallas_call(
         rim_kernel,
         out_shape=(shape((RADIUS, cols, 2 * inner)),) * 2,

time: 125 us -> 127 us (1.016)
  starting transfers between devices: 62.9 us -> 60.3 us
  Pallas kernels: 12.3 us -> 13.6 us
    ppermute x4, waiting for transfers between devices: 10.7 us -> 26.7 us  [line(): lax.ppermute(block, axis, [(i, i + by) for i in range(size) if 0 <= i + b...]
    ppermute x4, waiting for transfers between devices: 23 us -> 11.8 us  [ring(): lax.ppermute(block, axis, [(i, (i + by) % size) for i in range(size)])]
    all_to_all x1, waiting for transfers between devices: 10.5 us -> 5.08 us  [shards(): every = lax.all_to_all(copies, 'lat', 0, 0, tiled=True)]
    all_to_all x1, starting transfers between devices: 9.87 us -> 4.84 us  [shards(): every = lax.all_to_all(copies, 'lat', 0, 0, tiled=True)]
    all_to_all x1, starting transfers between devices: 7.88 us -> 10.8 us  [shards(): lax.all_to_all(half, 'lon', 0, 0, axis_index_groups=same_core, tiled=True)]
    unnamed x16 -> x18, local copies, waits for them, and re-layouts: 1.97 us -> 4.15 us
    ppermute x1, waiting for transfers between devices: 0.01 us -> 1.88 us  [shards(): got = lax.ppermute(give, 'lon', [(i, i ^ 1) for i in range(lon)])]
    ppermute x4, starting transfers between devices: 25.6 us -> 23.9 us  [line(): lax.ppermute(block, axis, [(i, i + by) for i in range(size) if 0 <= i + b...]
  transfers between devices with their start and end apart: 11 -> 11, of which waited for: 7 -> 8; matrix products, arithmetic and copies ran while one was open for 0% -> 0% of each run, Pallas kernels for 6% -> 6%
where the time goes in v8:
time: 127 us; the launch traced here: 125 us
  starting transfers between devices  60.3 us (47%)
  waiting for transfers between devices  45.5 us (36%)
  Pallas kernels  13.6 us (11%)
  local copies, waits for them, and re-layouts  4.18 us (3%)
    ppermute x4, waiting for transfers between devices, line(): lax.ppermute(block, axis, [(i, i + by) for i in range(size) if 0 <= i + b...  26.7 us
    ppermute x4, starting transfers between devices, line(): lax.ppermute(block, axis, [(i, i + by) for i in range(size) if 0 <= i + b...  23.9 us
    ppermute x4, starting transfers between devices, ring(): lax.ppermute(block, axis, [(i, (i + by) % size) for i in range(size)])  18.9 us
    ppermute x4, waiting for transfers between devices, ring(): lax.ppermute(block, axis, [(i, (i + by) % size) for i in range(size)])  11.8 us
    all_to_all x1, starting transfers between devices, shards(): lax.all_to_all(half, 'lon', 0, 0, axis_index_groups=same_core, tiled=True)  10.8 us
    pallas_call x1, Pallas kernels, backward(): pl.pallas_call(functools.partial(backward_kernel, lat_total), out_shape=(...  5.48 us
    all_to_all x1, waiting for transfers between devices, shards(): every = lax.all_to_all(copies, 'lat', 0, 0, tiled=True)  5.08 us
    all_to_all x1, starting transfers between devices, shards(): every = lax.all_to_all(copies, 'lat', 0, 0, tiled=True)  4.84 us
  transfers between devices with their start and end apart: 11, of which 8 were waited for; matrix products, arithmetic and copies ran while one was open for 0% of the time, Pallas kernels for 6%

profile of v8, /device:TPU:6, one launch (start us, length us, event | category | flops | bytes accessed | tf_op | source)
XLA Modules:
  0.0 125.0 jit_solution(10908619249617419306)
XLA Ops:
  0.7 1.0 copy-done.2
  1.7 0.9 copy-done.3
  2.7 11.3 %collective-permute-start.1 = (bf16[6,16,1024]{2,1,0:T(8,128)(2,1)S(1)}, bf16[6,16,1024]{2,1,0:T(8,128)(2,1)S(1)}, u32[]{:S(2)}, u32[]{:S(2)}) collective-permute-start(bf16[6,16,1024]{2,1,0:T(8,128)(2,1)S(1)} %get-tuple-element.46), channel_id=1, source_target_pairs={{64,0},{128,64},{192,128},{256,192},{320,256},{384,320},{448,384},... | collective-permute-start | bytes 589832 | tf_op jit(solution)/shard_map/ppermute | solution.py:306
  14.1 1.9 %collective-permute-start = (bf16[6,16,1024]{2,1,0:T(8,128)(2,1)S(1)}, bf16[6,16,1024]{2,1,0:T(8,128)(2,1)S(1)}, u32[]{:S(2)}, u32[]{:S(2)}) collective-permute-start(bf16[6,16,1024]{2,1,0:T(8,128)(2,1)S(1)} %get-tuple-element.47), channel_id=1, source_target_pairs={{0,64},{64,128},{128,192},{192,256},{256,320},{320,384},{384,448},... | collective-permute-start | bytes 589832 | tf_op jit(solution)/shard_map/ppermute | solution.py:306
  16.0 7.5 %collective-permute-done.1.below_ref = bf16[6,16,1024]{2,1,0:T(8,128)(2,1)S(1)} collective-permute-done((bf16[6,16,1024]{2,1,0:T(8,128)(2,1)S(1)}, bf16[6,16,1024]{2,1,0:T(8,128)(2,1)S(1)}, u32[]{:S(2)}, u32[]{:S(2)}) %collective-permute-start.1) | collective-permute-done | bytes 196640 | tf_op jit(solution)/shard_map/ppermute | solution.py:306
  23.5 12.1 %collective-permute-done.above_ref = bf16[6,16,1024]{2,1,0:T(8,128)(2,1)S(1)} collective-permute-done((bf16[6,16,1024]{2,1,0:T(8,128)(2,1)S(1)}, bf16[6,16,1024]{2,1,0:T(8,128)(2,1)S(1)}, u32[]{:S(2)}, u32[]{:S(2)}) %collective-permute-start) | collective-permute-done | bytes 196640 | tf_op jit(solution)/shard_map/ppermute | solution.py:306
  35.5 0.8 edge.1
  36.4 1.9 %collective-permute-start.2 = (bf16[24,8,1024]{2,1,0:T(8,128)(2,1)}, bf16[24,8,1024]{2,1,0:T(8,128)(2,1)S(1)}, u32[]{:S(2)}, u32[]{:S(2)}) collective-permute-start(bf16[24,8,1024]{2,1,0:T(8,128)(2,1)} %get-tuple-element.27), channel_id=1, source_target_pairs={{0,1},{1,2},{2,3},{3,4},{4,5},{5,6},{6,7},{7,8},{8,9},{9,10},{10,1... | collective-permute-start | bytes 1179656 | tf_op jit(solution)/shard_map/ppermute | solution.py:301
  38.3 7.6 %collective-permute-start.3 = (bf16[24,8,1024]{2,1,0:T(8,128)(2,1)S(1)}, bf16[24,8,1024]{2,1,0:T(8,128)(2,1)}, u32[]{:S(2)}, u32[]{:S(2)}) collective-permute-start(bf16[24,8,1024]{2,1,0:T(8,128)(2,1)S(1)} %get-tuple-element.28), channel_id=1, source_target_pairs={{0,63},{1,0},{2,1},{3,2},{4,3},{5,4},{6,5},{7,6},{8,7},{9,8},{10,9... | collective-permute-start | bytes 1179656 | tf_op jit(solution)/shard_map/ppermute | solution.py:301
  46.0 0.5 convolution_convert_fusion
  46.5 3.3 %collective-permute-done.2.west_ref = bf16[24,8,1024]{2,1,0:T(8,128)(2,1)S(1)} collective-permute-done((bf16[24,8,1024]{2,1,0:T(8,128)(2,1)}, bf16[24,8,1024]{2,1,0:T(8,128)(2,1)S(1)}, u32[]{:S(2)}, u32[]{:S(2)}) %collective-permute-start.2) | collective-permute-done | bytes 393248 | tf_op jit(solution)/shard_map/ppermute | solution.py:301
  49.8 1.4 %collective-permute-done.3.east_ref = bf16[24,8,1024]{2,1,0:T(8,128)(2,1)} collective-permute-done((bf16[24,8,1024]{2,1,0:T(8,128)(2,1)S(1)}, bf16[24,8,1024]{2,1,0:T(8,128)(2,1)}, u32[]{:S(2)}, u32[]{:S(2)}) %collective-permute-start.3) | collective-permute-done | bytes 393248 | tf_op jit(solution)/shard_map/ppermute | solution.py:301
  51.1 4.0 %forward.1 = (bf16[24,32,1024]{2,1,0:T(8,128)(2,1)S(1)}, f32[8,256]{1,0:T(8,128)S(1)}, f32[32,8,1024]{2,1,0:T(8,128)S(1)}, bf16[32,8,1024]{2,1,0:T(8,128)(2,1)S(1)}) custom-call(s32[2]{0:T(128)S(1)} %pad_add_fusion.place_ref, bf16[12,16,512]{2,1,0:T(8,128)(2,1)S(1)} %copy-done.4, bf16[24,16,1024]{2,1,0:T(8,128)(2,1)S(1)} %get-tuple-element.26.ext_ref, ...), custom_call_target="tpu_custom_call" | custom-call | flops 1000000000 | bytes 5000000 | tf_op jit(solution)/shard_map/forward/pallas_call | solution.py:250
  55.2 1.2 copy-done.5
  56.3 1.9 %collective-permute-start.4 = (bf16[32,8,1024]{2,1,0:T(8,128)(2,1)S(1)}, bf16[32,8,1024]{2,1,0:T(8,128)(2,1)S(1)}, u32[]{:S(2)}, u32[]{:S(2)}) collective-permute-start(bf16[32,8,1024]{2,1,0:T(8,128)(2,1)S(1)} %get-tuple-element.30), channel_id=1, source_target_pairs={{0,1},{1,0},{2,3},{3,2},{4,5},{5,4},{6,7},{7,6},{8,9},{9,8},{10,11... | collective-permute-start | bytes 1572872 | tf_op jit(solution)/shard_map/ppermute | solution.py:357
  58.3 1.9 %collective-permute-done.4.got_ref = bf16[32,8,1024]{2,1,0:T(8,128)(2,1)S(1)} collective-permute-done((bf16[32,8,1024]{2,1,0:T(8,128)(2,1)S(1)}, bf16[32,8,1024]{2,1,0:T(8,128)(2,1)S(1)}, u32[]{:S(2)}, u32[]{:S(2)}) %collective-permute-start.4) | collective-permute-done | bytes 524320 | tf_op jit(solution)/shard_map/ppermute | solution.py:357
  60.1 0.9 fold.1
  61.1 10.8 %all-to-all-start = ((bf16[32,8,1024]{2,1,0:T(8,128)(2,1)}), bf16[32,8,1024]{2,1,0:T(8,128)(2,1)S(1)}, u32[]{:S(2)}, u32[]{:S(2)}) async-start(bf16[32,8,1024]{2,1,0:T(8,128)(2,1)} %fold.1), calls=%async_computation | async-start | bytes 1048576 | tf_op jit(solution)/shard_map/all_to_all | solution.py:366
  71.9 5.5 %backward.1 = (bf16[12,16,512]{2,1,0:T(8,128)(2,1)}, bf16[12,16,1024]{2,1,0:T(8,128)(2,1)S(1)}, bf16[12,16,1024]{2,1,0:T(8,128)(2,1)S(1)}, bf16[24,8,1024]{2,1,0:T(8,128)(2,1)S(1)}, bf16[24,8,1024]{2,1,0:T(8,128)(2,1)S(1)}) custom-call(s32[2]{0:T(128)S(1)} %pad_add_fusion.place_ref, bf16[12,16,512]{2,1,0:T(8,128)(2,1)S(1)} %copy-done.4, ...), custom_call_target="tpu_custom_call" | custom-call | flops 20000000000 | bytes 70000000 | tf_op jit(solution)/shard_map/backward/pallas_call | solution.py:275
  77.3 2.0 %collective-permute-start.5 = (bf16[24,8,1024]{2,1,0:T(8,128)(2,1)S(1)}, bf16[24,8,1024]{2,1,0:T(8,128)(2,1)S(1)}, u32[]{:S(2)}, u32[]{:S(2)}) collective-permute-start(bf16[24,8,1024]{2,1,0:T(8,128)(2,1)S(1)} %get-tuple-element.38), channel_id=1, source_target_pairs={{0,1},{1,2},{2,3},{3,4},{4,5},{5,6},{6,7},{7,8},{8,9},{9,10},{10,1... | collective-permute-start | bytes 1179656 | tf_op jit(solution)/shard_map/ppermute | solution.py:301
  79.3 7.5 %collective-permute-start.6 = (bf16[24,8,1024]{2,1,0:T(8,128)(2,1)S(1)}, bf16[24,8,1024]{2,1,0:T(8,128)(2,1)S(1)}, u32[]{:S(2)}, u32[]{:S(2)}) collective-permute-start(bf16[24,8,1024]{2,1,0:T(8,128)(2,1)S(1)} %get-tuple-element.39), channel_id=1, source_target_pairs={{0,63},{1,0},{2,1},{3,2},{4,3},{5,4},{6,5},{7,6},{8,7},{9,8},{10,9... | collective-permute-start | bytes 1179656 | tf_op jit(solution)/shard_map/ppermute | solution.py:301
  86.8 7.2 %collective-permute-done.5.west_ref = bf16[24,8,1024]{2,1,0:T(8,128)(2,1)S(1)} collective-permute-done((bf16[24,8,1024]{2,1,0:T(8,128)(2,1)S(1)}, bf16[24,8,1024]{2,1,0:T(8,128)(2,1)S(1)}, u32[]{:S(2)}, u32[]{:S(2)}) %collective-permute-start.5) | collective-permute-done | bytes 393248 | tf_op jit(solution)/shard_map/ppermute | solution.py:301
  94.0 0.1 rim.1
  94.1 1.9 %collective-permute-start.7 = (bf16[6,16,1024]{2,1,0:T(8,128)(2,1)S(1)}, bf16[6,16,1024]{2,1,0:T(8,128)(2,1)S(1)}, u32[]{:S(2)}, u32[]{:S(2)}) collective-permute-start(bf16[6,16,1024]{2,1,0:T(8,128)(2,1)S(1)} %get-tuple-element.43), channel_id=1, source_target_pairs={{0,64},{64,128},{128,192},{192,256},{256,320},{320,384},{384,448},... | collective-permute-start | bytes 589832 | tf_op jit(solution)/shard_map/ppermute | solution.py:306
  96.0 8.7 %collective-permute-start.8 = (bf16[6,16,1024]{2,1,0:T(8,128)(2,1)S(1)}, bf16[6,16,1024]{2,1,0:T(8,128)(2,1)S(1)}, u32[]{:S(2)}, u32[]{:S(2)}) collective-permute-start(bf16[6,16,1024]{2,1,0:T(8,128)(2,1)S(1)} %get-tuple-element.40), channel_id=1, source_target_pairs={{64,0},{128,64},{192,128},{256,192},{320,256},{384,320},{448,384},... | collective-permute-start | bytes 589832 | tf_op jit(solution)/shard_map/ppermute | solution.py:306
  104.8 0.7 share.1
  105.5 4.8 %all-to-all-start.1 = ((bf16[8,8,1024]{2,1,0:T(8,128)(2,1)}), bf16[8,8,1024]{2,1,0:T(8,128)(2,1)S(1)}, u32[]{:S(2)}, u32[]{:S(2)}) async-start(bf16[8,8,1024]{2,1,0:T(8,128)(2,1)} %share.1), calls=%async_computation.1 | async-start | bytes 262144 | tf_op jit(solution)/shard_map/all_to_all | solution.py:389
  110.3 7.1 %collective-permute-done.8.below_ref = bf16[6,16,1024]{2,1,0:T(8,128)(2,1)S(1)} collective-permute-done((bf16[6,16,1024]{2,1,0:T(8,128)(2,1)S(1)}, bf16[6,16,1024]{2,1,0:T(8,128)(2,1)S(1)}, u32[]{:S(2)}, u32[]{:S(2)}) %collective-permute-start.8) | collective-permute-done | bytes 196640 | tf_op jit(solution)/shard_map/ppermute | solution.py:306
  117.5 1.0 copy-done.8
  118.5 0.8 finish.1
  119.3 5.1 %all-to-all-done.1.terms_ref = bf16[8,8,1024]{2,1,0:T(8,128)(2,1)S(1)} async-done(((bf16[8,8,1024]{2,1,0:T(8,128)(2,1)}), bf16[8,8,1024]{2,1,0:T(8,128)(2,1)S(1)}, u32[]{:S(2)}, u32[]{:S(2)}) %all-to-all-start.1) | async-done | bytes 131104 | tf_op jit(solution)/shard_map/all_to_all | solution.py:389
  124.4 0.6 mean.1
  (20 shorter events, 0.2 us)
Async XLA Ops:
  0.6 45.3 %copy-start = (bf16[512,1024]{1,0:T(8,128)(2,1)S(1)}, bf16[512,1024]{1,0:T(8,128)(2,1)}, u32[]{:S(2)}) copy-start(bf16[512,1024]{1,0:T(8,128)(2,1)} %param.9) | copy-start | bytes 3145732
  0.6 45.3 %copy-start.1 = (bf16[12,16,1024]{2,1,0:T(8,128)(2,1)S(1)}, bf16[12,16,1024]{2,1,0:T(8,128)(2,1)}, u32[]{:S(2)}) copy-start(bf16[12,16,1024]{2,1,0:T(8,128)(2,1)} %param.8) | copy-start | bytes 1179652
  0.7 1.0 copy-start.2
  1.7 0.9 copy-start.3
  2.7 48.5 %copy-start.4 = (bf16[12,16,512]{2,1,0:T(8,128)(2,1)S(1)}, bf16[12,16,512]{2,1,0:T(8,128)(2,1)}, u32[]{:S(2)}) copy-start(bf16[12,16,512]{2,1,0:T(8,128)(2,1)} %q_ref.3) | copy-start | bytes 589828
  2.7 20.8 %collective-permute-start.1 = (bf16[6,16,1024]{2,1,0:T(8,128)(2,1)S(1)}, bf16[6,16,1024]{2,1,0:T(8,128)(2,1)S(1)}, u32[]{:S(2)}, u32[]{:S(2)}) collective-permute-start(bf16[6,16,1024]{2,1,0:T(8,128)(2,1)S(1)} %get-tuple-element.46), channel_id=1, source_target_pairs={{64,0},{128,64},{192,128},{256,192},{320,256},{384,320},{448,384},... | collective-permute-start | bytes 589832 | tf_op jit(solution)/shard_map/ppermute | solution.py:306
  14.1 21.5 %collective-permute-start = (bf16[6,16,1024]{2,1,0:T(8,128)(2,1)S(1)}, bf16[6,16,1024]{2,1,0:T(8,128)(2,1)S(1)}, u32[]{:S(2)}, u32[]{:S(2)}) collective-permute-start(bf16[6,16,1024]{2,1,0:T(8,128)(2,1)S(1)} %get-tuple-element.47), channel_id=1, source_target_pairs={{0,64},{64,128},{128,192},{192,256},{256,320},{320,384},{384,448},... | collective-permute-start | bytes 589832 | tf_op jit(solution)/shard_map/ppermute | solution.py:306
  36.4 13.4 %collective-permute-start.2 = (bf16[24,8,1024]{2,1,0:T(8,128)(2,1)}, bf16[24,8,1024]{2,1,0:T(8,128)(2,1)S(1)}, u32[]{:S(2)}, u32[]{:S(2)}) collective-permute-start(bf16[24,8,1024]{2,1,0:T(8,128)(2,1)} %get-tuple-element.27), channel_id=1, source_target_pairs={{0,1},{1,2},{2,3},{3,4},{4,5},{5,6},{6,7},{7,8},{8,9},{9,10},{10,1... | collective-permute-start | bytes 1179656 | tf_op jit(solution)/shard_map/ppermute | solution.py:301
  38.3 12.8 %collective-permute-start.3 = (bf16[24,8,1024]{2,1,0:T(8,128)(2,1)S(1)}, bf16[24,8,1024]{2,1,0:T(8,128)(2,1)}, u32[]{:S(2)}, u32[]{:S(2)}) collective-permute-start(bf16[24,8,1024]{2,1,0:T(8,128)(2,1)S(1)} %get-tuple-element.28), channel_id=1, source_target_pairs={{0,63},{1,0},{2,1},{3,2},{4,3},{5,4},{6,5},{7,6},{8,7},{9,8},{10,9... | collective-permute-start | bytes 1179656 | tf_op jit(solution)/shard_map/ppermute | solution.py:301
  55.2 1.2 copy-start.5
  56.3 3.8 %collective-permute-start.4 = (bf16[32,8,1024]{2,1,0:T(8,128)(2,1)S(1)}, bf16[32,8,1024]{2,1,0:T(8,128)(2,1)S(1)}, u32[]{:S(2)}, u32[]{:S(2)}) collective-permute-start(bf16[32,8,1024]{2,1,0:T(8,128)(2,1)S(1)} %get-tuple-element.30), channel_id=1, source_target_pairs={{0,1},{1,0},{2,3},{3,2},{4,5},{5,4},{6,7},{7,6},{8,9},{9,8},{10,11... | collective-permute-start | bytes 1572872 | tf_op jit(solution)/shard_map/ppermute | solution.py:357
  60.1 11.7 %copy-start.6 = (bf16[24,32,1024]{2,1,0:T(8,128)(2,1)S(1)}, bf16[24,32,1024]{2,1,0:T(8,128)(2,1)}, u32[]{:S(2)}) copy-start(bf16[24,32,1024]{2,1,0:T(8,128)(2,1)} %copy-done.5) | copy-start | bytes 4718596
  61.1 43.7 %all-to-all-start = ((bf16[32,8,1024]{2,1,0:T(8,128)(2,1)}), bf16[32,8,1024]{2,1,0:T(8,128)(2,1)S(1)}, u32[]{:S(2)}, u32[]{:S(2)}) async-start(bf16[32,8,1024]{2,1,0:T(8,128)(2,1)} %fold.1), calls=%async_computation | async-start | bytes 1048576 | tf_op jit(solution)/shard_map/all_to_all | solution.py:366
  77.3 18.7 %copy-start.7 = (bf16[12,16,1024]{2,1,0:T(8,128)(2,1)}, bf16[12,16,1024]{2,1,0:T(8,128)(2,1)S(1)}, u32[]{:S(2)}) copy-start(bf16[12,16,1024]{2,1,0:T(8,128)(2,1)S(1)} %get-tuple-element.42.mid_ref) | copy-start | bytes 1179652
  77.3 16.6 %collective-permute-start.5 = (bf16[24,8,1024]{2,1,0:T(8,128)(2,1)S(1)}, bf16[24,8,1024]{2,1,0:T(8,128)(2,1)S(1)}, u32[]{:S(2)}, u32[]{:S(2)}) collective-permute-start(bf16[24,8,1024]{2,1,0:T(8,128)(2,1)S(1)} %get-tuple-element.38), channel_id=1, source_target_pairs={{0,1},{1,2},{2,3},{3,4},{4,5},{5,6},{6,7},{7,8},{8,9},{9,10},{10,1... | collective-permute-start | bytes 1179656 | tf_op jit(solution)/shard_map/ppermute | solution.py:301
  79.3 14.7 %collective-permute-start.6 = (bf16[24,8,1024]{2,1,0:T(8,128)(2,1)S(1)}, bf16[24,8,1024]{2,1,0:T(8,128)(2,1)S(1)}, u32[]{:S(2)}, u32[]{:S(2)}) collective-permute-start(bf16[24,8,1024]{2,1,0:T(8,128)(2,1)S(1)} %get-tuple-element.39), channel_id=1, source_target_pairs={{0,63},{1,0},{2,1},{3,2},{4,3},{5,4},{6,5},{7,6},{8,7},{9,8},{10,9... | collective-permute-start | bytes 1179656 | tf_op jit(solution)/shard_map/ppermute | solution.py:301
  94.1 16.3 %collective-permute-start.7 = (bf16[6,16,1024]{2,1,0:T(8,128)(2,1)S(1)}, bf16[6,16,1024]{2,1,0:T(8,128)(2,1)S(1)}, u32[]{:S(2)}, u32[]{:S(2)}) collective-permute-start(bf16[6,16,1024]{2,1,0:T(8,128)(2,1)S(1)} %get-tuple-element.43), channel_id=1, source_target_pairs={{0,64},{64,128},{128,192},{192,256},{256,320},{320,384},{384,448},... | collective-permute-start | bytes 589832 | tf_op jit(solution)/shard_map/ppermute | solution.py:306
  96.0 21.5 %collective-permute-start.8 = (bf16[6,16,1024]{2,1,0:T(8,128)(2,1)S(1)}, bf16[6,16,1024]{2,1,0:T(8,128)(2,1)S(1)}, u32[]{:S(2)}, u32[]{:S(2)}) collective-permute-start(bf16[6,16,1024]{2,1,0:T(8,128)(2,1)S(1)} %get-tuple-element.40), channel_id=1, source_target_pairs={{64,0},{128,64},{192,128},{256,192},{320,256},{384,320},{448,384},... | collective-permute-start | bytes 589832 | tf_op jit(solution)/shard_map/ppermute | solution.py:306
  105.5 18.9 %all-to-all-start.1 = ((bf16[8,8,1024]{2,1,0:T(8,128)(2,1)}), bf16[8,8,1024]{2,1,0:T(8,128)(2,1)S(1)}, u32[]{:S(2)}, u32[]{:S(2)}) async-start(bf16[8,8,1024]{2,1,0:T(8,128)(2,1)} %share.1), calls=%async_computation.1 | async-start | bytes 262144 | tf_op jit(solution)/shard_map/all_to_all | solution.py:389
  117.5 1.0 copy-start.8
